TPU v7x, 512 devices: a whole 4x4x16 slice. The times are simulated.
512 devices in a mesh: rot: 4 (over y), tile: 64 (over x_lo, z, core), nar: 2 (over x_hi).
Axes of the slice: x: 4 (x_hi: 2, x_lo: 2; x = x_hi * 2 + x_lo), y: 4, z: 16, core: 2. Of those that a mesh axis runs over, the one named last changes fastest.
Arguments:
- interp_index: int32 [8, 8, 2, 192, 384], P(None, 'rot', 'nar', 'tile'), may hold values from 0 to 4095
- interp_weight: bfloat16 [8, 8, 2, 192, 384], P(None, 'rot', 'nar', 'tile'), may hold values from 0 to 0.25
- volume: bfloat16 [2, 2, 64, 4096], P(None, 'nar', 'tile'), may hold values from -6 to 6
- spectrum: bfloat16 [2, 64, 2, 192, 384], P(None, 'tile', 'nar'), may hold values from -6 to 6
- ctf_filter: bfloat16 [64, 2, 192, 384], P('tile', 'nar'), may hold values from -1 to 1
- peak_count: int32 [4, 64], P('rot', 'tile'), may hold values from 1 to 4, 129 in all within a row
- peak_orient: int32 [1024], P(('rot', 'tile')), may hold values from 0 to 1
- peak_row: int32 [1024], P(('rot', 'tile')), may hold values from 0 to 383
- peak_col: int32 [1024], P(('rot', 'tile')), may hold values from 0 to 383
- ctf_grid: bfloat16 [512, 2, 18432], P('tile', 'nar'), may hold values from -1 to 1
Outputs:
- peak_max: float32 [64, 2, 73728], P('tile', 'nar')
- peak_mean: float32 [64, 2, 73728], P('tile', 'nar')
- refined: float32 [4, 256, 512], P('rot', None, 'tile')
- best: float32 [4, 256], P('rot')
Inputs may be any that keep to these rules, and one draw needn't show every extreme that they name: `peak_count`: in each orientation group the counts over all tiles sum to 129, and some tile has exactly 4.
All inputs are finite; a program needn't handle non-finite values.
Results may differ from a plain program's by a relative error of at most 0.013.
Values may be sent and summed in bfloat16 or wider, within the bound.
No kernel may reach another device: no remote copies, remote signals or barrier semaphores. Data moves between devices by JAX's collectives and lax.ppermute only.
A program may use at most 64 MiB of HBM per device.

v0:
```python
import jax
import jax.numpy as jnp
from jax import lax
from jax.sharding import PartitionSpec as P


def merged(x, axis, combine):
    everything = jax.tree.map(
        lambda part, kind: lax.all_gather(part.astype(kind), axis), x, (jnp.bfloat16, jnp.bfloat16)
    )

    def take(k):
        return jax.tree.map(lambda part, own: part[k].astype(own.dtype), everything, x)

    return lax.fori_loop(
        1, lax.axis_size(axis), lambda k, so_far: combine(so_far, take(k)), take(0)
    )


def dft_tables(length):
    steps = jnp.arange(length, dtype=jnp.int32)
    phase = (steps[:, None] * steps[None, :] % length).astype(jnp.float32) * (2.0 * jnp.pi / length)
    cosv = jnp.cos(phase).astype(jnp.bfloat16)
    sinv = jnp.sin(phase).astype(jnp.bfloat16)
    wide = jnp.concatenate([jnp.concatenate([cosv, sinv], 1), jnp.concatenate([-sinv, cosv], 1)], 0)
    back = jnp.stack([cosv, -sinv], axis=1)
    return (wide, back)


def combine_stats(first, second):
    return (jnp.maximum(first[0], second[0]), first[1] + second[1])


def shards(
    interp_index,
    interp_weight,
    volume,
    spectrum,
    ctf_filter,
    peak_count,
    peak_orient,
    peak_row,
    peak_col,
    ctf_grid,
):
    table = volume[:, 0, 0]
    values = table[:, interp_index]
    weighted = jnp.sum(
        interp_weight.astype(jnp.float32)[None] * values.astype(jnp.float32), axis=1
    ).astype(jnp.bfloat16)
    length = spectrum.shape[4]
    half = spectrum.shape[3]
    orients = weighted.shape[1]
    slots = peak_orient.shape[0]
    wide, back = dft_tables(length)
    spec = spectrum[:, 0, 0]
    filt = ctf_filter[0, 0]
    piece = lax.all_gather(weighted, "tile", axis=3, tiled=True)
    count = piece.shape[3]
    spec_rows = spec.astype(jnp.float32)
    filt_rows = filt.astype(jnp.float32)
    sr = piece[0, :, 0].astype(jnp.float32)
    si = piece[1, :, 0].astype(jnp.float32)
    cr = filt_rows * sr
    ci = filt_rows * si
    xr = spec_rows[0] * cr + spec_rows[1] * ci
    xi = spec_rows[1] * cr - spec_rows[0] * ci
    cross = jnp.stack([xr, xi], axis=2).astype(jnp.bfloat16)
    rows_out = jnp.dot(
        cross.reshape(orients * count, 2 * length), wide, preferred_element_type=jnp.float32
    )
    rows_out = rows_out.astype(jnp.bfloat16).reshape(orients, count, 2, length)
    picked_r = jnp.take(sr, peak_orient, axis=0)
    picked_i = jnp.take(si, peak_orient, axis=0)
    plain_r = spec_rows[0] * picked_r + spec_rows[1] * picked_i
    plain_i = spec_rows[1] * picked_r - spec_rows[0] * picked_i
    plain = jnp.stack([plain_r, plain_i], axis=2).astype(jnp.bfloat16)
    combined = jnp.concatenate([rows_out, plain], axis=0)
    halfimg = combined[:orients]
    plain = combined[orients:].astype(jnp.float32)
    offset = lax.axis_index("nar") * half
    back_rows = lax.dynamic_slice_in_dim(back, offset, half, 2)
    partial_value = jnp.einsum(
        "yck,okcx->oyx", back_rows, halfimg, preferred_element_type=jnp.float32
    )
    summed = lax.psum_scatter(
        partial_value.astype(jnp.bfloat16), "nar", scatter_dimension=2, tiled=True
    ).astype(jnp.float32)
    corr = summed * (1.0 / length)
    local_max = jnp.max(corr, axis=0)
    local_sum = jnp.sum(corr, axis=0)
    group_count = lax.axis_size("rot")
    top, total = merged((local_max, local_sum), "rot", combine_stats)
    mean = total / (orients * group_count)
    freq_rows = lax.axis_index("nar") * half + jnp.arange(half, dtype=jnp.int32)
    freq_cols = jnp.arange(length, dtype=jnp.int32)
    turns = (
        freq_rows[None, :, None] * peak_row[:, None, None]
        + freq_cols[None, None, :] * peak_col[:, None, None]
    ) % length
    phase = turns.astype(jnp.float32) * (2.0 * jnp.pi / length)
    shifted = plain[:, :, 0] * jnp.cos(phase) - plain[:, :, 1] * jnp.sin(phase)
    binned = jnp.sum(shifted.reshape(slots, half, length // 4, 4), axis=3).astype(jnp.bfloat16)
    valid = jnp.arange(slots, dtype=jnp.int32) < peak_count[0, 0]
    binned = jnp.where(valid[:, None, None], binned, jnp.zeros_like(binned)).reshape(slots, -1)
    grid_local = ctf_grid[:, 0]
    grid_count = grid_local.shape[0]
    listed = lax.axis_size("tile") * slots
    part = lax.dot_general(
        lax.all_gather(binned, "tile", axis=0, tiled=True),
        grid_local,
        (((1,), (1,)), ((), ())),
        preferred_element_type=jnp.float32,
    )
    refined = lax.psum(part, "nar") * (1.0 / length)
    best = lax.pmax(jnp.max(refined, axis=1), "tile")
    return (
        top.reshape(1, 1, -1),
        mean.reshape(1, 1, -1),
        refined.reshape(1, listed, grid_count),
        best.reshape(1, listed),
    )


def solution(mesh):
    return jax.shard_map(
        shards,
        mesh=mesh,
        in_specs=(
            P(None, "rot", "nar", "tile", None),
            P(None, "rot", "nar", "tile", None),
            P(None, "nar", "tile", None),
            P(None, "tile", "nar", None, None),
            P("tile", "nar", None, None),
            P("rot", "tile"),
            P(("rot", "tile")),
            P(("rot", "tile")),
            P(("rot", "tile")),
            P("tile", "nar", None),
        ),
        out_specs=(
            P("tile", "nar", None),
            P("tile", "nar", None),
            P("rot", None, "tile"),
            P("rot", None),
        ),
        check_vma=False,
    )
```

profile of v0, /device:TPU:1, one launch (start us, length us, event | category | flops | bytes accessed | tf_op | source)
XLA Modules:
  0.0 458.0 jit_solution(14823752766083478575)
XLA Ops:
  8.0 0.0 copy-start
  8.0 0.0 reduce-scatter.2.cloned.1.call-start
  8.1 3.0 fusion.46
  11.1 3.0 fusion.40
  14.1 2.9 cosine_convert_fusion
  17.0 3.2 sine_convert_fusion.1
  20.2 1.0 compare_select_fusion
  21.5 0.5 copy.61
  22.0 65.0 %gather_fusion = bf16[18432,2]{1,0:T(8,128)(2,1)} fusion(bf16[2,4096]{0,1:T(8,128)(2,1)S(1)} %bitcast.100, s32[18432]{0:T(1024)S(1)} %broadcast_clamp_fusion), kind=kCustom, calls=%fused_computation.2 | custom fusion | bytes 221184 | tf_op jit(solution)/shard_map/gather | solution.py:47
  87.0 5.6 %fusion = bf16[2,2,3,384]{0,3,2,1:T(8,128)(2,1)S(1)} fusion(bf16[8,2,3,384,2]{4,3,2,1,0:T(8,128)(2,1)} %bitcast.97, f32[8,2,3,384]{3,2,1,0:T(4,128)S(1)} %copy.60), kind=kLoop, calls=%fused_computation.6 | loop fusion | flops 105984 | bytes 156672 | tf_op jit(solution)/shard_map/reduce_sum | solution.py:48
  92.6 0.2 copy.63
  92.9 72.6 %all-gather = bf16[2,2,192,384]{3,1,0,2:T(2,128)(2,1)S(1)} all-gather(bf16[2,2,3,384]{3,1,0,2:T(2,128)(2,1)S(1)} %copy.63), channel_id=2, replica_groups=mesh['rot'=4,'tile'=64,'nar'=2] {'tile'}, dimensions={2}, use_global_device_ids=true | all-gather | bytes 599040 | tf_op jit(solution)/shard_map/all_gather | solution.py:58
  165.5 0.4 fusion.51
  165.9 0.2 fusion.19
  166.1 0.0 copy-start.6
  166.1 0.1 pad_maximum_fusion
  166.2 0.6 copy.66
  166.8 0.1 copy.80
  166.9 0.1 copy-done.4
  167.1 0.1 copy-done.5
  167.1 0.1 copy-done.6
  167.2 0.6 convolution_convert_fusion
  167.9 0.1 reshape.287
  168.0 0.2 copy-done.2
  168.2 0.1 copy-done.3
  168.3 1.4 fusion.7
  169.7 0.0 reduce-scatter.2.cloned.1.call-update
  169.7 0.2 all-gather.6.cloned.1.call-start
  170.0 0.1 convert_bitcast_fusion.1
  170.8 0.6 gather_fusion.2
  171.4 1.6 gather_fusion.1
  173.0 1.7 fusion.29
  174.8 0.2 maximum_convert_fusion
  174.9 1.2 fusion.50
  176.1 0.9 copy.72
  177.0 0.0 copy-start.11
  177.0 1.9 copy.73
  178.9 0.1 broadcast_multiply_fusion.2
  179.0 0.2 broadcast_multiply_fusion.1
  179.2 15.4 %subtract_reduce_fusion = bf16[4,192,96]{1,0,2:T(4,128)(2,1)} fusion(f32[4,192,96,4]{1,0,3,2:T(4,128)S(1)} %bitcast.96, f32[4,192,96,4]{1,0,3,2:T(4,128)S(1)} %bitcast.95, s32[4,96,4]{0,2,1:T(4,128)S(1)} %broadcast_multiply_fusion.1, s32[4,192]{1,0:T(4,128)S(1)} %broadcast_multiply_fusion.2), kind=kLoop, calls=%fused_computation.10 | loop fusion | flops 3760128 | bytes 2515968 | tf_op jit(solution)/shard_map/reduce_sum | solution.py:103
  194.6 1.1 copy.74
  195.7 0.3 convert_element_type.272
  196.0 0.8 select_bitcast_fusion
  196.8 0.0 all-gather.6.cloned.1.call-update
  196.8 0.0 reduce-scatter.2.cloned.1.call-done
  196.8 1.0 fusion.32
  197.9 11.8 %all-gather.2 = bf16[1536,192]{0,1:T(8,128)(2,1)S(1)} all-gather(bf16[384,192]{0,1:T(8,128)(2,1)S(1)} %get-tuple-element.155), channel_id=4, replica_groups=mesh['rot'=4,'tile'=64,'nar'=2] {'rot'}, dimensions={0}, use_global_device_ids=true | all-gather | bytes 737280 | tf_op jit(solution)/shard_map/all_gather | solution.py:9
  209.7 0.3 copy.77
  210.0 0.2 copy.69
  210.2 10.3 %all-gather.1 = bf16[1536,192]{0,1:T(8,128)(2,1)S(1)} all-gather(bf16[384,192]{0,1:T(8,128)(2,1)S(1)} %get-tuple-element.156), channel_id=3, replica_groups=mesh['rot'=4,'tile'=64,'nar'=2] {'rot'}, dimensions={0}, use_global_device_ids=true | all-gather | bytes 737280 | tf_op jit(solution)/shard_map/all_gather | solution.py:9
  220.5 0.3 copy.76
  220.8 0.2 copy.68
  220.9 0.5 while.17
  221.0 0.1 convert_add_fusion.2
  221.1 0.1 convert_add_fusion.2
  221.3 0.1 convert_add_fusion.2
  221.5 1.1 reshape.289
  222.6 1.1 reshape.288
  223.6 95.6 %all-gather.6.cloned.1.call-done = bf16[64,4,18432]{2,1,0:T(4,128)(2,1)} async-done(((bf16[1,4,18432]{2,1,0:T(4,128)(2,1)}), bf16[64,4,18432]{2,1,0:T(4,128)(2,1)}) %all-gather.6.cloned.1.call-update) | async-done | bytes 9437200 | tf_op jit(solution)/shard_map/all_gather | solution.py:110
  319.2 13.2 %reshape.350 = bf16[256,18432]{1,0:T(8,128)(2,1)} reshape(bf16[64,4,18432]{2,1,0:T(4,128)(2,1)} %all-gather.6.cloned.1.call-done) | data formatting | bytes 18874368
  332.4 6.2 %fusion.44 = f32[256,8]{0,1:T(8,128)S(1)} fusion(bf16[256,18432]{1,0:T(8,128)(2,1)} %reshape.350, bf16[8,1,18432]{2,0,1:T(8,128)(2,1)S(1)} %copy-done), kind=kOutput, calls=%fused_computation.76 | convolution fusion | flops 75497472 | bytes 9740288 | tf_op jit(solution)/shard_map/dot_general | solution.py:109
  338.6 5.3 %psum.7 = f32[256,8]{0,1:T(8,128)S(1)} all-reduce(f32[256,8]{0,1:T(8,128)S(1)} %fusion.44), channel_id=1, replica_groups=mesh['rot'=4,'tile'=64,'nar'=2] {'nar'}, use_global_device_ids=true, to_apply=%region_7.9 | all-reduce | flops 2048 | bytes 16384 | tf_op jit(solution)/shard_map/psum | solution.py:115
  343.9 0.6 multiply_reduce_fusion
  344.5 106.0 %pmax.7 = f32[1,256]{1,0:T(1,128)} all-reduce(f32[1,256]{1,0:T(1,128)S(1)} %bitcast.104), channel_id=1, replica_groups=mesh['rot'=4,'tile'=64,'nar'=2] {'tile'}, use_global_device_ids=true, to_apply=%region_9.11 | all-reduce | flops 256 | bytes 2048 | tf_op jit(solution)/shard_map/pmax | solution.py:116
  (33 shorter events, 0.3 us)
Async XLA Ops:
  8.0 324.4 %copy-start = (bf16[8,1,18432]{2,0,1:T(8,128)(2,1)S(1)}, bf16[8,1,18432]{2,0,1:T(8,128)(2,1)}, u32[]{:S(2)}) copy-start(bf16[8,1,18432]{2,0,1:T(8,128)(2,1)} %param.23) | copy-start | bytes 884740
  8.0 13.2 %copy-start.8 = (bf16[8,2,1,3,384]{4,1,3,2,0:T(2,128)(2,1)S(1)}, bf16[8,2,1,3,384]{4,1,3,2,0:T(2,128)(2,1)}, u32[]{:S(2)}) copy-start(bf16[8,2,1,3,384]{4,1,3,2,0:T(2,128)(2,1)} %param.15) | copy-start | bytes 110596
  8.0 13.3 %copy-start.7 = (bf16[1,1,192,384]{3,2,1,0:T(8,128)(2,1)S(1)}, bf16[1,1,192,384]{3,2,1,0:T(8,128)(2,1)}, u32[]{:S(2)}) copy-start(bf16[1,1,192,384]{3,2,1,0:T(8,128)(2,1)} %param.18) | copy-start | bytes 442372
  8.0 13.3 %copy-start.1 = (bf16[2,1,1,192,384]{4,3,2,1,0:T(8,128)(2,1)S(1)}, bf16[2,1,1,192,384]{4,3,2,1,0:T(8,128)(2,1)}, u32[]{:S(2)}) copy-start(bf16[2,1,1,192,384]{4,3,2,1,0:T(8,128)(2,1)} %param.17) | copy-start | bytes 884740
  8.0 188.8 %reduce-scatter.2.cloned.1.call-start = ((), (), s32[]{:S(2)}) async-start(), calls=%async_computation.1 | async-start | bytes 884736 | tf_op jit(solution)/shard_map/reduce_scatter | solution.py:86
  20.2 1.2 copy-start.9
  166.1 1.0 copy-start.4
  166.1 1.0 copy-start.5
  166.1 1.1 copy-start.6
  167.2 1.0 copy-start.2
  167.2 1.0 copy-start.3
  168.3 1.7 copy-start.12
  169.7 149.5 %all-gather.6.cloned.1.call-start = ((), (), s32[]{:S(2)}) async-start(), calls=%async_computation.2 | async-start | bytes 9584640 | tf_op jit(solution)/shard_map/all_gather | solution.py:110
  177.0 1.9 copy-start.11
  177.0 2.0 copy-start.10
Sparse Core Ops, SparseCore 0:
  169.8 17.4 reduce-scatter.1
Sparse Core Ops, SparseCore 1:
  196.9 122.3 all-gather.5
where the time goes:
time: 459 us; the launch traced here: 458 us
  blocking collectives  206 us (45%)
  waiting for transfers between devices  95.6 us (21%)
  local copies, waits for them, and re-layouts  91.6 us (20%)
  other arithmetic  39.7 us (9%)
  between operations  16.5 us (4%)
  matrix products  8.23 us (2%)
    pmax x1, blocking collectives, shards(): best = lax.pmax(jnp.max(refined, axis=1), 'tile')  106 us
    all_gather x1, waiting for transfers between devices, shards(): lax.all_gather(binned, 'tile', axis=0, tiled=True)  95.6 us
    all_gather x1, blocking collectives, shards(): piece = lax.all_gather(weighted, 'tile', axis=3, tiled=True)  72.6 us
    gather x1, local copies, waits for them, and re-layouts, shards(): values = table[:, interp_index]  65 us
    all_gather x2, blocking collectives, merged(): lax.all_gather(part.astype(kind), axis)  22.1 us
    reduce_sum x1, other arithmetic, shards(): jnp.sum(shifted.reshape(slots, half, length // 4, 4), axis=3)  15.4 us
    unnamed x29, local copies, waits for them, and re-layouts  14.4 us
  transfers between devices with their start and end apart: 2, of which 1 were waited for; matrix products, arithmetic and copies ran while one was open for 7% of the time, Pallas kernels for 0%

commit v1 on v0

v1 whole, which is shorter than its diff:
```python
import jax
import jax.numpy as jnp
import numpy as np
from jax import lax
from jax.experimental import pallas as pl
from jax.experimental.pallas import tpu as pltpu
from jax.sharding import PartitionSpec as P

BF = jnp.bfloat16
F32 = jnp.float32
I32 = jnp.int32
LANES = 128
DFT = 384
HALF = 192
ROWS = 3
TILES = 64
SLOTS = 4
WIDE = ROWS * DFT
BINS = 288
GRID = 8
BASE = 16
VMEM_LIMIT = 48 * 1024 * 1024

VM = pl.BlockSpec(memory_space=pltpu.VMEM)
SM = pl.BlockSpec(memory_space=pltpu.SMEM)
NN = (((1,), (0,)), ((), ()))
NT = (((1,), (1,)), ((), ()))


def bf(x):
    return np.asarray(x, np.float32).astype(jnp.bfloat16)


def split(x):
    high = bf(x)
    return high, bf(np.asarray(x, np.float64) - high.astype(np.float64))


def tables():
    steps = np.arange(DFT)
    phase = (steps[:, None] * steps[None, :] % DFT) * (2.0 * np.pi / DFT)
    cosv, sinv = np.cos(phase), np.sin(phase)
    back = np.zeros((2, DFT, 2 * HALF), np.float32)
    order = np.array([ROWS * t + j for j in range(ROWS) for t in range(TILES)])
    for n in range(2):
        back[n, :, :HALF] = cosv[:, n * HALF + order]
        back[n, :, HALF:] = -sinv[:, n * HALF + order]
    ch, cl = split(cosv)
    sh, sl = split(sinv)
    tabx = np.concatenate([ch, cl, sh, sl], 1)
    return bf(back), tabx


def interpolate(index, weight, table):
    blocks = index.shape[0] // 8
    kept = index.shape[0] // 8

    def kernel(index_ref, weight_ref, table_ref, out_ref, value_ref):
        def step(v, carry):
            rows = pl.ds(pl.multiple_of(v * 8, 8), 8)
            entry = index_ref[rows, :]
            low = entry & (LANES - 1)
            high = lax.shift_right_logical(entry, 7)
            bits = [(lax.shift_right_logical(high, b) & 1) == 1 for b in range(5)]
            weights = weight_ref[rows, :]

            def pick(c, level, first):
                if level < 0:
                    row = jnp.broadcast_to(table_ref[c, first : first + 1, :], (8, LANES))
                    return jnp.take_along_axis(row, low, axis=1)
                return jnp.where(
                    bits[level],
                    pick(c, level - 1, first + (1 << level)),
                    pick(c, level - 1, first),
                )

            for c in range(2):
                value_ref[c, rows, :] = pick(c, 4, 0) * weights
            return carry

        lax.fori_loop(0, blocks, step, 0)
        for c in range(2):
            total = value_ref[c, 0:kept, :]
            for k in range(1, 8):
                total = total + value_ref[c, k * kept : (k + 1) * kept, :]
            out_ref[c] = total

    return pl.pallas_call(
        kernel,
        out_shape=jax.ShapeDtypeStruct((2, kept, LANES), F32),
        in_specs=[VM] * 3,
        out_specs=VM,
        scratch_shapes=[pltpu.VMEM((2, index.shape[0], LANES), F32)],
        name="interpolate",
    )(index, weight, table)


def correlate(nar, own, other, spec, filt, tabx, back):
    def kernel(at_ref, own_ref, other_ref, spec_ref, filt_ref, tabx_ref, back_ref, keep_ref, send_ref):
        first = at_ref[1] == 0
        mine = own_ref[...].astype(F32)
        theirs = other_ref[...].astype(F32)
        sr = jnp.where(first, mine, theirs)
        si = jnp.where(first, theirs, mine)
        parts = []
        for o in range(2):
            for j in range(ROWS):
                at = slice(j * DFT, (j + 1) * DFT)
                so = slice(o * WIDE + j * DFT, o * WIDE + (j + 1) * DFT)
                c = filt_ref[:, at].astype(F32)
                mr = spec_ref[:, at].astype(F32)
                mi = spec_ref[:, WIDE + j * DFT : WIDE + (j + 1) * DFT].astype(F32)
                cr = c * sr[:, so]
                ci = c * si[:, so]
                xr = mr * cr + mi * ci
                xi = mi * cr - mr * ci
                parts.append(jnp.concatenate([xr.astype(BF), xi.astype(BF)], axis=1))
        cross = jnp.concatenate(parts, axis=0)
        cosv, sinv = tabx_ref[:, :DFT], tabx_ref[:, 2 * DFT : 3 * DFT]
        wide = jnp.concatenate(
            [jnp.concatenate([cosv, sinv], axis=1), jnp.concatenate([-sinv, cosv], axis=1)], axis=0
        )
        halfimg = lax.dot_general(cross, wide, NN, preferred_element_type=F32).astype(BF)
        table = back_ref[at_ref[0]]
        low = at_ref[0] == 0
        for o in range(2):
            rows = halfimg[o * HALF : (o + 1) * HALF]
            both = jnp.concatenate([rows[:, :DFT], rows[:, DFT:]], axis=0)
            sums = lax.dot_general(table, both, NN, preferred_element_type=F32)
            left, right = sums[:, :HALF], sums[:, HALF:]
            keep_ref[o] = jnp.where(low, left, right).astype(BF)
            send_ref[o] = jnp.where(low, right, left).astype(BF)

    shape = jax.ShapeDtypeStruct((2, DFT, HALF), BF)
    return pl.pallas_call(
        kernel,
        out_shape=(shape, shape),
        in_specs=[SM] + [VM] * 6,
        out_specs=(VM, VM),
        compiler_params=pltpu.CompilerParams(vmem_limit_bytes=VMEM_LIMIT),
        name="correlate",
    )(nar, own, other, spec, filt, tabx, back)


def score(spec, grid, slices, meta, tabx, taby):
    def kernel(spec_ref, grid_ref, slice_ref, meta_ref, tabx_ref, taby_ref, out_ref, place_ref):
        meta = meta_ref[...].astype(F32)
        lane = lax.broadcasted_iota(I32, (TILES, DFT), 1).astype(F32)
        count = meta[:, 20:21]
        tri_r = lax.broadcasted_iota(I32, (TILES, TILES), 0)
        tri_c = lax.broadcasted_iota(I32, (TILES, TILES), 1)
        before = jnp.where(tri_c < tri_r, 1.0, 0.0).astype(BF)
        spread = jnp.broadcast_to(count, (TILES, LANES)).astype(BF)
        offset = lax.dot_general(before, spread, NN, preferred_element_type=F32)[:, 0:1]
        hot_x, hot_y, place, listed = [], [], [], []
        for i in range(SLOTS):
            y0 = meta[:, 5 * i + 1 : 5 * i + 2] * BASE + meta[:, 5 * i + 2 : 5 * i + 3]
            x0 = meta[:, 5 * i + 3 : 5 * i + 4] * BASE + meta[:, 5 * i + 4 : 5 * i + 5]
            hot_x.append(jnp.where(lane == x0, 1.0, 0.0).astype(BF))
            hot_y.append(jnp.where(lane == y0, 1.0, 0.0).astype(BF))
            valid = count > float(i)
            seat = jnp.where(valid, offset + float(i), -1.0)
            hot = jnp.where(lane[:, :256] == seat, 1.0, 0.0)
            for h in range(2):
                place_ref[h, pl.ds(i, TILES, stride=SLOTS), :] = hot[:, h * LANES : (h + 1) * LANES]
            place.append(hot.astype(BF))
        hot_x = jnp.concatenate(hot_x, axis=0)
        hot_y = jnp.concatenate(hot_y, axis=0)
        place = jnp.concatenate(place, axis=0)
        wave = lax.dot_general(hot_x, tabx_ref[...], NN, preferred_element_type=F32)
        cx = wave[:, :DFT] + wave[:, DFT : 2 * DFT]
        sx = wave[:, 2 * DFT : 3 * DFT] + wave[:, 3 * DFT :]
        tilt = lax.dot_general(hot_y, taby_ref[...], NT, preferred_element_type=F32)
        rows = []
        for i in range(SLOTS):
            at = slice(i * TILES, (i + 1) * TILES)
            second = meta[:, 5 * i : 5 * i + 1] > 0.5
            pieces = []
            for j in range(ROWS):
                cols = slice(j * DFT, (j + 1) * DFT)
                mr = spec_ref[:, cols].astype(F32)
                mi = spec_ref[:, WIDE + j * DFT : WIDE + (j + 1) * DFT].astype(F32)

                def chosen(c):
                    part = [
                        slice_ref[:, (c * 2 + o) * WIDE + j * DFT : (c * 2 + o) * WIDE + (j + 1) * DFT]
                        for o in range(2)
                    ]
                    return jnp.where(second, part[1], part[0])

                sr, si = chosen(0), chosen(1)
                pr = (mr * sr + mi * si).astype(BF).astype(F32)
                pi = (mi * sr - mr * si).astype(BF).astype(F32)
                cy = tilt[at, j : j + 1] + tilt[at, 3 + j : 4 + j]
                sy = tilt[at, 6 + j : 7 + j] + tilt[at, 9 + j : 10 + j]
                pieces.append(
                    cy * (pr * cx[at] - pi * sx[at]) - sy * (pr * sx[at] + pi * cx[at])
                )
            rows.append(jnp.concatenate(pieces, axis=1))
        shifted = jnp.concatenate(rows, axis=0)
        high = shifted.astype(BF)
        bin_of = lax.shift_right_logical(lax.broadcasted_iota(I32, (WIDE, DFT), 0), 2)
        group = jnp.where(bin_of == lax.broadcasted_iota(I32, (WIDE, DFT), 1), 1.0, 0.0).astype(BF)
        low = (shifted - high.astype(F32)).astype(BF)
        binned = lax.dot_general(high, group, NN, preferred_element_type=F32)
        binned = binned + lax.dot_general(low, group, NN, preferred_element_type=F32)
        binned = binned.astype(BF)[:, :BINS]
        values = jnp.concatenate([grid_ref[:, q * BINS : (q + 1) * BINS] for q in range(GRID)], axis=0)
        scores = lax.dot_general(values, binned, NT, preferred_element_type=F32).astype(BF)
        packed = lax.dot_general(scores, place, NN, preferred_element_type=F32)
        lanes = lax.broadcasted_iota(I32, (TILES, LANES), 1)
        extra = jnp.zeros((TILES, LANES), F32)
        for q in range(GRID):
            block = packed[q * TILES : (q + 1) * TILES]
            out_ref[:, q * LANES : (q + 1) * LANES] = block[:, :LANES].astype(BF)
            extra = jnp.where(lanes == q, block[:, LANES : LANES + 1], extra)
        out_ref[:, GRID * LANES :] = extra.astype(BF)

    return pl.pallas_call(
        kernel,
        out_shape=(
            jax.ShapeDtypeStruct((TILES, (GRID + 1) * LANES), BF),
            jax.ShapeDtypeStruct((2, SLOTS * TILES, LANES), F32),
        ),
        in_specs=[VM] * 6,
        out_specs=(VM, VM),
        compiler_params=pltpu.CompilerParams(vmem_limit_bytes=VMEM_LIMIT),
        name="score",
    )(spec, grid, slices, meta, tabx, taby)


def expand(place, values, tops):
    def kernel(place_ref, value_ref, top_ref, refined_ref, best_ref):
        exact = dict(preferred_element_type=F32, precision=lax.Precision.HIGHEST)
        place = jnp.concatenate([place_ref[0], place_ref[1]], axis=1)
        refined_ref[...] = lax.dot_general(place, value_ref[...], NT, **exact)
        top = jnp.max(top_ref[...], axis=0, keepdims=True)
        top = jnp.broadcast_to(top, (8, top.shape[1]))
        best_ref[...] = lax.dot_general(top, place, NT, **exact)[0:1]

    return pl.pallas_call(
        kernel,
        out_shape=(
            jax.ShapeDtypeStruct((SLOTS * TILES, GRID), F32),
            jax.ShapeDtypeStruct((1, SLOTS * TILES), F32),
        ),
        in_specs=[VM] * 3,
        out_specs=(VM, VM),
        name="expand",
    )(place, values, tops)


def exchange(x, axis, bit):
    size = lax.axis_size(axis)
    return lax.ppermute(x, axis, [(k, k ^ bit) for k in range(size)])


def shards(
    interp_index,
    interp_weight,
    volume,
    spectrum,
    ctf_filter,
    peak_count,
    peak_orient,
    peak_row,
    peak_col,
    ctf_grid,
):
    back, tabx = [jnp.asarray(t) for t in tables()]
    nar = lax.axis_index("nar")
    tile = lax.axis_index("tile")

    taby = lax.dynamic_slice_in_dim(tabx, (nar * TILES + tile) * ROWS, ROWS, 0)
    taby = taby.reshape(ROWS, 4, DFT).transpose(1, 0, 2).reshape(4 * ROWS, DFT)
    taby = jnp.pad(taby, ((0, 16 - 4 * ROWS), (0, 0)))

    slices = interpolate(
        interp_index.reshape(-1, LANES),
        interp_weight.reshape(-1, LANES).astype(F32),
        volume.reshape(2, -1, LANES).astype(F32),
    ).astype(BF)

    spec = spectrum.reshape(2, TILES, WIDE).transpose(1, 0, 2).reshape(TILES, 2 * WIDE)
    filt = ctf_filter.reshape(TILES, WIDE)
    grid = ctf_grid.reshape(GRID, TILES, BINS).transpose(1, 0, 2).reshape(TILES, GRID * BINS)
    fields = jnp.stack(
        [peak_orient, peak_row // BASE, peak_row % BASE, peak_col // BASE, peak_col % BASE], axis=1
    ).reshape(-1)
    fields = jnp.pad(jnp.concatenate([fields, peak_count.reshape(1)]), (0, LANES - 5 * SLOTS - 1)).astype(BF)
    core = (jnp.arange(TILES, dtype=I32) % 2)[:, None]
    flat = slices.reshape(2, 1, 2 * WIDE)
    payload = jnp.concatenate(
        [
            jnp.where(core == 0, flat[0], flat[1]),
            spec,
            grid,
            jnp.broadcast_to(fields[None], (TILES, LANES)),
        ],
        axis=1,
    )
    got = lax.all_to_all(payload, "tile", 0, 0, tiled=True)
    mine = got[:, : 2 * WIDE]
    other = exchange(mine, "tile", 1)
    packed, place = score(
        got[:, 2 * WIDE : 4 * WIDE],
        got[:, 4 * WIDE : 4 * WIDE + GRID * BINS],
        slices.reshape(1, 4 * WIDE).astype(F32),
        got[:, 4 * WIDE + GRID * BINS :],
        tabx,
        taby,
    )
    keep, send = correlate(jnp.stack([nar, tile % 2]), mine, other, spec, filt, tabx, back)
    extra_rows = exchange(send, "nar", 1)

    sums = lax.all_to_all(packed, "tile", 0, 0, tiled=True)
    sums = jnp.sum(sums.astype(F32), axis=0)
    sums = lax.psum(sums, "nar") * (1.0 / DFT)
    last = jnp.zeros((GRID, LANES), F32).at[:, 0].set(sums[GRID * LANES : GRID * LANES + GRID])
    values = jnp.concatenate([sums[: GRID * LANES].reshape(GRID, LANES), last], axis=1)
    top = jnp.max(values, axis=0)

    corr = (keep.astype(F32) + extra_rows.astype(F32)) * (1.0 / DFT)
    stats = jnp.stack([jnp.maximum(corr[0], corr[1]), corr[0] + corr[1]]).astype(BF)
    others = [exchange(stats, "rot", bit) for bit in (1, 2, 3)]

    tops = lax.all_to_all(jnp.broadcast_to(top[None], (TILES, 2 * LANES)), "tile", 0, 0, tiled=True)
    refined, best = expand(place, values, tops)

    everything = [x.astype(F32) for x in [stats] + others]
    peak = jnp.maximum(
        jnp.maximum(everything[0][0], everything[1][0]), jnp.maximum(everything[2][0], everything[3][0])
    )
    total = (everything[0][1] + everything[1][1]) + (everything[2][1] + everything[3][1])
    return (
        peak.reshape(1, 1, -1),
        (total * (1.0 / 8)).reshape(1, 1, -1),
        refined.reshape(1, SLOTS * TILES, GRID),
        best,
    )


def solution(mesh):
    return jax.shard_map(
        shards,
        mesh=mesh,
        in_specs=(
            P(None, "rot", "nar", "tile", None),
            P(None, "rot", "nar", "tile", None),
            P(None, "nar", "tile", None),
            P(None, "tile", "nar", None, None),
            P("tile", "nar", None, None),
            P("rot", "tile"),
            P(("rot", "tile")),
            P(("rot", "tile")),
            P(("rot", "tile")),
            P("tile", "nar", None),
        ),
        out_specs=(
            P("tile", "nar", None),
            P("tile", "nar", None),
            P("rot", None, "tile"),
            P("rot", None),
        ),
        check_vma=False,
    )
```

time: 459 us -> 170 us (0.37)
  blocking collectives: 206 us -> 32.4 us
  local copies, waits for them, and re-layouts: 91.6 us -> 17.8 us
  waiting for transfers between devices: 95.6 us -> 51.8 us
  starting transfers between devices: 0.26 us -> 43.4 us
  other arithmetic: 39.7 us -> 8.02 us
  between operations: 16.5 us -> 1.7 us
  Pallas kernels: 0 us -> 13.5 us
  matrix products: 8.23 us -> 0 us
    pmax x1 -> x0, blocking collectives: 106 us -> none  [shards(): best = lax.pmax(jnp.max(refined, axis=1), 'tile')]
    all_gather x1 -> x0, waiting for transfers between devices: 95.6 us -> none  [shards(): lax.all_gather(binned, 'tile', axis=0, tiled=True)]
    all_gather x3 -> x0, blocking collectives: 94.7 us -> none  [the longest x1 72.6 us: shards(): piece = lax.all_gather(weighted, 'tile', axis=3, tiled=True)]
    gather x3 -> x0, local copies, waits for them, and re-layouts: 67.3 us -> none  [the longest x1 65 us: shards(): values = table[:, interp_index]]
    all_to_all x0 -> x2, waiting for transfers between devices: none -> 51.4 us  [the longest x1 45.2 us: shards(): got = lax.all_to_all(payload, 'tile', 0, 0, tiled=True)]
    all_to_all x0 -> x2, starting transfers between devices: none -> 27.1 us  [the longest x1 18.1 us: shards(): got = lax.all_to_all(payload, 'tile', 0, 0, tiled=True)]
    all_to_all x0 -> x1, blocking collectives: none -> 27.1 us  [shards(): lax.all_to_all(jnp.broadcast_to(top[None], (TILES, 2 * LANES)), 'tile', 0...]
    reduce_sum x3 -> x1, other arithmetic: 22.1 us -> 0.28 us  [shards(): sums = jnp.sum(sums.astype(F32), axis=0)]
  transfers between devices with their start and end apart: 2 -> 7, of which waited for: 1 -> 3; matrix products, arithmetic and copies ran while one was open for 7% -> 3% of each run, Pallas kernels for 0% -> 4%
where the time goes in v1:
time: 170 us; the launch traced here: 169 us
  waiting for transfers between devices  51.8 us (30%)
  starting transfers between devices  43.4 us (26%)
  blocking collectives  32.4 us (19%)
  local copies, waits for them, and re-layouts  17.8 us (10%)
  Pallas kernels  13.5 us (8%)
  other arithmetic  8.02 us (5%)
  between operations  1.7 us (1%)
    all_to_all x1, waiting for transfers between devices, shards(): got = lax.all_to_all(payload, 'tile', 0, 0, tiled=True)  45.2 us
    all_to_all x1, blocking collectives, shards(): lax.all_to_all(jnp.broadcast_to(top[None], (TILES, 2 * LANES)), 'tile', 0...  27.1 us
    all_to_all x1, starting transfers between devices, shards(): got = lax.all_to_all(payload, 'tile', 0, 0, tiled=True)  18.1 us
    ppermute x5, starting transfers between devices, exchange(): return lax.ppermute(x, axis, [(k, k ^ bit) for k in range(size)])  16.3 us
    unnamed x19, local copies, waits for them, and re-layouts  10.6 us
    all_to_all x1, starting transfers between devices, shards(): sums = lax.all_to_all(packed, 'tile', 0, 0, tiled=True)  9.03 us
    all_to_all x1, waiting for transfers between devices, shards(): sums = lax.all_to_all(packed, 'tile', 0, 0, tiled=True)  6.18 us
    psum x1, blocking collectives, shards(): sums = lax.psum(sums, 'nar') * (1.0 / DFT)  5.36 us
  transfers between devices with their start and end apart: 7, of which 3 were waited for; matrix products, arithmetic and copies ran while one was open for 3% of the time, Pallas kernels for 4%

profile of v1, /device:TPU:1, one launch (start us, length us, event | category | flops | bytes accessed | tf_op | source)
XLA Modules:
  0.0 168.7 jit_solution(18207479567725438692)
XLA Ops:
  1.3 0.7 convert_bitcast_fusion.3
  2.0 0.7 fusion.7
  2.7 0.1 copy.39
  2.8 0.1 reshape.223
  2.9 0.7 convert_bitcast_fusion
  3.7 0.6 copy.55
  4.3 0.8 copy.36
  5.1 0.7 reshape.230.weight_ref
  5.7 4.1 %interpolate.1 = f32[2,18,128]{2,1,0:T(8,128)} custom-call(s32[144,128]{1,0:T(8,128)} %bitcast.66, f32[144,128]{1,0:T(8,128)} %reshape.230.weight_ref, f32[2,32,128]{2,1,0:T(8,128)} %bitcast.64), custom_call_target="tpu_custom_call" | custom-call | tf_op jit(solution)/shard_map/interpolate/pallas_call | solution.py:88
  9.9 0.7 convert_element_type.48
  10.6 1.1 reshape.219
  11.7 0.3 copy.37
  12.1 0.6 reshape.221
  12.7 0.2 copy.53
  12.9 0.3 reshape.222
  13.3 0.1 fusion.4
  13.3 0.1 broadcast_select_fusion
  13.4 0.2 maximum_bitcast_fusion
  13.6 0.5 broadcast.149
  14.1 1.3 reduce.9
  15.4 0.0 copy-start
  15.4 1.9 %reshape.234 = bf16[64,2,3520]{2,1,0:T(2,128)(2,1)} reshape(bf16[64,7040]{1,0:T(8,128)(2,1)S(1)} %reduce.9) | data formatting | bytes 1802240
  17.3 18.1 %all-to-all-start = ((bf16[64,2,3520]{2,1,0:T(2,128)(2,1)}), bf16[64,2,3520]{2,1,0:T(2,128)(2,1)S(1)}, u32[]{:S(2)}, u32[]{:S(2)}) async-start(bf16[64,2,3520]{2,1,0:T(2,128)(2,1)} %reshape.234), calls=%async_computation | async-start | bytes 1835008 | tf_op jit(solution)/shard_map/all_to_all | solution.py:302
  35.5 45.2 %all-to-all-done = bf16[64,2,3520]{2,1,0:T(2,128)(2,1)S(1)} async-done(((bf16[64,2,3520]{2,1,0:T(2,128)(2,1)}), bf16[64,2,3520]{2,1,0:T(2,128)(2,1)S(1)}, u32[]{:S(2)}, u32[]{:S(2)}) %all-to-all-start) | async-done | bytes 901152 | tf_op jit(solution)/shard_map/all_to_all | solution.py:302
  80.7 2.4 %reshape.235 = bf16[64,1,7040]{2,1,0:T(2,128)(2,1)} reshape(bf16[64,2,3520]{2,1,0:T(2,128)(2,1)S(1)} %all-to-all-done) | data formatting | bytes 1802240
  83.1 1.6 copy.52
  84.7 0.1 fusion.12
  84.8 0.0 copy-start.4
  84.8 0.0 copy-start.1
  84.8 2.9 %score.1 = (bf16[64,1152]{1,0:T(8,128)(2,1)S(1)}, f32[2,256,128]{2,1,0:T(8,128)S(1)}) custom-call(bf16[64,2304]{1,0:T(8,128)(2,1)S(1)} %get-tuple-element.47.spec_ref, bf16[64,2304]{1,0:T(8,128)(2,1)S(1)} %get-tuple-element.46.grid_ref, f32[1,4608]{1,0:T(1,128)S(1)} %reshape.232.slice_ref, bf16[64,128]{1,0:T(8,128)(2,1)S(1)} %slice.116.meta_ref, ...), custom_call_target="tpu_custom_call" | custom-call | tf_op jit(solution)/shard_map/score/pallas_call | solution.py:219
  87.7 0.0 copy-start.2
  87.7 0.7 copy-done.2
  88.4 0.7 reduce.10
  89.1 0.9 reshape.236
  90.0 9.0 %all-to-all-start.1 = ((bf16[64,2,576]{2,1,0:T(2,128)(2,1)}), bf16[64,2,576]{2,1,0:T(2,128)(2,1)S(1)}, u32[]{:S(2)}, u32[]{:S(2)}) async-start(bf16[64,2,576]{2,1,0:T(2,128)(2,1)} %reshape.236), calls=%async_computation.1 | async-start | bytes 327680 | tf_op jit(solution)/shard_map/all_to_all | solution.py:316
  99.0 2.4 %collective-permute-start = (bf16[64,2304]{1,0:T(8,128)(2,1)S(1)}, bf16[64,2304]{1,0:T(8,128)(2,1)S(1)}, u32[]{:S(2)}, u32[]{:S(2)}) collective-permute-start(bf16[64,2304]{1,0:T(8,128)(2,1)S(1)} %get-tuple-element.48.own_ref), channel_id=1, source_target_pairs={{0,2},{2,0},{4,6},{6,4},{8,10},{10,8},{12,14},{14,12},{16,18},{18,... | collective-permute-start | bytes 884744 | tf_op jit(solution)/shard_map/ppermute | solution.py:255
  101.4 0.1 reshape.225.filt_ref
  101.5 0.7 compare_reduce_fusion
  102.2 0.1 pad_add_fusion.at_ref
  102.2 0.3 collective-permute-done.other_ref
  102.6 4.3 %correlate.1 = (bf16[2,384,192]{2,1,0:T(8,128)(2,1)S(1)}, bf16[2,384,192]{2,1,0:T(8,128)(2,1)}) custom-call(s32[2]{0:T(128)S(1)} %pad_add_fusion.at_ref, bf16[64,2304]{1,0:T(8,128)(2,1)S(1)} %get-tuple-element.48.own_ref, bf16[64,2304]{1,0:T(8,128)(2,1)S(1)} %collective-permute-done.other_ref, bf16[64,2304]{1,0:T(8,128)(2,1)S(1)} %bitcast.57, ...), custom_call_target="tpu_custom_call" | custom-call | tf_op jit(solution)/shard_map/correlate/pallas_call | solution.py:135
  106.9 4.3 %collective-permute-start.1 = (bf16[2,384,192]{2,1,0:T(8,128)(2,1)}, bf16[2,384,192]{2,1,0:T(8,128)(2,1)S(1)}, u32[]{:S(2)}, u32[]{:S(2)}) collective-permute-start(bf16[2,384,192]{2,1,0:T(8,128)(2,1)} %get-tuple-element.23), channel_id=1, source_target_pairs={{0,1},{1,0},{2,3},{3,2},{4,5},{5,4},{6,7},{7,6},{8,9},{9,8},{10,11... | collective-permute-start | bytes 884744 | tf_op jit(solution)/shard_map/ppermute | solution.py:255
  111.3 6.2 %all-to-all-done.1 = bf16[64,2,576]{2,1,0:T(2,128)(2,1)S(1)} async-done(((bf16[64,2,576]{2,1,0:T(2,128)(2,1)}), bf16[64,2,576]{2,1,0:T(2,128)(2,1)S(1)}, u32[]{:S(2)}, u32[]{:S(2)}) %all-to-all-start.1) | async-done | bytes 147488 | tf_op jit(solution)/shard_map/all_to_all | solution.py:316
  117.5 0.2 reshape.237
  117.7 0.3 convert_reduce_fusion
  118.0 5.4 %psum.7 = f32[1152]{0:T(1024)S(1)} all-reduce(f32[1152]{0:T(1024)S(1)} %convert_reduce_fusion), channel_id=1, replica_groups=mesh['rot'=4,'tile'=64,'nar'=2] {'nar'}, use_global_device_ids=true, to_apply=%region_1.2 | all-reduce | flops 1152 | bytes 9216 | tf_op jit(solution)/shard_map/psum | solution.py:318
  123.4 0.6 fusion.3
  124.0 0.1 copy.42
  124.1 0.1 add_multiply_fusion
  124.3 0.1 fusion.11
  124.4 5.0 %collective-permute-start.3 = (bf16[2,384,192]{2,1,0:T(8,128)(2,1)S(1)}, bf16[2,384,192]{2,1,0:T(8,128)(2,1)S(1)}, u32[]{:S(2)}, u32[]{:S(2)}) collective-permute-start(bf16[2,384,192]{2,1,0:T(8,128)(2,1)S(1)} %get-tuple-element.50), channel_id=1, source_target_pairs={{0,256},{128,384},{256,0},{384,128},{1,257},{129,385},{257,1},{385... | collective-permute-start | bytes 884744 | tf_op jit(solution)/shard_map/ppermute | solution.py:255
  129.4 2.3 %collective-permute-start.2 = (bf16[2,384,192]{2,1,0:T(8,128)(2,1)S(1)}, bf16[2,384,192]{2,1,0:T(8,128)(2,1)S(1)}, u32[]{:S(2)}, u32[]{:S(2)}) collective-permute-start(bf16[2,384,192]{2,1,0:T(8,128)(2,1)S(1)} %get-tuple-element.50), channel_id=1, source_target_pairs={{0,128},{128,0},{256,384},{384,256},{1,129},{129,1},{257,385},{385... | collective-permute-start | bytes 884744 | tf_op jit(solution)/shard_map/ppermute | solution.py:255
  131.7 2.3 %collective-permute-start.4 = (bf16[2,384,192]{2,1,0:T(8,128)(2,1)S(1)}, bf16[2,384,192]{2,1,0:T(8,128)(2,1)S(1)}, u32[]{:S(2)}, u32[]{:S(2)}) collective-permute-start(bf16[2,384,192]{2,1,0:T(8,128)(2,1)S(1)} %get-tuple-element.50), channel_id=1, source_target_pairs={{0,384},{128,256},{256,128},{384,0},{1,385},{129,257},{257,129},{3... | collective-permute-start | bytes 884744 | tf_op jit(solution)/shard_map/ppermute | solution.py:255
  134.0 0.6 fusion.10
  134.7 27.1 %all_to_all.29 = f32[64,1,256]{2,1,0:T(1,128)S(1)} all-to-all(f32[64,1,256]{2,1,0:T(1,128)S(1)} %broadcast_in_dim.48), channel_id=1, replica_groups=mesh['rot'=4,'tile'=64,'nar'=2] {'tile'}, dimensions={0} | all-to-all | bytes 131072 | tf_op jit(solution)/shard_map/all_to_all | solution.py:327
  161.8 0.6 copy.54
  162.4 2.2 %expand.1 = (f32[256,8]{1,0:T(8,128)}, f32[1,256]{1,0:T(1,128)}) custom-call(f32[2,256,128]{2,1,0:T(8,128)} %copy-done.2, f32[8,256]{1,0:T(8,128)} %get-tuple-element.54.value_ref, f32[64,256]{1,0:T(8,128)} %bitcast.63), custom_call_target="tpu_custom_call" | custom-call | tf_op jit(solution)/shard_map/expand/pallas_call | solution.py:241
  164.5 1.6 copy.43
  166.1 0.1 convert_element_type.53
  166.2 0.1 convert_element_type.52
  166.3 0.1 convert_element_type.54
  166.3 0.2 fusion.1
  166.5 1.1 mul.38
  167.6 1.1 max.43
  (24 shorter events, 0.3 us)
Async XLA Ops:
  0.6 11.4 %copy-start.3 = (bf16[8,1,18432]{2,0,1:T(8,128)(2,1)S(1)}, bf16[8,1,18432]{2,0,1:T(8,128)(2,1)}, u32[]{:S(2)}) copy-start(bf16[8,1,18432]{2,0,1:T(8,128)(2,1)} %param.23) | copy-start | bytes 884740
  15.4 20.0 %copy-start = (bf16[384,1536]{1,0:T(8,128)(2,1)S(1)}, bf16[384,1536]{1,0:T(8,128)(2,1)}, u32[]{:S(2)}) copy-start(bf16[384,1536]{1,0:T(8,128)(2,1)} %constant.122.clone.tabx_ref) | copy-start | bytes 3538948
  17.3 63.4 %all-to-all-start = ((bf16[64,2,3520]{2,1,0:T(2,128)(2,1)}), bf16[64,2,3520]{2,1,0:T(2,128)(2,1)S(1)}, u32[]{:S(2)}, u32[]{:S(2)}) async-start(bf16[64,2,3520]{2,1,0:T(2,128)(2,1)} %reshape.234), calls=%async_computation | async-start | bytes 1835008 | tf_op jit(solution)/shard_map/all_to_all | solution.py:302
  84.8 16.6 %copy-start.4 = (bf16[1,1,192,384]{3,2,1,0:T(8,128)(2,1)S(1)}, bf16[1,1,192,384]{3,2,1,0:T(8,128)(2,1)}, u32[]{:S(2)}) copy-start(bf16[1,1,192,384]{3,2,1,0:T(8,128)(2,1)} %param.18) | copy-start | bytes 442372
  84.8 17.8 %copy-start.1 = (bf16[2,384,384]{2,1,0:T(8,128)(2,1)S(1)}, bf16[2,384,384]{2,1,0:T(8,128)(2,1)}, u32[]{:S(2)}) copy-start(bf16[2,384,384]{2,1,0:T(8,128)(2,1)} %constant.121.clone.back_ref) | copy-start | bytes 1769476
  87.7 0.7 copy-start.2
  90.0 27.5 %all-to-all-start.1 = ((bf16[64,2,576]{2,1,0:T(2,128)(2,1)}), bf16[64,2,576]{2,1,0:T(2,128)(2,1)S(1)}, u32[]{:S(2)}, u32[]{:S(2)}) async-start(bf16[64,2,576]{2,1,0:T(2,128)(2,1)} %reshape.236), calls=%async_computation.1 | async-start | bytes 327680 | tf_op jit(solution)/shard_map/all_to_all | solution.py:316
  99.0 3.6 %collective-permute-start = (bf16[64,2304]{1,0:T(8,128)(2,1)S(1)}, bf16[64,2304]{1,0:T(8,128)(2,1)S(1)}, u32[]{:S(2)}, u32[]{:S(2)}) collective-permute-start(bf16[64,2304]{1,0:T(8,128)(2,1)S(1)} %get-tuple-element.48.own_ref), channel_id=1, source_target_pairs={{0,2},{2,0},{4,6},{6,4},{8,10},{10,8},{12,14},{14,12},{16,18},{18,... | collective-permute-start | bytes 884744 | tf_op jit(solution)/shard_map/ppermute | solution.py:255
  106.9 17.2 %collective-permute-start.1 = (bf16[2,384,192]{2,1,0:T(8,128)(2,1)}, bf16[2,384,192]{2,1,0:T(8,128)(2,1)S(1)}, u32[]{:S(2)}, u32[]{:S(2)}) collective-permute-start(bf16[2,384,192]{2,1,0:T(8,128)(2,1)} %get-tuple-element.23), channel_id=1, source_target_pairs={{0,1},{1,0},{2,3},{3,2},{4,5},{5,4},{6,7},{7,6},{8,9},{9,8},{10,11... | collective-permute-start | bytes 884744 | tf_op jit(solution)/shard_map/ppermute | solution.py:255
  124.4 41.7 %collective-permute-start.3 = (bf16[2,384,192]{2,1,0:T(8,128)(2,1)S(1)}, bf16[2,384,192]{2,1,0:T(8,128)(2,1)S(1)}, u32[]{:S(2)}, u32[]{:S(2)}) collective-permute-start(bf16[2,384,192]{2,1,0:T(8,128)(2,1)S(1)} %get-tuple-element.50), channel_id=1, source_target_pairs={{0,256},{128,384},{256,0},{384,128},{1,257},{129,385},{257,1},{385... | collective-permute-start | bytes 884744 | tf_op jit(solution)/shard_map/ppermute | solution.py:255
  129.4 36.8 %collective-permute-start.2 = (bf16[2,384,192]{2,1,0:T(8,128)(2,1)S(1)}, bf16[2,384,192]{2,1,0:T(8,128)(2,1)S(1)}, u32[]{:S(2)}, u32[]{:S(2)}) collective-permute-start(bf16[2,384,192]{2,1,0:T(8,128)(2,1)S(1)} %get-tuple-element.50), channel_id=1, source_target_pairs={{0,128},{128,0},{256,384},{384,256},{1,129},{129,1},{257,385},{385... | collective-permute-start | bytes 884744 | tf_op jit(solution)/shard_map/ppermute | solution.py:255
  131.7 34.5 %collective-permute-start.4 = (bf16[2,384,192]{2,1,0:T(8,128)(2,1)S(1)}, bf16[2,384,192]{2,1,0:T(8,128)(2,1)S(1)}, u32[]{:S(2)}, u32[]{:S(2)}) collective-permute-start(bf16[2,384,192]{2,1,0:T(8,128)(2,1)S(1)} %get-tuple-element.50), channel_id=1, source_target_pairs={{0,384},{128,256},{256,128},{384,0},{1,385},{129,257},{257,129},{3... | collective-permute-start | bytes 884744 | tf_op jit(solution)/shard_map/ppermute | solution.py:255

commit v2 on v1

v2 whole, which is shorter than its diff:
```python
import jax
import jax.numpy as jnp
import numpy as np
from jax import lax
from jax.experimental import pallas as pl
from jax.experimental.pallas import tpu as pltpu
from jax.sharding import PartitionSpec as P

BF = jnp.bfloat16
F32 = jnp.float32
I32 = jnp.int32
LANES = 128
DFT = 384
HALF = 192
ROWS = 3
TILES = 64
SLOTS = 4
WIDE = ROWS * DFT
BINS = 288
GRID = 8
BASE = 16
BLOCKS = 9
XROWS = 40
SROWS = 24
ORIENTS = 8
VMEM_LIMIT = 48 * 1024 * 1024

VM = pl.BlockSpec(memory_space=pltpu.VMEM)
SM = pl.BlockSpec(memory_space=pltpu.SMEM)
NN = (((1,), (0,)), ((), ()))
NT = (((1,), (1,)), ((), ()))


def bf(x):
    return np.asarray(x, np.float32).astype(jnp.bfloat16)


def split(x):
    high = bf(x)
    return high, bf(np.asarray(x, np.float64) - high.astype(np.float64))


def tables():
    steps = np.arange(DFT)
    phase = (steps[:, None] * steps[None, :] % DFT) * (2.0 * np.pi / DFT)
    cosv, sinv = np.cos(phase), np.sin(phase)
    rows = np.concatenate([steps[0::2], steps[1::2]])
    order = np.array([ROWS * t + j for j in range(ROWS) for t in range(TILES)])
    back = np.zeros((2, DFT, 2 * HALF), np.float32)
    for n in range(2):
        back[n, :, :HALF] = cosv[rows][:, n * HALF + order]
        back[n, :, HALF:] = -sinv[rows][:, n * HALF + order]
    ch, cl = split(cosv)
    sh, sl = split(sinv)
    return bf(back), np.concatenate([ch, cl, sh, sl], 1)


def every(ref, row, step):
    return ref[pl.ds(row, TILES, stride=step), :]


def prepare(spectrum, grid, meta):
    def kernel(spec_ref, grid_ref, meta_ref, out_ref, spec_s, out_s):
        for c in range(2):
            for b in range(ROWS):
                spec_s[c * ROWS + b] = spec_ref[c, :, b * LANES : (b + 1) * LANES].astype(F32)
        for c in range(2):
            for j in range(ROWS):
                for b in range(ROWS):
                    row = c * BLOCKS + j * ROWS + b
                    out_s[pl.ds(row, TILES, stride=XROWS), :] = spec_s[c * ROWS + b, pl.ds(j, TILES, stride=ROWS), :]
        for r in range(2 * BLOCKS):
            block = grid_ref[:, r * LANES : (r + 1) * LANES].astype(F32)
            out_s[pl.ds(2 * BLOCKS + r, TILES, stride=XROWS), :] = block
        fields = jnp.broadcast_to(meta_ref[...], (TILES, LANES))
        for r in range(4 * BLOCKS, XROWS):
            out_s[pl.ds(r, TILES, stride=XROWS), :] = fields
        out_ref[...] = out_s[...].astype(BF).reshape(out_ref.shape)

    return pl.pallas_call(
        kernel,
        out_shape=jax.ShapeDtypeStruct((TILES, XROWS, LANES), BF),
        in_specs=[VM] * 3,
        out_specs=VM,
        scratch_shapes=[
            pltpu.VMEM((2 * ROWS, HALF, LANES), F32),
            pltpu.VMEM((TILES * XROWS, LANES), F32),
        ],
        compiler_params=pltpu.CompilerParams(vmem_limit_bytes=VMEM_LIMIT),
        name="prepare",
    )(spectrum, grid, meta)


def interpolate(index, weight, table):
    steps = index.shape[0] // 16
    kept = index.shape[0] // 8

    def kernel(index_ref, weight_ref, table_ref, out_ref, own_ref, value_ref):
        def step(v, carry):
            pair = pl.ds(pl.multiple_of(v * 16, 16), 16)
            weights = weight_ref[pair, :].astype(F32)
            for s in range(2):
                rows = pl.ds(pl.multiple_of(v * 16 + s * 8, 8), 8)
                entry = index_ref[rows, :]
                low = entry & (LANES - 1)
                high = lax.shift_right_logical(entry, 7)
                bits = [(lax.shift_right_logical(high, b) & 1) == 1 for b in range(5)]

                def pick(c, level, first):
                    if level < 0:
                        row = jnp.broadcast_to(table_ref[c, first : first + 1, :], (8, LANES))
                        return jnp.take_along_axis(row, low, axis=1)
                    return jnp.where(
                        bits[level],
                        pick(c, level - 1, first + (1 << level)),
                        pick(c, level - 1, first),
                    )

                for c in range(2):
                    value_ref[c, rows, :] = pick(c, 4, 0) * weights[s * 8 : (s + 1) * 8]
            return carry

        lax.fori_loop(0, steps, step, 0)
        for c in range(2):
            total = value_ref[c, 0:kept, :]
            for k in range(1, 8):
                total = total + value_ref[c, k * kept : (k + 1) * kept, :]
            rounded = total.astype(BF)
            own_ref[c] = rounded.astype(F32)
            block = jnp.concatenate([rounded.astype(F32), jnp.zeros((SROWS - kept, LANES), F32)], axis=0).astype(BF)
            for t in range(c, TILES, 2):
                out_ref[t] = block

    return pl.pallas_call(
        kernel,
        out_shape=(
            jax.ShapeDtypeStruct((TILES, SROWS, LANES), BF),
            jax.ShapeDtypeStruct((2, kept, LANES), F32),
        ),
        in_specs=[VM] * 3,
        out_specs=(VM, VM),
        scratch_shapes=[pltpu.VMEM((2, index.shape[0], LANES), F32)],
        compiler_params=pltpu.CompilerParams(vmem_limit_bytes=VMEM_LIMIT),
        name="interpolate",
    )(index, weight, table)


def correlate(place, own, other, spectrum, filt, tabx, back):
    def kernel(at_ref, own_ref, other_ref, spec_ref, filt_ref, tabx_ref, back_ref, keep_ref, send_ref, sl_s, spec_s):
        first = at_ref[1] == 0
        mine = own_ref[...].astype(F32).reshape(TILES * SROWS, LANES)
        theirs = other_ref[...].astype(F32).reshape(TILES * SROWS, LANES)
        sl_s[0] = jnp.where(first, mine, theirs)
        sl_s[1] = jnp.where(first, theirs, mine)
        for c in range(2):
            for b in range(ROWS):
                spec_s[c * ROWS + b] = spec_ref[c, :, b * LANES : (b + 1) * LANES].astype(F32)
        for b in range(ROWS):
            spec_s[2 * ROWS + b] = filt_ref[:, b * LANES : (b + 1) * LANES].astype(F32)
        real = [[None] * (ROWS * ROWS) for _ in range(2)]
        imag = [[None] * (ROWS * ROWS) for _ in range(2)]
        for j in range(ROWS):
            for b in range(ROWS):
                mr = every(spec_s.at[b], j, ROWS)
                mi = every(spec_s.at[ROWS + b], j, ROWS)
                c = every(spec_s.at[2 * ROWS + b], j, ROWS)
                for o in range(2):
                    row = o * BLOCKS + j * ROWS + b
                    cr = c * every(sl_s.at[0], row, SROWS)
                    ci = c * every(sl_s.at[1], row, SROWS)
                    real[o][j * ROWS + b] = (mr * cr + mi * ci).astype(BF)
                    imag[o][j * ROWS + b] = (mi * cr - mr * ci).astype(BF)
        cross = jnp.concatenate(
            [
                jnp.concatenate(real[o][j * ROWS : (j + 1) * ROWS] + imag[o][j * ROWS : (j + 1) * ROWS], axis=1)
                for o in range(2)
                for j in range(ROWS)
            ],
            axis=0,
        )
        cosv, sinv = tabx_ref[:, :DFT], tabx_ref[:, 2 * DFT : 3 * DFT]
        wide = jnp.concatenate(
            [jnp.concatenate([cosv, sinv], axis=1), jnp.concatenate([-sinv, cosv], axis=1)], axis=0
        )
        halfimg = lax.dot_general(cross, wide, NN, preferred_element_type=F32).astype(BF)
        table = back_ref[at_ref[0]]
        low = at_ref[0] == 0
        for o in range(2):
            rows = halfimg[o * HALF : (o + 1) * HALF]
            both = jnp.concatenate([rows[:, :DFT], rows[:, DFT:]], axis=0)
            sums = lax.dot_general(table, both, NN, preferred_element_type=F32)
            left = jnp.concatenate([sums[:HALF, :HALF], sums[HALF:, :HALF]], axis=1)
            right = jnp.concatenate([sums[:HALF, HALF:], sums[HALF:, HALF:]], axis=1)
            keep_ref[o] = jnp.where(low, left, right).astype(BF)
            send_ref[o] = jnp.where(low, right, left).astype(BF)

    shape = jax.ShapeDtypeStruct((2, HALF, DFT), BF)
    return pl.pallas_call(
        kernel,
        out_shape=(shape, shape),
        in_specs=[SM] + [VM] * 6,
        out_specs=(VM, VM),
        scratch_shapes=[
            pltpu.VMEM((2, TILES * SROWS, LANES), F32),
            pltpu.VMEM((3 * ROWS, HALF, LANES), F32),
        ],
        compiler_params=pltpu.CompilerParams(vmem_limit_bytes=VMEM_LIMIT),
        name="correlate",
    )(place, own, other, spectrum, filt, tabx, back)


def score(got, slices, tabx, taby):
    def kernel(got_ref, slice_ref, tabx_ref, taby_ref, out_ref, place_ref, got_s):
        got_s[...] = got_ref[...].astype(F32).reshape(got_s.shape)
        meta = every(got_s, 4 * BLOCKS, XROWS)
        lane = lax.broadcasted_iota(I32, (TILES, DFT), 1).astype(F32)
        count = meta[:, 20:21]
        tri_r = lax.broadcasted_iota(I32, (TILES, TILES), 0)
        tri_c = lax.broadcasted_iota(I32, (TILES, TILES), 1)
        before = jnp.where(tri_c < tri_r, 1.0, 0.0).astype(BF)
        spread = jnp.broadcast_to(count, (TILES, LANES)).astype(BF)
        offset = lax.dot_general(before, spread, NN, preferred_element_type=F32)[:, 0:1]
        hot_x, hot_y, place = [], [], []
        for i in range(SLOTS):
            y0 = meta[:, 5 * i + 1 : 5 * i + 2] * BASE + meta[:, 5 * i + 2 : 5 * i + 3]
            x0 = meta[:, 5 * i + 3 : 5 * i + 4] * BASE + meta[:, 5 * i + 4 : 5 * i + 5]
            hot_x.append(jnp.where(lane == x0, 1.0, 0.0).astype(BF))
            hot_y.append(jnp.where(lane == y0, 1.0, 0.0).astype(BF))
            seat = jnp.where(count > float(i), offset + float(i), -1.0)
            hot = jnp.where(lane[:, :256] == seat, 1.0, 0.0)
            for h in range(2):
                place_ref[h, pl.ds(i, TILES, stride=SLOTS), :] = hot[:, h * LANES : (h + 1) * LANES]
            place.append(hot.astype(BF))
        hot_x = jnp.concatenate(hot_x, axis=0)
        hot_y = jnp.concatenate(hot_y, axis=0)
        place = jnp.concatenate(place, axis=0)
        wave = lax.dot_general(hot_x, tabx_ref[...], NN, preferred_element_type=F32)
        cx = wave[:, :DFT] + wave[:, DFT : 2 * DFT]
        sx = wave[:, 2 * DFT : 3 * DFT] + wave[:, 3 * DFT :]
        tilt = lax.dot_general(hot_y, taby_ref[...], NT, preferred_element_type=F32)
        pieces = [[] for _ in range(SLOTS)]
        for j in range(ROWS):
            for b in range(ROWS):
                r = j * ROWS + b
                cols = slice(b * LANES, (b + 1) * LANES)
                mr = every(got_s, r, XROWS)
                mi = every(got_s, BLOCKS + r, XROWS)
                plain = []
                for o in range(2):
                    sr = slice_ref[0, o * BLOCKS + r : o * BLOCKS + r + 1, :]
                    si = slice_ref[1, o * BLOCKS + r : o * BLOCKS + r + 1, :]
                    plain.append(((mr * sr + mi * si).astype(BF).astype(F32), (mi * sr - mr * si).astype(BF).astype(F32)))
                for i in range(SLOTS):
                    at = slice(i * TILES, (i + 1) * TILES)
                    second = meta[:, 5 * i : 5 * i + 1] > 0.5
                    pr = jnp.where(second, plain[1][0], plain[0][0])
                    pi = jnp.where(second, plain[1][1], plain[0][1])
                    cy = tilt[at, j : j + 1] + tilt[at, 3 + j : 4 + j]
                    sy = tilt[at, 6 + j : 7 + j] + tilt[at, 9 + j : 10 + j]
                    wx, vx = cx[at, cols], sx[at, cols]
                    pieces[i].append(cy * (pr * wx - pi * vx) - sy * (pr * vx + pi * wx))
        shifted = jnp.concatenate([jnp.concatenate(p, axis=1) for p in pieces], axis=0)
        high = shifted.astype(BF)
        bin_of = lax.shift_right_logical(lax.broadcasted_iota(I32, (WIDE, DFT), 0), 2)
        group = jnp.where(bin_of == lax.broadcasted_iota(I32, (WIDE, DFT), 1), 1.0, 0.0).astype(BF)
        low = (shifted - high.astype(F32)).astype(BF)
        binned = lax.dot_general(high, group, NN, preferred_element_type=F32)
        binned = binned + lax.dot_general(low, group, NN, preferred_element_type=F32)
        binned = binned.astype(BF)[:, :BINS]
        grid = jnp.concatenate([every(got_s, 2 * BLOCKS + r, XROWS).astype(BF) for r in range(2 * BLOCKS)], axis=1)
        values = jnp.concatenate([grid[:, q * BINS : (q + 1) * BINS] for q in range(GRID)], axis=0)
        scores = lax.dot_general(values, binned, NT, preferred_element_type=F32).astype(BF)
        packed = lax.dot_general(scores, place, NN, preferred_element_type=F32)
        lanes = lax.broadcasted_iota(I32, (TILES, LANES), 1)
        extra = jnp.zeros((TILES, LANES), F32)
        for q in range(GRID):
            block = packed[q * TILES : (q + 1) * TILES]
            out_ref[:, q * LANES : (q + 1) * LANES] = block[:, :LANES].astype(BF)
            extra = jnp.where(lanes == q, block[:, LANES : LANES + 1], extra)
        out_ref[:, GRID * LANES :] = extra.astype(BF)

    return pl.pallas_call(
        kernel,
        out_shape=(
            jax.ShapeDtypeStruct((TILES, (GRID + 1) * LANES), BF),
            jax.ShapeDtypeStruct((2, SLOTS * TILES, LANES), F32),
        ),
        in_specs=[VM] * 4,
        out_specs=(VM, VM),
        scratch_shapes=[pltpu.VMEM((TILES * XROWS, LANES), F32)],
        compiler_params=pltpu.CompilerParams(vmem_limit_bytes=VMEM_LIMIT),
        name="score",
    )(got, slices, tabx, taby)


def expand(place, values, tops):
    def kernel(place_ref, value_ref, top_ref, refined_ref, best_ref):
        place = jnp.concatenate([place_ref[0], place_ref[1]], axis=1)
        top = jnp.max(top_ref[...], axis=0, keepdims=True)
        rows = jnp.concatenate([value_ref[...], jnp.broadcast_to(top, (8, top.shape[1]))], axis=0)
        out = lax.dot_general(rows, place, NT, preferred_element_type=F32, precision=lax.Precision.HIGHEST)
        refined_ref[...] = out[:GRID]
        best_ref[...] = out[GRID : GRID + 1]

    return pl.pallas_call(
        kernel,
        out_shape=(
            jax.ShapeDtypeStruct((GRID, SLOTS * TILES), F32),
            jax.ShapeDtypeStruct((1, SLOTS * TILES), F32),
        ),
        in_specs=[VM] * 3,
        out_specs=(VM, VM),
        name="expand",
    )(place, values, tops)


def finish(parts):
    def kernel(*refs):
        ins, (top_ref, mean_ref) = refs[:4], refs[4:]
        for b in range(ROWS):
            cols = slice(b * LANES, (b + 1) * LANES)
            tops = [ref[0, :, cols].astype(F32) for ref in ins]
            sums = [ref[1, :, cols].astype(F32) for ref in ins]
            top = jnp.maximum(jnp.maximum(tops[0], tops[1]), jnp.maximum(tops[2], tops[3]))
            top_ref[pl.ds(b, HALF, stride=ROWS), :] = top
            total = (sums[0] + sums[1]) + (sums[2] + sums[3])
            mean_ref[pl.ds(b, HALF, stride=ROWS), :] = total * (1.0 / ORIENTS)

    shape = jax.ShapeDtypeStruct((ROWS * HALF, LANES), F32)
    return pl.pallas_call(
        kernel,
        out_shape=(shape, shape),
        in_specs=[VM] * 4,
        out_specs=(VM, VM),
        name="finish",
    )(*parts)


def exchange(x, axis, bit):
    size = lax.axis_size(axis)
    return lax.ppermute(x, axis, [(k, k ^ bit) for k in range(size)])


def shards(
    interp_index,
    interp_weight,
    volume,
    spectrum,
    ctf_filter,
    peak_count,
    peak_orient,
    peak_row,
    peak_col,
    ctf_grid,
):
    back, tabx = [jnp.asarray(t) for t in tables()]
    nar = lax.axis_index("nar")
    tile = lax.axis_index("tile")

    taby = lax.dynamic_slice_in_dim(tabx, (nar * TILES + tile) * ROWS, ROWS, 0)
    taby = taby.reshape(ROWS, 4, DFT).transpose(1, 0, 2).reshape(4 * ROWS, DFT)
    taby = jnp.pad(taby, ((0, 16 - 4 * ROWS), (0, 0)))

    fields = jnp.stack(
        [peak_orient, peak_row // BASE, peak_row % BASE, peak_col // BASE, peak_col % BASE], axis=1
    ).reshape(1, -1)
    fields = jnp.concatenate([fields, peak_count.reshape(1, 1)], axis=1).astype(F32)
    fields = jnp.pad(fields, ((0, 0), (0, LANES - 5 * SLOTS - 1)))
    grid = ctf_grid.reshape(GRID, TILES, BINS).transpose(1, 0, 2).reshape(TILES, GRID * BINS)
    spec = spectrum.reshape(2, HALF, DFT)
    filt = ctf_filter.reshape(HALF, DFT)
    got = lax.all_to_all(prepare(spec, grid, fields), "tile", 0, 0, tiled=True)

    blocks, slices = interpolate(
        interp_index.reshape(-1, LANES),
        interp_weight.reshape(-1, LANES),
        volume.reshape(2, -1, LANES).astype(F32),
    )
    mine = lax.all_to_all(blocks, "tile", 0, 0, tiled=True)
    packed, place = score(got, slices, tabx, taby)
    other = exchange(mine, "tile", 1)
    keep, send = correlate(jnp.stack([nar, tile % 2]), mine, other, spec, filt, tabx, back)
    extra_rows = exchange(send, "nar", 1)

    sums = lax.all_to_all(packed, "tile", 0, 0, tiled=True)
    sums = jnp.sum(sums.astype(F32), axis=0)
    sums = lax.psum(sums, "nar") * (1.0 / DFT)
    last = jnp.zeros((GRID, LANES), F32).at[:, 0].set(sums[GRID * LANES : GRID * LANES + GRID])
    values = jnp.concatenate([sums[: GRID * LANES].reshape(GRID, LANES), last], axis=1)
    top = jnp.max(values, axis=0)

    corr = (keep.astype(F32) + extra_rows.astype(F32)) * (1.0 / DFT)
    stats = jnp.stack([jnp.maximum(corr[0], corr[1]), corr[0] + corr[1]]).astype(BF)
    others = [exchange(stats, "rot", bit) for bit in (1, 2, 3)]

    tops = lax.all_to_all(jnp.broadcast_to(top[None], (TILES, 2 * LANES)), "tile", 0, 0, tiled=True)
    refined, best = expand(place, values, tops)

    peak, mean = finish([stats] + others)
    return (
        peak.reshape(1, 1, -1),
        mean.reshape(1, 1, -1),
        refined.T.reshape(1, SLOTS * TILES, GRID),
        best,
    )


def solution(mesh):
    return jax.shard_map(
        shards,
        mesh=mesh,
        in_specs=(
            P(None, "rot", "nar", "tile", None),
            P(None, "rot", "nar", "tile", None),
            P(None, "nar", "tile", None),
            P(None, "tile", "nar", None, None),
            P("tile", "nar", None, None),
            P("rot", "tile"),
            P(("rot", "tile")),
            P(("rot", "tile")),
            P(("rot", "tile")),
            P("tile", "nar", None),
        ),
        out_specs=(
            P("tile", "nar", None),
            P("tile", "nar", None),
            P("rot", None, "tile"),
            P("rot", None),
        ),
        check_vma=False,
    )
```

time: 170 us -> 155 us (0.912)
  blocking collectives: 32.4 us -> 5.36 us
  waiting for transfers between devices: 51.8 us -> 65.6 us
  starting transfers between devices: 43.4 us -> 52.1 us
  local copies, waits for them, and re-layouts: 17.8 us -> 10.9 us
  other arithmetic: 8.02 us -> 4.93 us
    all_to_all x1 -> x0, blocking collectives: 27.1 us -> none  [shards(): lax.all_to_all(jnp.broadcast_to(top[None], (TILES, 2 * LANES)), 'tile', 0...]
    all_to_all x1 -> x3, starting transfers between devices: 18.1 us -> 29.2 us  [the longest x1 18.1 us: shards(): mine = lax.all_to_all(blocks, 'tile', 0, 0, tiled=True)]
    ppermute x5, waiting for transfers between devices: 0.35 us -> 9.68 us  [exchange(): return lax.ppermute(x, axis, [(k, k ^ bit) for k in range(size)])]
    unnamed x19 -> x33, local copies, waits for them, and re-layouts: 10.6 us -> 7.24 us
    all_to_all x1, waiting for transfers between devices: 6.18 us -> 9.14 us  [shards(): sums = lax.all_to_all(packed, 'tile', 0, 0, tiled=True)]
    all_to_all x1, starting transfers between devices: 9.03 us -> 7.11 us  [shards(): sums = lax.all_to_all(packed, 'tile', 0, 0, tiled=True)]
    pallas_call x2 -> x4, Pallas kernels: 6.28 us -> 8.02 us  [the longest x1 2.73 us: interpolate(): pl.pallas_call(kernel, out_shape=(jax.ShapeDtypeStruct((TILES, SROWS, LAN...]
    all_to_all x1 -> x3, waiting for transfers between devices: 45.2 us -> 46.8 us  [the longest x1 22.8 us: shards(): mine = lax.all_to_all(blocks, 'tile', 0, 0, tiled=True)]
  transfers between devices with their start and end apart: 7 -> 9, of which waited for: 3 -> 6; matrix products, arithmetic and copies ran while one was open for 3% -> 4% of each run, Pallas kernels for 4% -> 4%
where the time goes in v2:
time: 155 us
  waiting for transfers between devices  65.6 us (42%)
  starting transfers between devices  52.1 us (34%)
  Pallas kernels  14 us (9%)
  local copies, waits for them, and re-layouts  10.9 us (7%)
  blocking collectives  5.36 us (3%)
  other arithmetic  4.93 us (3%)
  between operations  1.68 us (1%)
    all_to_all x1, waiting for transfers between devices, shards(): mine = lax.all_to_all(blocks, 'tile', 0, 0, tiled=True)  22.8 us
    all_to_all x1, starting transfers between devices, shards(): mine = lax.all_to_all(blocks, 'tile', 0, 0, tiled=True)  18.1 us
    ppermute x5, starting transfers between devices, exchange(): return lax.ppermute(x, axis, [(k, k ^ bit) for k in range(size)])  15.8 us
    all_to_all x1, waiting for transfers between devices, shards(): got = lax.all_to_all(prepare(spec, grid, fields), 'tile', 0, 0, tiled=True)  13.1 us
    all_to_all x1, waiting for transfers between devices, shards(): lax.all_to_all(jnp.broadcast_to(top[None], (TILES, 2 * LANES)), 'tile', 0...  10.9 us
    ppermute x5, waiting for transfers between devices, exchange(): return lax.ppermute(x, axis, [(k, k ^ bit) for k in range(size)])  9.68 us
    all_to_all x1, waiting for transfers between devices, shards(): sums = lax.all_to_all(packed, 'tile', 0, 0, tiled=True)  9.14 us
    unnamed x33, local copies, waits for them, and re-layouts  7.24 us
  transfers between devices with their start and end apart: 9, of which 6 were waited for; matrix products, arithmetic and copies ran while one was open for 4% of the time, Pallas kernels for 4%

profile of v2, /device:TPU:1, one launch (start us, length us, event | category | flops | bytes accessed | tf_op | source)
XLA Modules:
  0.0 154.6 jit_solution(11924359283705807213)
XLA Ops:
  0.6 0.0 copy-start.12
  0.6 0.0 copy-start.11
  0.7 0.0 copy-start.13
  0.7 0.7 convert_bitcast_fusion
  1.4 0.8 copy.24
  2.3 0.0 copy-start.6
  2.3 0.9 copy-done.6
  3.1 2.7 %interpolate.1 = (bf16[64,24,128]{2,1,0:T(8,128)(2,1)}, f32[2,18,128]{2,1,0:T(8,128)S(1)}) custom-call(s32[144,128]{1,0:T(8,128)S(1)} %bitcast.49, bf16[144,128]{1,0:T(8,128)(2,1)S(1)} %reshape.124.weight_ref, f32[2,32,128]{2,1,0:T(8,128)S(1)} %bitcast.48), custom_call_target="tpu_custom_call" | custom-call | tf_op jit(solution)/shard_map/interpolate/pallas_call | solution.py:134
  5.9 18.1 %all-to-all-start = ((bf16[64,24,128]{2,1,0:T(8,128)(2,1)}), bf16[64,24,128]{2,1,0:T(8,128)(2,1)S(1)}, u32[]{:S(2)}, u32[]{:S(2)}) async-start(bf16[64,24,128]{2,1,0:T(8,128)(2,1)} %get-tuple-element.26), calls=%async_computation | async-start | bytes 786432 | tf_op jit(solution)/shard_map/all_to_all | solution.py:379
  24.0 0.0 copy-start.1
  24.7 0.0 copy-done.12
  24.7 0.0 copy-done.11
  24.7 0.0 copy-done.13
  24.7 0.1 copy.26
  24.8 0.1 concatenate.18
  24.9 1.6 %reshape.129 = bf16[8,64,288]{2,1,0:T(8,128)(2,1)S(1)} reshape(bf16[8,1,18432]{2,0,1:T(8,128)(2,1)} %param.23) | data formatting | bytes 589824 | tf_op jit(solution)/shard_map/reshape | solution.py:369
  26.5 0.2 copy.34
  26.8 0.3 reshape.130.grid_ref
  27.1 0.1 add_convert_fusion.1
  27.2 0.0 copy-start.2
  27.2 1.2 prepare.1
  28.4 22.8 %all-to-all-done.own_ref = bf16[64,24,128]{2,1,0:T(8,128)(2,1)S(1)} async-done(((bf16[64,24,128]{2,1,0:T(8,128)(2,1)}), bf16[64,24,128]{2,1,0:T(8,128)(2,1)S(1)}, u32[]{:S(2)}, u32[]{:S(2)}) %all-to-all-start) | async-done | bytes 393248 | tf_op jit(solution)/shard_map/all_to_all | solution.py:379
  51.2 4.7 %all-to-all-start.1 = ((bf16[64,40,128]{2,1,0:T(8,128)(2,1)}), bf16[64,40,128]{2,1,0:T(8,128)(2,1)S(1)}, u32[]{:S(2)}, u32[]{:S(2)}) async-start(bf16[64,40,128]{2,1,0:T(8,128)(2,1)} %prepare.1), calls=%async_computation.1 | async-start | bytes 1310720 | tf_op jit(solution)/shard_map/all_to_all | solution.py:372
  55.9 2.4 %collective-permute-start = (bf16[64,24,128]{2,1,0:T(8,128)(2,1)S(1)}, bf16[64,24,128]{2,1,0:T(8,128)(2,1)S(1)}, u32[]{:S(2)}, u32[]{:S(2)}) collective-permute-start(bf16[64,24,128]{2,1,0:T(8,128)(2,1)S(1)} %all-to-all-done.own_ref), channel_id=1, source_target_pairs={{0,2},{2,0},{4,6},{6,4},{8,10},{10,8},{12,14},{14,12},{16,18},{18,... | collective-permute-start | bytes 1179656 | tf_op jit(solution)/shard_map/ppermute | solution.py:341
  58.3 0.1 pad_add_fusion.at_ref
  58.4 1.2 collective-permute-done.other_ref
  59.6 0.0 copy-done.2
  59.6 0.9 copy-done.5
  60.5 3.0 %correlate.1 = (bf16[2,192,384]{2,1,0:T(8,128)(2,1)S(1)}, bf16[2,192,384]{2,1,0:T(8,128)(2,1)}) custom-call(s32[2]{0:T(128)S(1)} %pad_add_fusion.at_ref, bf16[64,24,128]{2,1,0:T(8,128)(2,1)S(1)} %all-to-all-done.own_ref, bf16[64,24,128]{2,1,0:T(8,128)(2,1)S(1)} %collective-permute-done.other_ref, bf16[2,192,384]{2,1,0:T(8,128)(2,1)S(1)} %bitcast.45, ...), custom_call_target="tpu_custom_call" | custom-call | tf_op jit(solution)/shard_map/correlate/pallas_call | solution.py:198
  63.5 0.7 copy-done.3
  64.3 4.3 %collective-permute-start.1 = (bf16[2,192,384]{2,1,0:T(8,128)(2,1)}, bf16[2,192,384]{2,1,0:T(8,128)(2,1)S(1)}, u32[]{:S(2)}, u32[]{:S(2)}) collective-permute-start(bf16[2,192,384]{2,1,0:T(8,128)(2,1)} %get-tuple-element.28), channel_id=1, source_target_pairs={{0,1},{1,0},{2,3},{3,2},{4,5},{5,4},{6,7},{7,6},{8,9},{9,8},{10,11... | collective-permute-start | bytes 884744 | tf_op jit(solution)/shard_map/ppermute | solution.py:341
  68.7 0.6 compare_reduce_fusion
  69.3 8.4 %collective-permute-done.1 = bf16[2,192,384]{2,1,0:T(8,128)(2,1)S(1)} collective-permute-done((bf16[2,192,384]{2,1,0:T(8,128)(2,1)}, bf16[2,192,384]{2,1,0:T(8,128)(2,1)S(1)}, u32[]{:S(2)}, u32[]{:S(2)}) %collective-permute-start.1) | collective-permute-done | bytes 294944 | tf_op jit(solution)/shard_map/ppermute | solution.py:341
  77.8 1.0 add_multiply_fusion
  78.8 13.1 %all-to-all-done.1.got_ref = bf16[64,40,128]{2,1,0:T(8,128)(2,1)S(1)} async-done(((bf16[64,40,128]{2,1,0:T(8,128)(2,1)}), bf16[64,40,128]{2,1,0:T(8,128)(2,1)S(1)}, u32[]{:S(2)}, u32[]{:S(2)}) %all-to-all-start.1) | async-done | bytes 655392 | tf_op jit(solution)/shard_map/all_to_all | solution.py:372
  91.9 3.0 %score.1 = (bf16[64,1152]{1,0:T(8,128)(2,1)S(1)}, f32[2,256,128]{2,1,0:T(8,128)S(1)}) custom-call(bf16[64,40,128]{2,1,0:T(8,128)(2,1)S(1)} %all-to-all-done.1.got_ref, f32[2,18,128]{2,1,0:T(8,128)S(1)} %get-tuple-element.31.slice_ref, bf16[384,1536]{1,0:T(8,128)(2,1)S(1)} %copy-done, bf16[16,384]{1,0:T(8,128)(2,1)S(1)} %pad.12.taby_ref), custom_call_target="tpu_custom_call" | custom-call | tf_op jit(solution)/shard_map/score/pallas_call | solution.py:282
  94.9 0.7 copy-done.4
  95.6 0.5 broadcast.105
  96.1 0.7 reduce.9
  96.8 0.9 reshape.136
  97.7 7.1 %all-to-all-start.2 = ((bf16[64,2,576]{2,1,0:T(2,128)(2,1)}), bf16[64,2,576]{2,1,0:T(2,128)(2,1)S(1)}, u32[]{:S(2)}, u32[]{:S(2)}) async-start(bf16[64,2,576]{2,1,0:T(2,128)(2,1)} %reshape.136), calls=%async_computation.2 | async-start | bytes 327680 | tf_op jit(solution)/shard_map/all_to_all | solution.py:385
  104.9 4.6 %collective-permute-start.4 = (bf16[2,192,384]{2,1,0:T(8,128)(2,1)S(1)}, bf16[2,192,384]{2,1,0:T(8,128)(2,1)S(1)}, u32[]{:S(2)}, u32[]{:S(2)}) collective-permute-start(bf16[2,192,384]{2,1,0:T(8,128)(2,1)S(1)} %pad_maximum_fusion.refs_0_), channel_id=1, source_target_pairs={{0,384},{128,256},{256,128},{384,0},{1,385},{129,257},{257,129},{3... | collective-permute-start | bytes 884744 | tf_op jit(solution)/shard_map/ppermute | solution.py:341
  109.6 2.3 %collective-permute-start.3 = (bf16[2,192,384]{2,1,0:T(8,128)(2,1)S(1)}, bf16[2,192,384]{2,1,0:T(8,128)(2,1)S(1)}, u32[]{:S(2)}, u32[]{:S(2)}) collective-permute-start(bf16[2,192,384]{2,1,0:T(8,128)(2,1)S(1)} %pad_maximum_fusion.refs_0_), channel_id=1, source_target_pairs={{0,256},{128,384},{256,0},{384,128},{1,257},{129,385},{257,1},{385... | collective-permute-start | bytes 884744 | tf_op jit(solution)/shard_map/ppermute | solution.py:341
  111.8 2.1 %collective-permute-start.2 = (bf16[2,192,384]{2,1,0:T(8,128)(2,1)S(1)}, bf16[2,192,384]{2,1,0:T(8,128)(2,1)S(1)}, u32[]{:S(2)}, u32[]{:S(2)}) collective-permute-start(bf16[2,192,384]{2,1,0:T(8,128)(2,1)S(1)} %pad_maximum_fusion.refs_0_), channel_id=1, source_target_pairs={{0,128},{128,0},{256,384},{384,256},{1,129},{129,1},{257,385},{385... | collective-permute-start | bytes 884744 | tf_op jit(solution)/shard_map/ppermute | solution.py:341
  114.0 9.1 %all-to-all-done.2 = bf16[64,2,576]{2,1,0:T(2,128)(2,1)S(1)} async-done(((bf16[64,2,576]{2,1,0:T(2,128)(2,1)}), bf16[64,2,576]{2,1,0:T(2,128)(2,1)S(1)}, u32[]{:S(2)}, u32[]{:S(2)}) %all-to-all-start.2) | async-done | bytes 147488 | tf_op jit(solution)/shard_map/all_to_all | solution.py:385
  123.1 0.2 reshape.137
  123.4 0.3 convert_reduce_fusion
  123.6 5.4 %psum.7 = f32[1152]{0:T(1024)S(1)} all-reduce(f32[1152]{0:T(1024)S(1)} %convert_reduce_fusion), channel_id=1, replica_groups=mesh['rot'=4,'tile'=64,'nar'=2] {'nar'}, use_global_device_ids=true, to_apply=%region_1.2 | all-reduce | flops 1152 | bytes 9216 | tf_op jit(solution)/shard_map/psum | solution.py:387
  129.0 0.7 fusion
  129.7 0.1 copy.28
  129.8 0.6 fusion.5
  130.4 0.7 broadcast_in_dim.2
  131.0 6.5 %all-to-all-start.3 = ((f32[64,1,256]{2,1,0:T(1,128)}), f32[64,1,256]{2,1,0:T(1,128)S(1)}, u32[]{:S(2)}, u32[]{:S(2)}) async-start(f32[64,1,256]{2,1,0:T(1,128)} %broadcast_in_dim.2), calls=%async_computation.3 | async-start | bytes 131072 | tf_op jit(solution)/shard_map/all_to_all | solution.py:396
  137.5 0.0 collective-permute-done.4.refs_3_
  137.5 0.0 collective-permute-done.3.refs_2_
  137.5 0.0 copy-start.9
  137.5 0.0 collective-permute-done.2.refs_1_
  137.5 0.7 copy-done.8
  138.2 0.1 copy-done.9
  138.3 0.7 copy-done.10
  139.0 2.2 %finish.1 = (f32[576,128]{1,0:T(8,128)}, f32[576,128]{1,0:T(8,128)}) custom-call(bf16[2,192,384]{2,1,0:T(8,128)(2,1)} %copy-done.7, bf16[2,192,384]{2,1,0:T(8,128)(2,1)} %copy-done.10, bf16[2,192,384]{2,1,0:T(8,128)(2,1)} %copy-done.9, bf16[2,192,384]{2,1,0:T(8,128)(2,1)} %copy-done.8), custom_call_target="tpu_custom_call" | custom-call | tf_op jit(solution)/shard_map/finish/pallas_call | solution.py:330
  141.2 10.9 %all-to-all-done.3 = f32[64,1,256]{2,1,0:T(1,128)S(1)} async-done(((f32[64,1,256]{2,1,0:T(1,128)}), f32[64,1,256]{2,1,0:T(1,128)S(1)}, u32[]{:S(2)}, u32[]{:S(2)}) %all-to-all-start.3) | async-done | bytes 65568 | tf_op jit(solution)/shard_map/all_to_all | solution.py:396
  152.1 0.6 copy.35
  152.7 1.9 %expand.1 = (f32[8,256]{1,0:T(8,128)}, f32[1,256]{1,0:T(1,128)}) custom-call(f32[2,256,128]{2,1,0:T(8,128)} %copy-done.4, f32[8,256]{1,0:T(8,128)} %get-tuple-element.37.value_ref, f32[64,256]{1,0:T(8,128)} %bitcast.51), custom_call_target="tpu_custom_call" | custom-call | tf_op jit(solution)/shard_map/expand/pallas_call | solution.py:305
  (23 shorter events, 0.3 us)
Async XLA Ops:
  0.6 24.0 %copy-start.12 = (s32[4]{0:T(128)S(1)}, s32[4]{0:T(128)}, u32[]{:S(2)}) copy-start(s32[4]{0:T(128)} %param.22) | copy-start | bytes 52
  0.6 24.0 %copy-start.11 = (s32[4]{0:T(128)S(1)}, s32[4]{0:T(128)}, u32[]{:S(2)}) copy-start(s32[4]{0:T(128)} %param.21) | copy-start | bytes 52
  0.7 24.1 %copy-start.13 = (s32[4]{0:T(128)S(1)}, s32[4]{0:T(128)}, u32[]{:S(2)}) copy-start(s32[4]{0:T(128)} %param.20) | copy-start | bytes 52
  2.3 0.9 copy-start.6
  5.9 45.3 %all-to-all-start = ((bf16[64,24,128]{2,1,0:T(8,128)(2,1)}), bf16[64,24,128]{2,1,0:T(8,128)(2,1)S(1)}, u32[]{:S(2)}, u32[]{:S(2)}) async-start(bf16[64,24,128]{2,1,0:T(8,128)(2,1)} %get-tuple-element.26), calls=%async_computation | async-start | bytes 786432 | tf_op jit(solution)/shard_map/all_to_all | solution.py:379
  24.0 3.2 %copy-start.1 = (bf16[2,1,1,192,384]{4,3,2,1,0:T(8,128)(2,1)S(1)}, bf16[2,1,1,192,384]{4,3,2,1,0:T(8,128)(2,1)}, u32[]{:S(2)}) copy-start(bf16[2,1,1,192,384]{4,3,2,1,0:T(8,128)(2,1)} %param.17) | copy-start | bytes 884740
  27.2 32.4 %copy-start = (bf16[384,1536]{1,0:T(8,128)(2,1)S(1)}, bf16[384,1536]{1,0:T(8,128)(2,1)}, u32[]{:S(2)}) copy-start(bf16[384,1536]{1,0:T(8,128)(2,1)} %constant.110.clone.tabx_ref) | copy-start | bytes 3538948
  27.2 32.4 %copy-start.2 = (bf16[2,384,384]{2,1,0:T(8,128)(2,1)S(1)}, bf16[2,384,384]{2,1,0:T(8,128)(2,1)}, u32[]{:S(2)}) copy-start(bf16[2,384,384]{2,1,0:T(8,128)(2,1)} %constant.109.clone.back_ref) | copy-start | bytes 1769476
  51.2 40.7 %all-to-all-start.1 = ((bf16[64,40,128]{2,1,0:T(8,128)(2,1)}), bf16[64,40,128]{2,1,0:T(8,128)(2,1)S(1)}, u32[]{:S(2)}, u32[]{:S(2)}) async-start(bf16[64,40,128]{2,1,0:T(8,128)(2,1)} %prepare.1), calls=%async_computation.1 | async-start | bytes 1310720 | tf_op jit(solution)/shard_map/all_to_all | solution.py:372
  55.9 3.7 %collective-permute-start = (bf16[64,24,128]{2,1,0:T(8,128)(2,1)S(1)}, bf16[64,24,128]{2,1,0:T(8,128)(2,1)S(1)}, u32[]{:S(2)}, u32[]{:S(2)}) collective-permute-start(bf16[64,24,128]{2,1,0:T(8,128)(2,1)S(1)} %all-to-all-done.own_ref), channel_id=1, source_target_pairs={{0,2},{2,0},{4,6},{6,4},{8,10},{10,8},{12,14},{14,12},{16,18},{18,... | collective-permute-start | bytes 1179656 | tf_op jit(solution)/shard_map/ppermute | solution.py:341
  59.6 0.9 copy-start.5
  63.5 0.7 copy-start.3
  64.3 13.5 %collective-permute-start.1 = (bf16[2,192,384]{2,1,0:T(8,128)(2,1)}, bf16[2,192,384]{2,1,0:T(8,128)(2,1)S(1)}, u32[]{:S(2)}, u32[]{:S(2)}) collective-permute-start(bf16[2,192,384]{2,1,0:T(8,128)(2,1)} %get-tuple-element.28), channel_id=1, source_target_pairs={{0,1},{1,0},{2,3},{3,2},{4,5},{5,4},{6,7},{7,6},{8,9},{9,8},{10,11... | collective-permute-start | bytes 884744 | tf_op jit(solution)/shard_map/ppermute | solution.py:341
  94.9 0.7 copy-start.4
  97.7 25.5 %all-to-all-start.2 = ((bf16[64,2,576]{2,1,0:T(2,128)(2,1)}), bf16[64,2,576]{2,1,0:T(2,128)(2,1)S(1)}, u32[]{:S(2)}, u32[]{:S(2)}) async-start(bf16[64,2,576]{2,1,0:T(2,128)(2,1)} %reshape.136), calls=%async_computation.2 | async-start | bytes 327680 | tf_op jit(solution)/shard_map/all_to_all | solution.py:385
  104.9 32.6 %copy-start.7 = (bf16[2,192,384]{2,1,0:T(8,128)(2,1)}, bf16[2,192,384]{2,1,0:T(8,128)(2,1)S(1)}, u32[]{:S(2)}) copy-start(bf16[2,192,384]{2,1,0:T(8,128)(2,1)S(1)} %pad_maximum_fusion.refs_0_) | copy-start | bytes 884740
  104.9 32.6 %collective-permute-start.4 = (bf16[2,192,384]{2,1,0:T(8,128)(2,1)S(1)}, bf16[2,192,384]{2,1,0:T(8,128)(2,1)S(1)}, u32[]{:S(2)}, u32[]{:S(2)}) collective-permute-start(bf16[2,192,384]{2,1,0:T(8,128)(2,1)S(1)} %pad_maximum_fusion.refs_0_), channel_id=1, source_target_pairs={{0,384},{128,256},{256,128},{384,0},{1,385},{129,257},{257,129},{3... | collective-permute-start | bytes 884744 | tf_op jit(solution)/shard_map/ppermute | solution.py:341
  109.6 28.0 %collective-permute-start.3 = (bf16[2,192,384]{2,1,0:T(8,128)(2,1)S(1)}, bf16[2,192,384]{2,1,0:T(8,128)(2,1)S(1)}, u32[]{:S(2)}, u32[]{:S(2)}) collective-permute-start(bf16[2,192,384]{2,1,0:T(8,128)(2,1)S(1)} %pad_maximum_fusion.refs_0_), channel_id=1, source_target_pairs={{0,256},{128,384},{256,0},{384,128},{1,257},{129,385},{257,1},{385... | collective-permute-start | bytes 884744 | tf_op jit(solution)/shard_map/ppermute | solution.py:341
  111.8 25.7 %collective-permute-start.2 = (bf16[2,192,384]{2,1,0:T(8,128)(2,1)S(1)}, bf16[2,192,384]{2,1,0:T(8,128)(2,1)S(1)}, u32[]{:S(2)}, u32[]{:S(2)}) collective-permute-start(bf16[2,192,384]{2,1,0:T(8,128)(2,1)S(1)} %pad_maximum_fusion.refs_0_), channel_id=1, source_target_pairs={{0,128},{128,0},{256,384},{384,256},{1,129},{129,1},{257,385},{385... | collective-permute-start | bytes 884744 | tf_op jit(solution)/shard_map/ppermute | solution.py:341
  131.0 21.1 %all-to-all-start.3 = ((f32[64,1,256]{2,1,0:T(1,128)}), f32[64,1,256]{2,1,0:T(1,128)S(1)}, u32[]{:S(2)}, u32[]{:S(2)}) async-start(f32[64,1,256]{2,1,0:T(1,128)} %broadcast_in_dim.2), calls=%async_computation.3 | async-start | bytes 131072 | tf_op jit(solution)/shard_map/all_to_all | solution.py:396
  137.5 0.7 copy-start.8
  137.5 0.8 copy-start.9
  138.3 0.7 copy-start.10

commit v3 on v2

--- a/solution.py
+++ b/solution.py
@@ -22,7 +22,11 @@
 BLOCKS = 9
 XROWS = 40
 SROWS = 24
+SHARE = 16
+SPAN = 5
 ORIENTS = 8
+REST = SHARE + 2 * BLOCKS
+META = REST + 4 * BLOCKS - 2 * SHARE
 VMEM_LIMIT = 48 * 1024 * 1024
 
 VM = pl.BlockSpec(memory_space=pltpu.VMEM)
@@ -59,99 +63,101 @@
     return ref[pl.ds(row, TILES, stride=step), :]
 
 
-def prepare(spectrum, grid, meta):
-    def kernel(spec_ref, grid_ref, meta_ref, out_ref, spec_s, out_s):
+def prepare(rot, index, weight, table, spectrum, grid, orient, row, col, count):
+    def kernel(
+        rot_ref, index_ref, weight_ref, table_ref, spec_ref, grid_ref, orient_ref, row_ref, col_ref, count_ref,
+        out_ref, own_ref, table_s, weight_s, value_s, spec_s, all_s, out_s,
+    ):
+        table_s[...] = table_ref[...].astype(F32)
+        for k in range(8):
+            for o in range(2):
+                w = weight_ref[k, o].astype(F32)
+                for b in range(ROWS):
+                    at = pl.ds(k * 2 * BLOCKS + o * BLOCKS + b, ROWS, stride=ROWS)
+                    weight_s[at, :] = w[:, b * LANES : (b + 1) * LANES]
+
+        def step(v, carry):
+            rows = pl.ds(pl.multiple_of(v * 8, 8), 8)
+            entry = index_ref[rows, :]
+            low = entry & (LANES - 1)
+            high = lax.shift_right_logical(entry, 7)
+            bits = [(lax.shift_right_logical(high, b) & 1) == 1 for b in range(5)]
+
+            def pick(c, level, first):
+                if level < 0:
+                    line = table_s[c : c + 1, first * LANES : (first + 1) * LANES]
+                    return jnp.take_along_axis(jnp.broadcast_to(line, (8, LANES)), low, axis=1)
+                return jnp.where(
+                    bits[level],
+                    pick(c, level - 1, first + (1 << level)),
+                    pick(c, level - 1, first),
+                )
+
+            for c in range(2):
+                value_s[c, rows, :] = pick(c, 4, 0) * weight_s[rows, :]
+            return carry
+
+        lax.fori_loop(0, 2 * BLOCKS, step, 0)
+        for c in range(2):
+            total = value_s[c, 0 : 2 * BLOCKS, :]
+            for k in range(1, 8):
+                total = total + value_s[c, k * 2 * BLOCKS : (k + 1) * 2 * BLOCKS, :]
+            own_ref[c] = total.astype(BF).astype(F32)
+
+        odd = (lax.broadcasted_iota(I32, (TILES, LANES), 0) & 1) == 1
+        for r in range(2 * BLOCKS):
+            row = jnp.where(odd, own_ref[1, r : r + 1, :], own_ref[0, r : r + 1, :])
+            out_s[pl.ds(SHARE + r, TILES, stride=XROWS), :] = row
         for c in range(2):
             for b in range(ROWS):
                 spec_s[c * ROWS + b] = spec_ref[c, :, b * LANES : (b + 1) * LANES].astype(F32)
         for c in range(2):
             for j in range(ROWS):
                 for b in range(ROWS):
-                    row = c * BLOCKS + j * ROWS + b
-                    out_s[pl.ds(row, TILES, stride=XROWS), :] = spec_s[c * ROWS + b, pl.ds(j, TILES, stride=ROWS), :]
+                    all_s[c * BLOCKS + j * ROWS + b] = spec_s[c * ROWS + b, pl.ds(j, TILES, stride=ROWS), :]
         for r in range(2 * BLOCKS):
-            block = grid_ref[:, r * LANES : (r + 1) * LANES].astype(F32)
-            out_s[pl.ds(2 * BLOCKS + r, TILES, stride=XROWS), :] = block
-        fields = jnp.broadcast_to(meta_ref[...], (TILES, LANES))
-        for r in range(4 * BLOCKS, XROWS):
+            all_s[2 * BLOCKS + r] = grid_ref[:, r * LANES : (r + 1) * LANES].astype(F32)
+        for r in range(SHARE):
+            out_s[pl.ds(r, TILES, stride=XROWS), :] = all_s[(rot_ref[0] & 1) * SHARE + r]
+        for r in range(META - REST):
+            out_s[pl.ds(REST + r, TILES, stride=XROWS), :] = all_s[2 * SHARE + r]
+        lane = lax.broadcasted_iota(I32, (1, LANES), 1)
+        fields = jnp.where(lane == 5 * SLOTS, count_ref[0, 0], 0)
+        for i in range(SLOTS):
+            y, x = row_ref[i], col_ref[i]
+            items = (orient_ref[i], y >> 4, y & (BASE - 1), x >> 4, x & (BASE - 1))
+            for k, item in enumerate(items):
+                fields = jnp.where(lane == 5 * i + k, item, fields)
+        fields = jnp.broadcast_to(fields.astype(F32), (TILES, LANES))
+        for r in range(META, XROWS):
             out_s[pl.ds(r, TILES, stride=XROWS), :] = fields
         out_ref[...] = out_s[...].astype(BF).reshape(out_ref.shape)
 
     return pl.pallas_call(
         kernel,
-        out_shape=jax.ShapeDtypeStruct((TILES, XROWS, LANES), BF),
-        in_specs=[VM] * 3,
-        out_specs=VM,
+        out_shape=(
+            jax.ShapeDtypeStruct((TILES, XROWS, LANES), BF),
+            jax.ShapeDtypeStruct((2, 2 * BLOCKS, LANES), F32),
+        ),
+        in_specs=[SM] + [VM] * 5 + [SM] * 4,
+        out_specs=(VM, VM),
         scratch_shapes=[
+            pltpu.VMEM(table.shape, F32),
+            pltpu.VMEM(index.shape, F32),
+            pltpu.VMEM((2,) + index.shape, F32),
             pltpu.VMEM((2 * ROWS, HALF, LANES), F32),
+            pltpu.VMEM((4 * BLOCKS, TILES, LANES), F32),
             pltpu.VMEM((TILES * XROWS, LANES), F32),
         ],
         compiler_params=pltpu.CompilerParams(vmem_limit_bytes=VMEM_LIMIT),
         name="prepare",
-    )(spectrum, grid, meta)
-
-
-def interpolate(index, weight, table):
-    steps = index.shape[0] // 16
-    kept = index.shape[0] // 8
-
-    def kernel(index_ref, weight_ref, table_ref, out_ref, own_ref, value_ref):
-        def step(v, carry):
-            pair = pl.ds(pl.multiple_of(v * 16, 16), 16)
-            weights = weight_ref[pair, :].astype(F32)
-            for s in range(2):
-                rows = pl.ds(pl.multiple_of(v * 16 + s * 8, 8), 8)
-                entry = index_ref[rows, :]
-                low = entry & (LANES - 1)
-                high = lax.shift_right_logical(entry, 7)
-                bits = [(lax.shift_right_logical(high, b) & 1) == 1 for b in range(5)]
-
-                def pick(c, level, first):
-                    if level < 0:
-                        row = jnp.broadcast_to(table_ref[c, first : first + 1, :], (8, LANES))
-                        return jnp.take_along_axis(row, low, axis=1)
-                    return jnp.where(
-                        bits[level],
-                        pick(c, level - 1, first + (1 << level)),
-                        pick(c, level - 1, first),
-                    )
-
-                for c in range(2):
-                    value_ref[c, rows, :] = pick(c, 4, 0) * weights[s * 8 : (s + 1) * 8]
-            return carry
-
-        lax.fori_loop(0, steps, step, 0)
-        for c in range(2):
-            total = value_ref[c, 0:kept, :]
-            for k in range(1, 8):
-                total = total + value_ref[c, k * kept : (k + 1) * kept, :]
-            rounded = total.astype(BF)
-            own_ref[c] = rounded.astype(F32)
-            block = jnp.concatenate([rounded.astype(F32), jnp.zeros((SROWS - kept, LANES), F32)], axis=0).astype(BF)
-            for t in range(c, TILES, 2):
-                out_ref[t] = block
-
-    return pl.pallas_call(
-        kernel,
-        out_shape=(
-            jax.ShapeDtypeStruct((TILES, SROWS, LANES), BF),
-            jax.ShapeDtypeStruct((2, kept, LANES), F32),
-        ),
-        in_specs=[VM] * 3,
-        out_specs=(VM, VM),
-        scratch_shapes=[pltpu.VMEM((2, index.shape[0], LANES), F32)],
-        compiler_params=pltpu.CompilerParams(vmem_limit_bytes=VMEM_LIMIT),
-        name="interpolate",
-    )(index, weight, table)
+    )(rot, index, weight, table, spectrum, grid, orient, row, col, count)
 
 
 def correlate(place, own, other, spectrum, filt, tabx, back):
     def kernel(at_ref, own_ref, other_ref, spec_ref, filt_ref, tabx_ref, back_ref, keep_ref, send_ref, sl_s, spec_s):
-        first = at_ref[1] == 0
-        mine = own_ref[...].astype(F32).reshape(TILES * SROWS, LANES)
-        theirs = other_ref[...].astype(F32).reshape(TILES * SROWS, LANES)
-        sl_s[0] = jnp.where(first, mine, theirs)
-        sl_s[1] = jnp.where(first, theirs, mine)
+        sl_s[at_ref[1]] = own_ref[...].astype(F32).reshape(TILES * SROWS, LANES)
+        sl_s[1 - at_ref[1]] = other_ref[...].astype(F32).reshape(TILES * SROWS, LANES)
         for c in range(2):
             for b in range(ROWS):
                 spec_s[c * ROWS + b] = spec_ref[c, :, b * LANES : (b + 1) * LANES].astype(F32)
@@ -209,10 +215,23 @@
     )(place, own, other, spectrum, filt, tabx, back)
 
 
-def score(got, slices, tabx, taby):
-    def kernel(got_ref, slice_ref, tabx_ref, taby_ref, out_ref, place_ref, got_s):
+def score(rot, got, share, slices, tabx, taby):
+    def kernel(
+        rot_ref, got_ref, share_ref, slice_ref, tabx_ref, taby_ref,
+        out_ref, place_ref, got_s, share_s, out_s,
+    ):
         got_s[...] = got_ref[...].astype(F32).reshape(got_s.shape)
-        meta = every(got_s, 4 * BLOCKS, XROWS)
+        side = rot_ref[0] & 1
+        share_s[1 - side] = share_ref[...].astype(F32).reshape(TILES * SHARE, LANES)
+        for r in range(SHARE):
+            share_s[side, pl.ds(r, TILES, stride=SHARE), :] = every(got_s, r, XROWS)
+
+        def sent(row):
+            if row < 2 * SHARE:
+                return every(share_s.at[row // SHARE], row % SHARE, SHARE)
+            return every(got_s, REST + row - 2 * SHARE, XROWS)
+
+        meta = every(got_s, META, XROWS)
         lane = lax.broadcasted_iota(I32, (TILES, DFT), 1).astype(F32)
         count = meta[:, 20:21]
         tri_r = lax.broadcasted_iota(I32, (TILES, TILES), 0)
@@ -243,8 +262,8 @@
             for b in range(ROWS):
                 r = j * ROWS + b
                 cols = slice(b * LANES, (b + 1) * LANES)
-                mr = every(got_s, r, XROWS)
-                mi = every(got_s, BLOCKS + r, XROWS)
+                mr = sent(r)
+                mi = sent(BLOCKS + r)
                 plain = []
                 for o in range(2):
                     sr = slice_ref[0, o * BLOCKS + r : o * BLOCKS + r + 1, :]
@@ -267,7 +286,7 @@
         binned = lax.dot_general(high, group, NN, preferred_element_type=F32)
         binned = binned + lax.dot_general(low, group, NN, preferred_element_type=F32)
         binned = binned.astype(BF)[:, :BINS]
-        grid = jnp.concatenate([every(got_s, 2 * BLOCKS + r, XROWS).astype(BF) for r in range(2 * BLOCKS)], axis=1)
+        grid = jnp.concatenate([sent(2 * BLOCKS + r).astype(BF) for r in range(2 * BLOCKS)], axis=1)
         values = jnp.concatenate([grid[:, q * BINS : (q + 1) * BINS] for q in range(GRID)], axis=0)
         scores = lax.dot_general(values, binned, NT, preferred_element_type=F32).astype(BF)
         packed = lax.dot_general(scores, place, NN, preferred_element_type=F32)
@@ -275,43 +294,70 @@
         extra = jnp.zeros((TILES, LANES), F32)
         for q in range(GRID):
             block = packed[q * TILES : (q + 1) * TILES]
-            out_ref[:, q * LANES : (q + 1) * LANES] = block[:, :LANES].astype(BF)
+            out_s[:, q // SPAN, q % SPAN * LANES : (q % SPAN + 1) * LANES] = block[:, :LANES]
             extra = jnp.where(lanes == q, block[:, LANES : LANES + 1], extra)
-        out_ref[:, GRID * LANES :] = extra.astype(BF)
+        out_s[:, 1, (SPAN - 2) * LANES : (SPAN - 1) * LANES] = extra
+        out_s[:, 1, (SPAN - 1) * LANES :] = jnp.zeros((TILES, LANES), F32)
+        out_ref[...] = out_s[...].astype(BF)
 
     return pl.pallas_call(
         kernel,
         out_shape=(
-            jax.ShapeDtypeStruct((TILES, (GRID + 1) * LANES), BF),
+            jax.ShapeDtypeStruct((TILES, 2, SPAN * LANES), BF),
             jax.ShapeDtypeStruct((2, SLOTS * TILES, LANES), F32),
         ),
-        in_specs=[VM] * 4,
-        out_specs=(VM, VM),
-        scratch_shapes=[pltpu.VMEM((TILES * XROWS, LANES), F32)],
+        in_specs=[SM] + [VM] * 5,
+        out_specs=(VM, VM),
+        scratch_shapes=[pltpu.VMEM((TILES * XROWS, LANES), F32), pltpu.VMEM((2, TILES * SHARE, LANES), F32), pltpu.VMEM((TILES, 2, SPAN * LANES), F32)],
         compiler_params=pltpu.CompilerParams(vmem_limit_bytes=VMEM_LIMIT),
         name="score",
-    )(got, slices, tabx, taby)
-
-
-def expand(place, values, tops):
-    def kernel(place_ref, value_ref, top_ref, refined_ref, best_ref):
-        place = jnp.concatenate([place_ref[0], place_ref[1]], axis=1)
-        top = jnp.max(top_ref[...], axis=0, keepdims=True)
-        rows = jnp.concatenate([value_ref[...], jnp.broadcast_to(top, (8, top.shape[1]))], axis=0)
-        out = lax.dot_general(rows, place, NT, preferred_element_type=F32, precision=lax.Precision.HIGHEST)
-        refined_ref[...] = out[:GRID]
-        best_ref[...] = out[GRID : GRID + 1]
+    )(rot, got, share, slices, tabx, taby)
+
+
+def expand(place, sums):
+    def kernel(place_ref, sum_ref, refined_ref, top_ref):
+        place = jnp.concatenate([place_ref[0].astype(BF), place_ref[1].astype(BF)], axis=1)
+        lane = lax.broadcasted_iota(I32, (GRID, LANES), 1)
+        row = lax.broadcasted_iota(I32, (GRID, LANES), 0)
+        sums = [sum_ref[r // SPAN : r // SPAN + 1, r % SPAN * LANES : (r % SPAN + 1) * LANES] for r in range(GRID + 1)]
+        last = jnp.broadcast_to(sums[GRID], (GRID, LANES))
+        last = jnp.sum(jnp.where(lane == row, last, 0.0), axis=1, keepdims=True)
+        rest = jnp.concatenate([jnp.concatenate(sums[:GRID], axis=0), jnp.where(lane == 0, last, 0.0)], axis=1) * (1.0 / DFT)
+        parts = []
+        for _ in range(3):
+            parts.append(rest.astype(BF).astype(F32))
+            rest = rest - parts[-1]
+        parts = jnp.concatenate(parts, axis=0).astype(BF)
+        out = lax.dot_general(parts, place, NT, preferred_element_type=F32)
+        refined = (out[:GRID] + out[GRID : 2 * GRID]) + out[2 * GRID :]
+        refined_ref[...] = refined
+        top = jnp.max(refined, axis=0, keepdims=True)
+        top_ref[...] = jnp.broadcast_to(top[None], top_ref.shape)
 
     return pl.pallas_call(
         kernel,
         out_shape=(
             jax.ShapeDtypeStruct((GRID, SLOTS * TILES), F32),
-            jax.ShapeDtypeStruct((1, SLOTS * TILES), F32),
+            jax.ShapeDtypeStruct((TILES, 1, SLOTS * TILES), F32),
         ),
-        in_specs=[VM] * 3,
+        in_specs=[VM] * 2,
         out_specs=(VM, VM),
         name="expand",
-    )(place, values, tops)
+    )(place, sums)
+
+
+def highest(tops, scores):
+    def kernel(top_ref, score_ref, best_ref, out_ref):
+        best_ref[...] = jnp.max(top_ref[...], axis=0)
+        out_ref[...] = score_ref[...]
+
+    return pl.pallas_call(
+        kernel,
+        out_shape=(jax.ShapeDtypeStruct(tops.shape[1:], F32), jax.ShapeDtypeStruct(scores.shape, F32)),
+        in_specs=[VM] * 2,
+        out_specs=(VM, VM),
+        name="highest",
+    )(tops, scores)
 
 
 def finish(parts):
@@ -321,8 +367,9 @@
             cols = slice(b * LANES, (b + 1) * LANES)
             tops = [ref[0, :, cols].astype(F32) for ref in ins]
             sums = [ref[1, :, cols].astype(F32) for ref in ins]
-            top = jnp.maximum(jnp.maximum(tops[0], tops[1]), jnp.maximum(tops[2], tops[3]))
-            top_ref[pl.ds(b, HALF, stride=ROWS), :] = top
+            top_ref[pl.ds(b, HALF, stride=ROWS), :] = jnp.maximum(
+                jnp.maximum(tops[0], tops[1]), jnp.maximum(tops[2], tops[3])
+            )
             total = (sums[0] + sums[1]) + (sums[2] + sums[3])
             mean_ref[pl.ds(b, HALF, stride=ROWS), :] = total * (1.0 / ORIENTS)
 
@@ -332,6 +379,7 @@
         out_shape=(shape, shape),
         in_specs=[VM] * 4,
         out_specs=(VM, VM),
+        cost_estimate=pl.CostEstimate(flops=1, transcendentals=0, bytes_accessed=1),
         name="finish",
     )(*parts)
 
@@ -361,42 +409,42 @@
     taby = taby.reshape(ROWS, 4, DFT).transpose(1, 0, 2).reshape(4 * ROWS, DFT)
     taby = jnp.pad(taby, ((0, 16 - 4 * ROWS), (0, 0)))
 
-    fields = jnp.stack(
-        [peak_orient, peak_row // BASE, peak_row % BASE, peak_col // BASE, peak_col % BASE], axis=1
-    ).reshape(1, -1)
-    fields = jnp.concatenate([fields, peak_count.reshape(1, 1)], axis=1).astype(F32)
-    fields = jnp.pad(fields, ((0, 0), (0, LANES - 5 * SLOTS - 1)))
     grid = ctf_grid.reshape(GRID, TILES, BINS).transpose(1, 0, 2).reshape(TILES, GRID * BINS)
     spec = spectrum.reshape(2, HALF, DFT)
     filt = ctf_filter.reshape(HALF, DFT)
-    got = lax.all_to_all(prepare(spec, grid, fields), "tile", 0, 0, tiled=True)
-
-    blocks, slices = interpolate(
+    rot = lax.axis_index("rot").reshape(1)
+    blocks, slices = prepare(
+        rot,
         interp_index.reshape(-1, LANES),
-        interp_weight.reshape(-1, LANES),
-        volume.reshape(2, -1, LANES).astype(F32),
+        interp_weight.reshape(8, 2, ROWS, DFT),
+        volume.reshape(2, -1),
+        spec,
+        grid,
+        peak_orient,
+        peak_row,
+        peak_col,
+        peak_count,
     )
-    mine = lax.all_to_all(blocks, "tile", 0, 0, tiled=True)
-    packed, place = score(got, slices, tabx, taby)
+    got = lax.all_to_all(blocks, "tile", 0, 0, tiled=True)
+    share, mine = exchange(got[:, :SHARE], "rot", 1), got[:, SHARE:]
     other = exchange(mine, "tile", 1)
     keep, send = correlate(jnp.stack([nar, tile % 2]), mine, other, spec, filt, tabx, back)
+    got, share, send = lax.optimization_barrier((got, share, send))
     extra_rows = exchange(send, "nar", 1)
-
+    packed, place = score(rot, got, share, slices, tabx, taby)
     sums = lax.all_to_all(packed, "tile", 0, 0, tiled=True)
-    sums = jnp.sum(sums.astype(F32), axis=0)
-    sums = lax.psum(sums, "nar") * (1.0 / DFT)
-    last = jnp.zeros((GRID, LANES), F32).at[:, 0].set(sums[GRID * LANES : GRID * LANES + GRID])
-    values = jnp.concatenate([sums[: GRID * LANES].reshape(GRID, LANES), last], axis=1)
-    top = jnp.max(values, axis=0)
 
     corr = (keep.astype(F32) + extra_rows.astype(F32)) * (1.0 / DFT)
     stats = jnp.stack([jnp.maximum(corr[0], corr[1]), corr[0] + corr[1]]).astype(BF)
     others = [exchange(stats, "rot", bit) for bit in (1, 2, 3)]
 
-    tops = lax.all_to_all(jnp.broadcast_to(top[None], (TILES, 2 * LANES)), "tile", 0, 0, tiled=True)
-    refined, best = expand(place, values, tops)
-
+    sums = jnp.sum(sums.astype(F32), axis=0)
+    sums = sums + exchange(sums, "nar", 1)
+    refined, tops = expand(place, sums)
+    tops = lax.all_to_all(tops, "tile", 0, 0)
     peak, mean = finish([stats] + others)
+    tops, peak, mean = lax.optimization_barrier((tops, peak, mean))
+    best, refined = highest(tops, refined)
     return (
         peak.reshape(1, 1, -1),
         mean.reshape(1, 1, -1),

time: 155 us -> 145 us (0.935)
  blocking collectives: 5.36 us -> 54 us
  waiting for transfers between devices: 65.6 us -> 24 us
  starting transfers between devices: 52.1 us -> 37.9 us
  other arithmetic: 4.93 us -> 1.02 us
  Pallas kernels: 14 us -> 17.1 us
  local copies, waits for them, and re-layouts: 10.9 us -> 8.26 us
    all_to_all x0 -> x1, blocking collectives: none -> 54 us  [shards(): got = lax.all_to_all(blocks, 'tile', 0, 0, tiled=True)]
    all_to_all x3 -> x1, waiting for transfers between devices: 46.8 us -> 10.9 us  [shards(): tops = lax.all_to_all(tops, 'tile', 0, 0)]
    all_to_all x3 -> x1, starting transfers between devices: 29.2 us -> 7.18 us  [shards(): tops = lax.all_to_all(tops, 'tile', 0, 0)]
    ppermute x5 -> x7, starting transfers between devices: 15.8 us -> 22 us  [exchange(): return lax.ppermute(x, axis, [(k, k ^ bit) for k in range(size)])]
    psum x1 -> x0, blocking collectives: 5.36 us -> none  [shards(): sums = lax.psum(sums, 'nar') * (1.0 / DFT)]
    ppermute x5 -> x7, waiting for transfers between devices: 9.68 us -> 4.65 us  [exchange(): return lax.ppermute(x, axis, [(k, k ^ bit) for k in range(size)])]
    pallas_call x3, Pallas kernels: 6.94 us -> 10.1 us  [the longest x1 4.99 us: score(): pl.pallas_call(kernel, out_shape=(jax.ShapeDtypeStruct((TILES, 2, SPAN *...]
    unnamed x33 -> x35, local copies, waits for them, and re-layouts: 7.24 us -> 5.31 us
  transfers between devices with their start and end apart: 9 -> 9, of which waited for: 6 -> 4; matrix products, arithmetic and copies ran while one was open for 4% -> 1% of each run, Pallas kernels for 4% -> 8%
where the time goes in v3:
time: 145 us; the launch traced here: 144 us
  blocking collectives  54 us (37%)
  starting transfers between devices  37.9 us (26%)
  waiting for transfers between devices  24 us (17%)
  Pallas kernels  17.1 us (12%)
  local copies, waits for them, and re-layouts  8.26 us (6%)
  between operations  1.68 us (1%)
    all_to_all x1, blocking collectives, shards(): got = lax.all_to_all(blocks, 'tile', 0, 0, tiled=True)  54 us
    ppermute x7, starting transfers between devices, exchange(): return lax.ppermute(x, axis, [(k, k ^ bit) for k in range(size)])  22 us
    all_to_all x1, waiting for transfers between devices, shards(): tops = lax.all_to_all(tops, 'tile', 0, 0)  10.9 us
    all_to_all x1, starting transfers between devices, shards(): sums = lax.all_to_all(packed, 'tile', 0, 0, tiled=True)  8.73 us
    all_to_all x1, waiting for transfers between devices, shards(): sums = lax.all_to_all(packed, 'tile', 0, 0, tiled=True)  8.43 us
    all_to_all x1, starting transfers between devices, shards(): tops = lax.all_to_all(tops, 'tile', 0, 0)  7.18 us
    unnamed x35, local copies, waits for them, and re-layouts  5.31 us
    pallas_call x1, Pallas kernels, score(): pl.pallas_call(kernel, out_shape=(jax.ShapeDtypeStruct((TILES, 2, SPAN *...  4.99 us
  transfers between devices with their start and end apart: 9, of which 4 were waited for; matrix products, arithmetic and copies ran while one was open for 1% of the time, Pallas kernels for 8%

profile of v3, /device:TPU:1, one launch (start us, length us, event | category | flops | bytes accessed | tf_op | source)
XLA Modules:
  0.0 143.9 jit_solution(17240399815556291443)
XLA Ops:
  0.6 0.0 copy-start.7
  0.6 0.0 copy-start.8
  0.7 0.0 copy-start.1
  0.7 0.0 copy-start.9
  0.7 0.0 copy-start.10
  0.7 0.0 copy-start.11
  0.7 0.8 copy.23
  1.5 1.6 %reshape.52 = bf16[8,64,288]{2,1,0:T(8,128)(2,1)S(1)} reshape(bf16[8,1,18432]{2,0,1:T(8,128)(2,1)} %param.21) | data formatting | bytes 589824 | tf_op jit(solution)/shard_map/reshape | solution.py:412
  3.1 0.2 copy.22
  3.4 0.3 reshape.53.grid_ref
  4.3 0.0 copy-done.7
  4.4 0.0 copy-done.8
  4.4 0.0 copy-done.1
  4.4 0.0 copy-done.9
  4.4 0.0 copy-done.10
  4.4 0.0 copy-done.11
  4.4 3.7 %prepare.1 = (bf16[64,40,128]{2,1,0:T(8,128)(2,1)S(1)}, f32[2,18,128]{2,1,0:T(8,128)S(1)}) custom-call(s32[1]{0:T(128)} %bitcast.rot_ref, s32[144,128]{1,0:T(8,128)S(1)} %bitcast.27, bf16[8,2,3,384]{3,2,1,0:T(4,128)(2,1)S(1)} %bitcast.25, bf16[2,4096]{1,0:T(2,128)(2,1)S(1)} %bitcast.28, bf16[2,192,384]{2,1,0:T(8,128)(2,1)S(1)} %bitcast.23, ...), custom_call_target="tpu_custom_call" | custom-call | tf_op jit(solution)/shard_map/prepare/pallas_call | solution.py:136
  8.1 0.0 copy-start
  8.1 0.0 copy-start.2
  8.1 54.0 %all_to_all.15.got_ref = bf16[64,40,128]{2,1,0:T(8,128)(2,1)S(1)} all-to-all(bf16[64,40,128]{2,1,0:T(8,128)(2,1)S(1)} %get-tuple-element.22), channel_id=1, replica_groups=mesh['rot'=4,'tile'=64,'nar'=2] {'tile'}, dimensions={0} | all-to-all | bytes 1310720 | tf_op jit(solution)/shard_map/all_to_all | solution.py:428
  62.2 1.9 %collective-permute-start.1 = (bf16[64,24,128]{2,1,0:T(8,128)(2,1)S(1)}, bf16[64,24,128]{2,1,0:T(8,128)(2,1)S(1)}, u32[]{:S(2)}, u32[]{:S(2)}) collective-permute-start(bf16[64,24,128]{2,1,0:T(8,128)(2,1)S(1)} %slice.19.own_ref), channel_id=1, source_target_pairs={{0,2},{2,0},{4,6},{6,4},{8,10},{10,8},{12,14},{14,12},{16,18},{18,... | collective-permute-start | bytes 1179656 | tf_op jit(solution)/shard_map/ppermute | solution.py:389
  64.1 0.7 slice.18
  64.8 3.2 %collective-permute-start = (bf16[64,16,128]{2,1,0:T(8,128)(2,1)}, bf16[64,16,128]{2,1,0:T(8,128)(2,1)}, u32[]{:S(2)}, u32[]{:S(2)}) collective-permute-start(bf16[64,16,128]{2,1,0:T(8,128)(2,1)} %slice.18), channel_id=1, source_target_pairs={{0,128},{128,0},{256,384},{384,256},{1,129},{129,1},{257,385},{385... | collective-permute-start | bytes 786440 | tf_op jit(solution)/shard_map/ppermute | solution.py:389
  68.1 0.1 pad_add_fusion.at_ref
  68.1 0.0 collective-permute-done.1.other_ref
  68.1 0.0 copy-done
  68.1 0.0 copy-done.2
  68.1 0.0 copy-start.6
  68.2 0.9 copy-done.6
  69.1 3.0 %correlate.1 = (bf16[2,192,384]{2,1,0:T(8,128)(2,1)S(1)}, bf16[2,192,384]{2,1,0:T(8,128)(2,1)}) custom-call(s32[2]{0:T(128)S(1)} %pad_add_fusion.at_ref, bf16[64,24,128]{2,1,0:T(8,128)(2,1)S(1)} %slice.19.own_ref, bf16[64,24,128]{2,1,0:T(8,128)(2,1)S(1)} %collective-permute-done.1.other_ref, bf16[2,192,384]{2,1,0:T(8,128)(2,1)S(1)} %bitcast.24, ...), custom_call_target="tpu_custom_call" | custom-call | tf_op jit(solution)/shard_map/correlate/pallas_call | solution.py:204
  72.1 0.7 copy-done.3
  72.8 1.6 %collective-permute-done.share_ref = bf16[64,16,128]{2,1,0:T(8,128)(2,1)} collective-permute-done((bf16[64,16,128]{2,1,0:T(8,128)(2,1)}, bf16[64,16,128]{2,1,0:T(8,128)(2,1)}, u32[]{:S(2)}, u32[]{:S(2)}) %collective-permute-start) | collective-permute-done | bytes 262176 | tf_op jit(solution)/shard_map/ppermute | solution.py:389
  74.4 4.3 %collective-permute-start.3 = (bf16[2,192,384]{2,1,0:T(8,128)(2,1)}, bf16[2,192,384]{2,1,0:T(8,128)(2,1)S(1)}, u32[]{:S(2)}, u32[]{:S(2)}) collective-permute-start(bf16[2,192,384]{2,1,0:T(8,128)(2,1)} %get-tuple-element.31), channel_id=1, source_target_pairs={{0,1},{1,0},{2,3},{3,2},{4,5},{5,4},{6,7},{7,6},{8,9},{9,8},{10,11... | collective-permute-start | bytes 884744 | tf_op jit(solution)/shard_map/ppermute | solution.py:389
  78.8 0.0 copy-start.4
  78.9 5.0 %score.1 = (bf16[64,2,640]{2,1,0:T(2,128)(2,1)}, f32[2,256,128]{2,1,0:T(8,128)S(1)}) custom-call(s32[1]{0:T(128)} %bitcast.rot_ref, bf16[64,40,128]{2,1,0:T(8,128)(2,1)S(1)} %all_to_all.15.got_ref, bf16[64,16,128]{2,1,0:T(8,128)(2,1)} %collective-permute-done.share_ref, f32[2,18,128]{2,1,0:T(8,128)S(1)} %get-tuple-element.26.slice_ref, ...), custom_call_target="tpu_custom_call" | custom-call | tf_op jit(solution)/shard_map/score/pallas_call | solution.py:303
  83.8 0.7 copy-done.5
  84.5 8.7 %all-to-all-start.1 = ((bf16[64,2,640]{2,1,0:T(2,128)(2,1)}), bf16[64,2,640]{2,1,0:T(2,128)(2,1)S(1)}, u32[]{:S(2)}, u32[]{:S(2)}) async-start(bf16[64,2,640]{2,1,0:T(2,128)(2,1)} %get-tuple-element.28), calls=%async_computation.1 | async-start | bytes 327680 | tf_op jit(solution)/shard_map/all_to_all | solution.py:435
  93.3 0.0 collective-permute-done.3
  93.3 0.0 copy-done.4
  93.3 0.1 add_multiply_fusion
  93.5 0.0 copy-start.12
  93.5 3.2 %collective-permute-start.4 = (bf16[2,192,384]{2,1,0:T(8,128)(2,1)S(1)}, bf16[2,192,384]{2,1,0:T(8,128)(2,1)S(1)}, u32[]{:S(2)}, u32[]{:S(2)}) collective-permute-start(bf16[2,192,384]{2,1,0:T(8,128)(2,1)S(1)} %pad_maximum_fusion.refs_0_), channel_id=1, source_target_pairs={{0,128},{128,0},{256,384},{384,256},{1,129},{129,1},{257,385},{385... | collective-permute-start | bytes 884744 | tf_op jit(solution)/shard_map/ppermute | solution.py:389
  96.7 4.5 %collective-permute-start.5 = (bf16[2,192,384]{2,1,0:T(8,128)(2,1)S(1)}, bf16[2,192,384]{2,1,0:T(8,128)(2,1)S(1)}, u32[]{:S(2)}, u32[]{:S(2)}) collective-permute-start(bf16[2,192,384]{2,1,0:T(8,128)(2,1)S(1)} %pad_maximum_fusion.refs_0_), channel_id=1, source_target_pairs={{0,256},{128,384},{256,0},{384,128},{1,257},{129,385},{257,1},{385... | collective-permute-start | bytes 884744 | tf_op jit(solution)/shard_map/ppermute | solution.py:389
  101.3 1.9 %collective-permute-start.6 = (bf16[2,192,384]{2,1,0:T(8,128)(2,1)S(1)}, bf16[2,192,384]{2,1,0:T(8,128)(2,1)S(1)}, u32[]{:S(2)}, u32[]{:S(2)}) collective-permute-start(bf16[2,192,384]{2,1,0:T(8,128)(2,1)S(1)} %pad_maximum_fusion.refs_0_), channel_id=1, source_target_pairs={{0,384},{128,256},{256,128},{384,0},{1,385},{129,257},{257,129},{3... | collective-permute-start | bytes 884744 | tf_op jit(solution)/shard_map/ppermute | solution.py:389
  103.2 8.4 %all-to-all-done.1 = bf16[64,2,640]{2,1,0:T(2,128)(2,1)S(1)} async-done(((bf16[64,2,640]{2,1,0:T(2,128)(2,1)}), bf16[64,2,640]{2,1,0:T(2,128)(2,1)S(1)}, u32[]{:S(2)}, u32[]{:S(2)}) %all-to-all-start.1) | async-done | bytes 163872 | tf_op jit(solution)/shard_map/all_to_all | solution.py:435
  111.6 0.2 convert_reduce_fusion
  111.8 2.8 %collective-permute-start.2 = (f32[2,640]{1,0:T(2,128)S(1)}, f32[2,640]{1,0:T(2,128)S(1)}, u32[]{:S(2)}, u32[]{:S(2)}) collective-permute-start(f32[2,640]{1,0:T(2,128)S(1)} %convert_reduce_fusion), channel_id=1, source_target_pairs={{0,1},{1,0},{2,3},{3,2},{4,5},{5,4},{6,7},{7,6},{8,9},{9,8},{10,11... | collective-permute-start | bytes 15368 | tf_op jit(solution)/shard_map/ppermute | solution.py:389
  114.7 3.0 %collective-permute-done.2 = f32[2,640]{1,0:T(2,128)S(1)} collective-permute-done((f32[2,640]{1,0:T(2,128)S(1)}, f32[2,640]{1,0:T(2,128)S(1)}, u32[]{:S(2)}, u32[]{:S(2)}) %collective-permute-start.2) | collective-permute-done | bytes 5152 | tf_op jit(solution)/shard_map/ppermute | solution.py:389
  117.7 0.6 add.25.sum_ref
  118.3 1.8 %expand.1 = (f32[8,256]{1,0:T(8,128)}, f32[64,1,256]{2,1,0:T(1,128)}) custom-call(f32[2,256,128]{2,1,0:T(8,128)} %copy-done.5, f32[2,640]{1,0:T(2,128)} %add.25.sum_ref), custom_call_target="tpu_custom_call" | custom-call | tf_op jit(solution)/shard_map/expand/pallas_call | solution.py:337
  120.1 7.2 %all-to-all-start.2 = ((f32[64,1,256]{2,1,0:T(1,128)}), f32[64,1,256]{2,1,0:T(1,128)S(1)}, u32[]{:S(2)}, u32[]{:S(2)}) async-start(f32[64,1,256]{2,1,0:T(1,128)} %get-tuple-element.29), calls=%async_computation.2 | async-start | bytes 131072 | tf_op jit(solution)/shard_map/all_to_all | solution.py:444
  127.2 0.0 collective-permute-done.4.refs_1_
  127.2 0.0 copy-start.13
  127.3 0.0 collective-permute-done.5.refs_2_
  127.3 0.0 copy-start.14
  127.3 0.0 collective-permute-done.6.refs_3_
  127.3 0.0 copy-done.12
  127.3 0.7 copy-done.13
  128.0 0.1 copy-done.14
  128.1 0.7 copy-done.15
  128.8 2.2 %finish.1 = (f32[576,128]{1,0:T(8,128)}, f32[576,128]{1,0:T(8,128)}) custom-call(bf16[2,192,384]{2,1,0:T(8,128)(2,1)} %copy-done.12, bf16[2,192,384]{2,1,0:T(8,128)(2,1)} %copy-done.13, bf16[2,192,384]{2,1,0:T(8,128)(2,1)} %copy-done.14, bf16[2,192,384]{2,1,0:T(8,128)(2,1)} %copy-done.15), custom_call_target="tpu_custom_call" | custom-call | flops 1 | bytes 1 | tf_op jit(solution)/shard_map/finish/pallas_call | solution.py:377
  130.9 10.9 %all-to-all-done.2.top_ref = f32[64,1,256]{2,1,0:T(1,128)S(1)} async-done(((f32[64,1,256]{2,1,0:T(1,128)}), f32[64,1,256]{2,1,0:T(1,128)S(1)}, u32[]{:S(2)}, u32[]{:S(2)}) %all-to-all-start.2) | async-done | bytes 65568 | tf_op jit(solution)/shard_map/all_to_all | solution.py:444
  141.8 0.6 copy-done.16
  142.4 1.4 %highest.1 = (f32[1,256]{1,0:T(1,128)}, f32[8,256]{1,0:T(8,128)}) custom-call(f32[64,1,256]{2,1,0:T(1,128)} %copy-done.16, f32[8,256]{1,0:T(8,128)} %get-tuple-element.37.score_ref), custom_call_target="tpu_custom_call" | custom-call | tf_op jit(solution)/shard_map/highest/pallas_call | solution.py:354
  (11 shorter events, 0.2 us)
Async XLA Ops:
  0.6 3.7 %copy-start.7 = (s32[8,2,1,3,384]{4,2,3,1,0:T(1,128)S(1)}, s32[8,2,1,3,384]{4,2,3,1,0:T(1,128)}, u32[]{:S(2)}) copy-start(s32[8,2,1,3,384]{4,2,3,1,0:T(1,128)} %param.12) | copy-start | bytes 221188
  0.6 3.7 %copy-start.8 = (bf16[2,1,1,4096]{3,0,2,1:T(2,128)(2,1)S(1)}, bf16[2,1,1,4096]{3,0,2,1:T(2,128)(2,1)}, u32[]{:S(2)}) copy-start(bf16[2,1,1,4096]{3,0,2,1:T(2,128)(2,1)} %param.14) | copy-start | bytes 49156
  0.7 3.7 %copy-start.1 = (bf16[2,1,1,192,384]{4,3,2,1,0:T(8,128)(2,1)S(1)}, bf16[2,1,1,192,384]{4,3,2,1,0:T(8,128)(2,1)}, u32[]{:S(2)}) copy-start(bf16[2,1,1,192,384]{4,3,2,1,0:T(8,128)(2,1)} %param.15) | copy-start | bytes 884740
  0.7 3.7 %copy-start.9 = (s32[4]{0:T(128)S(1)}, s32[4]{0:T(128)}, u32[]{:S(2)}) copy-start(s32[4]{0:T(128)} %orient_ref.1) | copy-start | bytes 52
  0.7 3.7 %copy-start.10 = (s32[4]{0:T(128)S(1)}, s32[4]{0:T(128)}, u32[]{:S(2)}) copy-start(s32[4]{0:T(128)} %row_ref.1) | copy-start | bytes 52
  0.7 3.7 %copy-start.11 = (s32[4]{0:T(128)S(1)}, s32[4]{0:T(128)}, u32[]{:S(2)}) copy-start(s32[4]{0:T(128)} %col_ref.1) | copy-start | bytes 52
  8.1 60.1 %copy-start = (bf16[384,1536]{1,0:T(8,128)(2,1)S(1)}, bf16[384,1536]{1,0:T(8,128)(2,1)}, u32[]{:S(2)}) copy-start(bf16[384,1536]{1,0:T(8,128)(2,1)} %constant.45.clone.tabx_ref) | copy-start | bytes 3538948
  8.1 60.1 %copy-start.2 = (bf16[2,384,384]{2,1,0:T(8,128)(2,1)S(1)}, bf16[2,384,384]{2,1,0:T(8,128)(2,1)}, u32[]{:S(2)}) copy-start(bf16[2,384,384]{2,1,0:T(8,128)(2,1)} %constant.44.clone.back_ref) | copy-start | bytes 1769476
  62.2 6.0 %collective-permute-start.1 = (bf16[64,24,128]{2,1,0:T(8,128)(2,1)S(1)}, bf16[64,24,128]{2,1,0:T(8,128)(2,1)S(1)}, u32[]{:S(2)}, u32[]{:S(2)}) collective-permute-start(bf16[64,24,128]{2,1,0:T(8,128)(2,1)S(1)} %slice.19.own_ref), channel_id=1, source_target_pairs={{0,2},{2,0},{4,6},{6,4},{8,10},{10,8},{12,14},{14,12},{16,18},{18,... | collective-permute-start | bytes 1179656 | tf_op jit(solution)/shard_map/ppermute | solution.py:389
  64.8 9.6 %collective-permute-start = (bf16[64,16,128]{2,1,0:T(8,128)(2,1)}, bf16[64,16,128]{2,1,0:T(8,128)(2,1)}, u32[]{:S(2)}, u32[]{:S(2)}) collective-permute-start(bf16[64,16,128]{2,1,0:T(8,128)(2,1)} %slice.18), channel_id=1, source_target_pairs={{0,128},{128,0},{256,384},{384,256},{1,129},{129,1},{257,385},{385... | collective-permute-start | bytes 786440 | tf_op jit(solution)/shard_map/ppermute | solution.py:389
  68.1 0.9 copy-start.6
  72.1 0.7 copy-start.3
  74.4 18.9 %collective-permute-start.3 = (bf16[2,192,384]{2,1,0:T(8,128)(2,1)}, bf16[2,192,384]{2,1,0:T(8,128)(2,1)S(1)}, u32[]{:S(2)}, u32[]{:S(2)}) collective-permute-start(bf16[2,192,384]{2,1,0:T(8,128)(2,1)} %get-tuple-element.31), channel_id=1, source_target_pairs={{0,1},{1,0},{2,3},{3,2},{4,5},{5,4},{6,7},{7,6},{8,9},{9,8},{10,11... | collective-permute-start | bytes 884744 | tf_op jit(solution)/shard_map/ppermute | solution.py:389
  78.8 14.5 %copy-start.4 = (bf16[2,192,384]{2,1,0:T(8,128)(2,1)S(1)}, bf16[2,192,384]{2,1,0:T(8,128)(2,1)}, u32[]{:S(2)}) copy-start(bf16[2,192,384]{2,1,0:T(8,128)(2,1)} %copy-done.3) | copy-start | bytes 884740
  83.8 0.7 copy-start.5
  84.5 27.1 %all-to-all-start.1 = ((bf16[64,2,640]{2,1,0:T(2,128)(2,1)}), bf16[64,2,640]{2,1,0:T(2,128)(2,1)S(1)}, u32[]{:S(2)}, u32[]{:S(2)}) async-start(bf16[64,2,640]{2,1,0:T(2,128)(2,1)} %get-tuple-element.28), calls=%async_computation.1 | async-start | bytes 327680 | tf_op jit(solution)/shard_map/all_to_all | solution.py:435
  93.5 33.8 %copy-start.12 = (bf16[2,192,384]{2,1,0:T(8,128)(2,1)}, bf16[2,192,384]{2,1,0:T(8,128)(2,1)S(1)}, u32[]{:S(2)}) copy-start(bf16[2,192,384]{2,1,0:T(8,128)(2,1)S(1)} %pad_maximum_fusion.refs_0_) | copy-start | bytes 884740
  93.5 33.7 %collective-permute-start.4 = (bf16[2,192,384]{2,1,0:T(8,128)(2,1)S(1)}, bf16[2,192,384]{2,1,0:T(8,128)(2,1)S(1)}, u32[]{:S(2)}, u32[]{:S(2)}) collective-permute-start(bf16[2,192,384]{2,1,0:T(8,128)(2,1)S(1)} %pad_maximum_fusion.refs_0_), channel_id=1, source_target_pairs={{0,128},{128,0},{256,384},{384,256},{1,129},{129,1},{257,385},{385... | collective-permute-start | bytes 884744 | tf_op jit(solution)/shard_map/ppermute | solution.py:389
  96.7 30.5 %collective-permute-start.5 = (bf16[2,192,384]{2,1,0:T(8,128)(2,1)S(1)}, bf16[2,192,384]{2,1,0:T(8,128)(2,1)S(1)}, u32[]{:S(2)}, u32[]{:S(2)}) collective-permute-start(bf16[2,192,384]{2,1,0:T(8,128)(2,1)S(1)} %pad_maximum_fusion.refs_0_), channel_id=1, source_target_pairs={{0,256},{128,384},{256,0},{384,128},{1,257},{129,385},{257,1},{385... | collective-permute-start | bytes 884744 | tf_op jit(solution)/shard_map/ppermute | solution.py:389
  101.3 26.0 %collective-permute-start.6 = (bf16[2,192,384]{2,1,0:T(8,128)(2,1)S(1)}, bf16[2,192,384]{2,1,0:T(8,128)(2,1)S(1)}, u32[]{:S(2)}, u32[]{:S(2)}) collective-permute-start(bf16[2,192,384]{2,1,0:T(8,128)(2,1)S(1)} %pad_maximum_fusion.refs_0_), channel_id=1, source_target_pairs={{0,384},{128,256},{256,128},{384,0},{1,385},{129,257},{257,129},{3... | collective-permute-start | bytes 884744 | tf_op jit(solution)/shard_map/ppermute | solution.py:389
  111.8 5.9 %collective-permute-start.2 = (f32[2,640]{1,0:T(2,128)S(1)}, f32[2,640]{1,0:T(2,128)S(1)}, u32[]{:S(2)}, u32[]{:S(2)}) collective-permute-start(f32[2,640]{1,0:T(2,128)S(1)} %convert_reduce_fusion), channel_id=1, source_target_pairs={{0,1},{1,0},{2,3},{3,2},{4,5},{5,4},{6,7},{7,6},{8,9},{9,8},{10,11... | collective-permute-start | bytes 15368 | tf_op jit(solution)/shard_map/ppermute | solution.py:389
  120.1 21.8 %all-to-all-start.2 = ((f32[64,1,256]{2,1,0:T(1,128)}), f32[64,1,256]{2,1,0:T(1,128)S(1)}, u32[]{:S(2)}, u32[]{:S(2)}) async-start(f32[64,1,256]{2,1,0:T(1,128)} %get-tuple-element.29), calls=%async_computation.2 | async-start | bytes 131072 | tf_op jit(solution)/shard_map/all_to_all | solution.py:444
  127.2 0.7 copy-start.13
  127.3 0.8 copy-start.14
  128.1 0.7 copy-start.15
  141.8 0.6 copy-start.16

commit v4 on v3

--- a/solution.py
+++ b/solution.py
@@ -31,6 +31,7 @@
 
 VM = pl.BlockSpec(memory_space=pltpu.VMEM)
 SM = pl.BlockSpec(memory_space=pltpu.SMEM)
+HB = pl.BlockSpec(memory_space=pltpu.HBM)
 NN = (((1,), (0,)), ((), ()))
 NT = (((1,), (1,)), ((), ()))
 
@@ -59,21 +60,32 @@
     return bf(back), np.concatenate([ch, cl, sh, sl], 1)
 
 
+def stay(x):
+    return pltpu.with_memory_space_constraint(x, pltpu.HBM)
+
+
 def every(ref, row, step):
     return ref[pl.ds(row, TILES, stride=step), :]
 
 
 def prepare(rot, index, weight, table, spectrum, grid, orient, row, col, count):
     def kernel(
-        rot_ref, index_ref, weight_ref, table_ref, spec_ref, grid_ref, orient_ref, row_ref, col_ref, count_ref,
-        out_ref, own_ref, table_s, weight_s, value_s, spec_s, all_s, out_s,
+        rot_ref, count_ref, *refs,
     ):
+        sources, (out_ref, own_ref), scratch = refs[:8], refs[8:10], refs[10:]
+        targets, (sems, table_s, weight_s, value_s, spec_s, grid_s, all_s, out_s) = scratch[:8], scratch[8:]
+        copies = [pltpu.make_async_copy(a, b, sems.at[i]) for i, (a, b) in enumerate(zip(sources, targets))]
+        for copy in copies:
+            copy.start()
+        index_ref, weight_ref, table_ref, spec_ref, grid_ref, orient_ref, row_ref, col_ref = targets
+        for copy in copies[:3]:
+            copy.wait()
         table_s[...] = table_ref[...].astype(F32)
         for k in range(8):
-            for o in range(2):
-                w = weight_ref[k, o].astype(F32)
+            for j in range(ROWS):
+                w = weight_ref[k, 0, j].astype(F32)
                 for b in range(ROWS):
-                    at = pl.ds(k * 2 * BLOCKS + o * BLOCKS + b, ROWS, stride=ROWS)
+                    at = pl.ds(k * 2 * BLOCKS + j * ROWS + b, 2, stride=BLOCKS)
                     weight_s[at, :] = w[:, b * LANES : (b + 1) * LANES]
 
         def step(v, carry):
@@ -104,6 +116,8 @@
                 total = total + value_s[c, k * 2 * BLOCKS : (k + 1) * 2 * BLOCKS, :]
             own_ref[c] = total.astype(BF).astype(F32)
 
+        for copy in copies[3:]:
+            copy.wait()
         odd = (lax.broadcasted_iota(I32, (TILES, LANES), 0) & 1) == 1
         for r in range(2 * BLOCKS):
             row = jnp.where(odd, own_ref[1, r : r + 1, :], own_ref[0, r : r + 1, :])
@@ -115,8 +129,19 @@
             for j in range(ROWS):
                 for b in range(ROWS):
                     all_s[c * BLOCKS + j * ROWS + b] = spec_s[c * ROWS + b, pl.ds(j, TILES, stride=ROWS), :]
-        for r in range(2 * BLOCKS):
-            all_s[2 * BLOCKS + r] = grid_ref[:, r * LANES : (r + 1) * LANES].astype(F32)
+        for k in range(TILES * BINS // LANES):
+            grid_s[k * GRID : (k + 1) * GRID, :] = grid_ref[:, k * LANES : (k + 1) * LANES].astype(F32)
+        for a in range(4):
+            first, shift = divmod(a * BINS, LANES)
+            pieces = []
+            for q in range(GRID):
+                blocks = [
+                    grid_s[pl.ds((first + k) * GRID + q, TILES // 4, stride=BLOCKS * GRID), :] for k in range(3)
+                ]
+                pieces.append(jnp.concatenate(blocks, axis=1)[:, shift : shift + BINS])
+            row = jnp.concatenate(pieces, axis=1)
+            for r in range(2 * BLOCKS):
+                all_s[2 * BLOCKS + r, pl.ds(a, TILES // 4, stride=4), :] = row[:, r * LANES : (r + 1) * LANES]
         for r in range(SHARE):
             out_s[pl.ds(r, TILES, stride=XROWS), :] = all_s[(rot_ref[0] & 1) * SHARE + r]
         for r in range(META - REST):
@@ -139,25 +164,40 @@
             jax.ShapeDtypeStruct((TILES, XROWS, LANES), BF),
             jax.ShapeDtypeStruct((2, 2 * BLOCKS, LANES), F32),
         ),
-        in_specs=[SM] + [VM] * 5 + [SM] * 4,
+        in_specs=[SM, SM] + [HB] * 8,
         out_specs=(VM, VM),
-        scratch_shapes=[
+        scratch_shapes=[pltpu.VMEM(x.shape, x.dtype) for x in (index, weight, table, spectrum, grid)]
+        + [pltpu.SMEM(x.shape, x.dtype) for x in (orient, row, col)]
+        + [
+            pltpu.SemaphoreType.DMA((8,)),
             pltpu.VMEM(table.shape, F32),
             pltpu.VMEM(index.shape, F32),
             pltpu.VMEM((2,) + index.shape, F32),
             pltpu.VMEM((2 * ROWS, HALF, LANES), F32),
+            pltpu.VMEM((GRID * TILES * BINS // LANES, LANES), F32),
             pltpu.VMEM((4 * BLOCKS, TILES, LANES), F32),
             pltpu.VMEM((TILES * XROWS, LANES), F32),
         ],
         compiler_params=pltpu.CompilerParams(vmem_limit_bytes=VMEM_LIMIT),
         name="prepare",
-    )(rot, index, weight, table, spectrum, grid, orient, row, col, count)
+    )(rot, count, *[stay(x) for x in (index, weight, table, spectrum, grid, orient, row, col)])
 
 
 def correlate(place, own, other, spectrum, filt, tabx, back):
-    def kernel(at_ref, own_ref, other_ref, spec_ref, filt_ref, tabx_ref, back_ref, keep_ref, send_ref, sl_s, spec_s):
+    def kernel(
+        at_ref, own_ref, other_ref, spec_hbm, filt_hbm, tabx_ref, back_ref, keep_ref, send_ref,
+        sl_s, spec_s, spec_ref, filt_ref, sems,
+    ):
+        copies = [
+            pltpu.make_async_copy(spec_hbm, spec_ref, sems.at[0]),
+            pltpu.make_async_copy(filt_hbm, filt_ref, sems.at[1]),
+        ]
+        for copy in copies:
+            copy.start()
         sl_s[at_ref[1]] = own_ref[...].astype(F32).reshape(TILES * SROWS, LANES)
         sl_s[1 - at_ref[1]] = other_ref[...].astype(F32).reshape(TILES * SROWS, LANES)
+        for copy in copies:
+            copy.wait()
         for c in range(2):
             for b in range(ROWS):
                 spec_s[c * ROWS + b] = spec_ref[c, :, b * LANES : (b + 1) * LANES].astype(F32)
@@ -204,21 +244,24 @@
     return pl.pallas_call(
         kernel,
         out_shape=(shape, shape),
-        in_specs=[SM] + [VM] * 6,
+        in_specs=[SM, VM, VM, HB, HB, VM, VM],
         out_specs=(VM, VM),
         scratch_shapes=[
             pltpu.VMEM((2, TILES * SROWS, LANES), F32),
             pltpu.VMEM((3 * ROWS, HALF, LANES), F32),
+            pltpu.VMEM(spectrum.shape, BF),
+            pltpu.VMEM(filt.shape, BF),
+            pltpu.SemaphoreType.DMA((2,)),
         ],
         compiler_params=pltpu.CompilerParams(vmem_limit_bytes=VMEM_LIMIT),
         name="correlate",
-    )(place, own, other, spectrum, filt, tabx, back)
+    )(place, own, other, stay(spectrum), stay(filt), tabx, back)
 
 
 def score(rot, got, share, slices, tabx, taby):
     def kernel(
         rot_ref, got_ref, share_ref, slice_ref, tabx_ref, taby_ref,
-        out_ref, place_ref, got_s, share_s, out_s,
+        out_ref, place_hbm, got_s, share_s, place_s, place_ref, sem, out_s,
     ):
         got_s[...] = got_ref[...].astype(F32).reshape(got_s.shape)
         side = rot_ref[0] & 1
@@ -248,8 +291,11 @@
             seat = jnp.where(count > float(i), offset + float(i), -1.0)
             hot = jnp.where(lane[:, :256] == seat, 1.0, 0.0)
             for h in range(2):
-                place_ref[h, pl.ds(i, TILES, stride=SLOTS), :] = hot[:, h * LANES : (h + 1) * LANES]
+                place_s[h, pl.ds(i, TILES, stride=SLOTS), :] = hot[:, h * LANES : (h + 1) * LANES]
             place.append(hot.astype(BF))
+        place_ref[...] = place_s[...].astype(BF)
+        leave = pltpu.make_async_copy(place_ref, place_hbm, sem)
+        leave.start()
         hot_x = jnp.concatenate(hot_x, axis=0)
         hot_y = jnp.concatenate(hot_y, axis=0)
         place = jnp.concatenate(place, axis=0)
@@ -258,7 +304,10 @@
         sx = wave[:, 2 * DFT : 3 * DFT] + wave[:, 3 * DFT :]
         tilt = lax.dot_general(hot_y, taby_ref[...], NT, preferred_element_type=F32)
         pieces = [[] for _ in range(SLOTS)]
+        second = [jnp.broadcast_to(meta[:, 5 * i : 5 * i + 1], (TILES, LANES)) > 0.5 for i in range(SLOTS)]
         for j in range(ROWS):
+            cosines = jnp.broadcast_to(tilt[:, j : j + 1] + tilt[:, 3 + j : 4 + j], (SLOTS * TILES, LANES))
+            sines = jnp.broadcast_to(tilt[:, 6 + j : 7 + j] + tilt[:, 9 + j : 10 + j], (SLOTS * TILES, LANES))
             for b in range(ROWS):
                 r = j * ROWS + b
                 cols = slice(b * LANES, (b + 1) * LANES)
@@ -271,11 +320,9 @@
                     plain.append(((mr * sr + mi * si).astype(BF).astype(F32), (mi * sr - mr * si).astype(BF).astype(F32)))
                 for i in range(SLOTS):
                     at = slice(i * TILES, (i + 1) * TILES)
-                    second = meta[:, 5 * i : 5 * i + 1] > 0.5
-                    pr = jnp.where(second, plain[1][0], plain[0][0])
-                    pi = jnp.where(second, plain[1][1], plain[0][1])
-                    cy = tilt[at, j : j + 1] + tilt[at, 3 + j : 4 + j]
-                    sy = tilt[at, 6 + j : 7 + j] + tilt[at, 9 + j : 10 + j]
+                    pr = jnp.where(second[i], plain[1][0], plain[0][0])
+                    pi = jnp.where(second[i], plain[1][1], plain[0][1])
+                    cy, sy = cosines[at], sines[at]
                     wx, vx = cx[at, cols], sx[at, cols]
                     pieces[i].append(cy * (pr * wx - pi * vx) - sy * (pr * vx + pi * wx))
         shifted = jnp.concatenate([jnp.concatenate(p, axis=1) for p in pieces], axis=0)
@@ -299,24 +346,26 @@
         out_s[:, 1, (SPAN - 2) * LANES : (SPAN - 1) * LANES] = extra
         out_s[:, 1, (SPAN - 1) * LANES :] = jnp.zeros((TILES, LANES), F32)
         out_ref[...] = out_s[...].astype(BF)
+        leave.wait()
 
     return pl.pallas_call(
         kernel,
         out_shape=(
             jax.ShapeDtypeStruct((TILES, 2, SPAN * LANES), BF),
-            jax.ShapeDtypeStruct((2, SLOTS * TILES, LANES), F32),
+            jax.ShapeDtypeStruct((2, SLOTS * TILES, LANES), BF),
         ),
         in_specs=[SM] + [VM] * 5,
-        out_specs=(VM, VM),
-        scratch_shapes=[pltpu.VMEM((TILES * XROWS, LANES), F32), pltpu.VMEM((2, TILES * SHARE, LANES), F32), pltpu.VMEM((TILES, 2, SPAN * LANES), F32)],
+        out_specs=(VM, HB),
+        scratch_shapes=[pltpu.VMEM((TILES * XROWS, LANES), F32), pltpu.VMEM((2, TILES * SHARE, LANES), F32), pltpu.VMEM((2, SLOTS * TILES, LANES), F32), pltpu.VMEM((2, SLOTS * TILES, LANES), BF), pltpu.SemaphoreType.DMA, pltpu.VMEM((TILES, 2, SPAN * LANES), F32)],
         compiler_params=pltpu.CompilerParams(vmem_limit_bytes=VMEM_LIMIT),
+        cost_estimate=pl.CostEstimate(flops=6_000_000_000, transcendentals=0, bytes_accessed=8_000_000),
         name="score",
     )(rot, got, share, slices, tabx, taby)
 
 
 def expand(place, sums):
     def kernel(place_ref, sum_ref, refined_ref, top_ref):
-        place = jnp.concatenate([place_ref[0].astype(BF), place_ref[1].astype(BF)], axis=1)
+        place = jnp.concatenate([place_ref[0], place_ref[1]], axis=1)
         lane = lax.broadcasted_iota(I32, (GRID, LANES), 1)
         row = lax.broadcasted_iota(I32, (GRID, LANES), 0)
         sums = [sum_ref[r // SPAN : r // SPAN + 1, r % SPAN * LANES : (r % SPAN + 1) * LANES] for r in range(GRID + 1)]
@@ -346,20 +395,6 @@
     )(place, sums)
 
 
-def highest(tops, scores):
-    def kernel(top_ref, score_ref, best_ref, out_ref):
-        best_ref[...] = jnp.max(top_ref[...], axis=0)
-        out_ref[...] = score_ref[...]
-
-    return pl.pallas_call(
-        kernel,
-        out_shape=(jax.ShapeDtypeStruct(tops.shape[1:], F32), jax.ShapeDtypeStruct(scores.shape, F32)),
-        in_specs=[VM] * 2,
-        out_specs=(VM, VM),
-        name="highest",
-    )(tops, scores)
-
-
 def finish(parts):
     def kernel(*refs):
         ins, (top_ref, mean_ref) = refs[:4], refs[4:]
@@ -409,14 +444,14 @@
     taby = taby.reshape(ROWS, 4, DFT).transpose(1, 0, 2).reshape(4 * ROWS, DFT)
     taby = jnp.pad(taby, ((0, 16 - 4 * ROWS), (0, 0)))
 
-    grid = ctf_grid.reshape(GRID, TILES, BINS).transpose(1, 0, 2).reshape(TILES, GRID * BINS)
+    grid = ctf_grid.reshape(GRID, TILES * BINS)
     spec = spectrum.reshape(2, HALF, DFT)
     filt = ctf_filter.reshape(HALF, DFT)
     rot = lax.axis_index("rot").reshape(1)
     blocks, slices = prepare(
         rot,
         interp_index.reshape(-1, LANES),
-        interp_weight.reshape(8, 2, ROWS, DFT),
+        interp_weight.transpose(0, 2, 3, 1, 4),
         volume.reshape(2, -1),
         spec,
         grid,
@@ -429,7 +464,7 @@
     share, mine = exchange(got[:, :SHARE], "rot", 1), got[:, SHARE:]
     other = exchange(mine, "tile", 1)
     keep, send = correlate(jnp.stack([nar, tile % 2]), mine, other, spec, filt, tabx, back)
-    got, share, send = lax.optimization_barrier((got, share, send))
+    got, send = lax.optimization_barrier((got, send))
     extra_rows = exchange(send, "nar", 1)
     packed, place = score(rot, got, share, slices, tabx, taby)
     sums = lax.all_to_all(packed, "tile", 0, 0, tiled=True)
@@ -444,7 +479,7 @@
     tops = lax.all_to_all(tops, "tile", 0, 0)
     peak, mean = finish([stats] + others)
     tops, peak, mean = lax.optimization_barrier((tops, peak, mean))
-    best, refined = highest(tops, refined)
+    best = jnp.max(tops, axis=0)
     return (
         peak.reshape(1, 1, -1),
         mean.reshape(1, 1, -1),

time: 145 us -> 137 us (0.945)
  local copies, waits for them, and re-layouts: 8.26 us -> 2.32 us
  waiting for transfers between devices: 24 us -> 22.2 us
    unnamed x35 -> x14, local copies, waits for them, and re-layouts: 5.31 us -> 1.5 us
    reshape x3 -> x0, local copies, waits for them, and re-layouts: 2.13 us -> none  [shards(): ctf_grid.reshape(GRID, TILES, BINS).transpose(1, 0, 2)]
    ppermute x7, waiting for transfers between devices: 4.65 us -> 2.87 us  [exchange(): return lax.ppermute(x, axis, [(k, k ^ bit) for k in range(size)])]
    pallas_call x2 -> x1, Pallas kernels: 4.45 us -> 3.94 us  [correlate(): pl.pallas_call(kernel, out_shape=(shape, shape), in_specs=[SM, VM, VM, HB...]
  transfers between devices with their start and end apart: 9 -> 9, of which waited for: 4 -> 3; matrix products, arithmetic and copies ran while one was open for 1% -> 1% of each run, Pallas kernels for 8% -> 10%
where the time goes in v4:
time: 137 us; the launch traced here: 136 us
  blocking collectives  54 us (39%)
  starting transfers between devices  36.9 us (27%)
  waiting for transfers between devices  22.2 us (16%)
  Pallas kernels  17.3 us (13%)
  local copies, waits for them, and re-layouts  2.32 us (2%)
  other arithmetic  1.68 us (1%)
  between operations  1.57 us (1%)
    all_to_all x1, blocking collectives, shards(): got = lax.all_to_all(blocks, 'tile', 0, 0, tiled=True)  54 us
    ppermute x7, starting transfers between devices, exchange(): return lax.ppermute(x, axis, [(k, k ^ bit) for k in range(size)])  22.1 us
    all_to_all x1, waiting for transfers between devices, shards(): tops = lax.all_to_all(tops, 'tile', 0, 0)  10.9 us
    all_to_all x1, waiting for transfers between devices, shards(): sums = lax.all_to_all(packed, 'tile', 0, 0, tiled=True)  8.5 us
    all_to_all x1, starting transfers between devices, shards(): sums = lax.all_to_all(packed, 'tile', 0, 0, tiled=True)  7.68 us
    all_to_all x1, starting transfers between devices, shards(): tops = lax.all_to_all(tops, 'tile', 0, 0)  7.18 us
    pallas_call x1, Pallas kernels, score(): pl.pallas_call(kernel, out_shape=(jax.ShapeDtypeStruct((TILES, 2, SPAN *...  5.3 us
    pallas_call x1, Pallas kernels, prepare(): pl.pallas_call(kernel, out_shape=(jax.ShapeDtypeStruct((TILES, XROWS, LAN...  4.19 us
  transfers between devices with their start and end apart: 9, of which 3 were waited for; matrix products, arithmetic and copies ran while one was open for 1% of the time, Pallas kernels for 10%

profile of v4, /device:TPU:1, one launch (start us, length us, event | category | flops | bytes accessed | tf_op | source)
XLA Modules:
  0.0 136.1 jit_solution(4610457500083463907)
XLA Ops:
  1.3 4.2 %prepare.1 = (bf16[64,40,128]{2,1,0:T(8,128)(2,1)S(1)}, f32[2,18,128]{2,1,0:T(8,128)S(1)}) custom-call(s32[1]{0:T(128)} %bitcast.rot_ref, s32[1,1]{1,0:T(1,128)S(6)} %copy.16.count_ref, s32[144,128]{1,0:T(8,128)} %bitcast.22, bf16[8,1,3,2,384]{4,3,2,1,0:T(2,128)(2,1)} %bitcast.24, bf16[2,4096]{1,0:T(2,128)(2,1)} %bitcast.25, bf16[2,192,384]{2,1,0:T(8,128)(2,1)} %bitcast.18, ...), custom_call_target="tpu_custom_call" | custom-call | tf_op jit(solution)/shard_map/prepare/pallas_call | solution.py:161
  5.5 0.0 copy-start
  5.5 0.0 copy-start.1
  5.5 54.0 %all_to_all.15.got_ref = bf16[64,40,128]{2,1,0:T(8,128)(2,1)S(1)} all-to-all(bf16[64,40,128]{2,1,0:T(8,128)(2,1)S(1)} %get-tuple-element.19), channel_id=1, replica_groups=mesh['rot'=4,'tile'=64,'nar'=2] {'tile'}, dimensions={0} | all-to-all | bytes 1310720 | tf_op jit(solution)/shard_map/all_to_all | solution.py:463
  59.6 1.9 %collective-permute-start = (bf16[64,24,128]{2,1,0:T(8,128)(2,1)S(1)}, bf16[64,24,128]{2,1,0:T(8,128)(2,1)S(1)}, u32[]{:S(2)}, u32[]{:S(2)}) collective-permute-start(bf16[64,24,128]{2,1,0:T(8,128)(2,1)S(1)} %slice.18.own_ref), channel_id=1, source_target_pairs={{0,2},{2,0},{4,6},{6,4},{8,10},{10,8},{12,14},{14,12},{16,18},{18,... | collective-permute-start | bytes 1179656 | tf_op jit(solution)/shard_map/ppermute | solution.py:424
  61.5 0.7 slice.19
  62.3 3.2 %collective-permute-start.1 = (bf16[64,16,128]{2,1,0:T(8,128)(2,1)}, bf16[64,16,128]{2,1,0:T(8,128)(2,1)}, u32[]{:S(2)}, u32[]{:S(2)}) collective-permute-start(bf16[64,16,128]{2,1,0:T(8,128)(2,1)} %slice.19), channel_id=1, source_target_pairs={{0,128},{128,0},{256,384},{384,256},{1,129},{129,1},{257,385},{385... | collective-permute-start | bytes 786440 | tf_op jit(solution)/shard_map/ppermute | solution.py:424
  65.5 0.0 copy-done
  65.5 0.1 pad_add_fusion.at_ref
  65.6 0.0 collective-permute-done.other_ref
  65.6 0.0 copy-done.1
  65.6 3.9 %correlate.1 = (bf16[2,192,384]{2,1,0:T(8,128)(2,1)S(1)}, bf16[2,192,384]{2,1,0:T(8,128)(2,1)}) custom-call(s32[2]{0:T(128)S(1)} %pad_add_fusion.at_ref, bf16[64,24,128]{2,1,0:T(8,128)(2,1)S(1)} %slice.18.own_ref, bf16[64,24,128]{2,1,0:T(8,128)(2,1)S(1)} %collective-permute-done.other_ref, bf16[2,192,384]{2,1,0:T(8,128)(2,1)} %bitcast.19, ...), custom_call_target="tpu_custom_call" | custom-call | tf_op jit(solution)/shard_map/correlate/pallas_call | solution.py:244
  69.6 4.4 %collective-permute-start.3 = (bf16[2,192,384]{2,1,0:T(8,128)(2,1)}, bf16[2,192,384]{2,1,0:T(8,128)(2,1)S(1)}, u32[]{:S(2)}, u32[]{:S(2)}) collective-permute-start(bf16[2,192,384]{2,1,0:T(8,128)(2,1)} %get-tuple-element.27), channel_id=1, source_target_pairs={{0,1},{1,0},{2,3},{3,2},{4,5},{5,4},{6,7},{7,6},{8,9},{9,8},{10,11... | collective-permute-start | bytes 884744 | tf_op jit(solution)/shard_map/ppermute | solution.py:424
  73.9 0.0 collective-permute-done.1.share_ref
  74.0 5.3 %score.1 = (bf16[64,2,640]{2,1,0:T(2,128)(2,1)}, bf16[2,256,128]{2,1,0:T(8,128)(2,1)S(1)}) custom-call(s32[1]{0:T(128)} %bitcast.rot_ref, bf16[64,40,128]{2,1,0:T(8,128)(2,1)S(1)} %all_to_all.15.got_ref, bf16[64,16,128]{2,1,0:T(8,128)(2,1)} %collective-permute-done.1.share_ref, f32[2,18,128]{2,1,0:T(8,128)S(1)} %get-tuple-element.22.slice_ref, ...), custom_call_target="tpu_custom_call" | custom-call | flops 6000000000 | bytes 8000000 | tf_op jit(solution)/shard_map/score/pallas_call | solution.py:351
  79.3 0.0 copy-start.2
  79.3 7.7 %all-to-all-start.1 = ((bf16[64,2,640]{2,1,0:T(2,128)(2,1)}), bf16[64,2,640]{2,1,0:T(2,128)(2,1)S(1)}, u32[]{:S(2)}, u32[]{:S(2)}) async-start(bf16[64,2,640]{2,1,0:T(2,128)(2,1)} %get-tuple-element.24), calls=%async_computation.1 | async-start | bytes 327680 | tf_op jit(solution)/shard_map/all_to_all | solution.py:470
  87.0 0.0 collective-permute-done.3
  87.0 0.1 add_multiply_fusion
  87.1 0.0 copy-done.2
  87.2 0.0 copy-start.3
  87.2 2.1 %collective-permute-start.4 = (bf16[2,192,384]{2,1,0:T(8,128)(2,1)S(1)}, bf16[2,192,384]{2,1,0:T(8,128)(2,1)S(1)}, u32[]{:S(2)}, u32[]{:S(2)}) collective-permute-start(bf16[2,192,384]{2,1,0:T(8,128)(2,1)S(1)} %pad_maximum_fusion.refs_0_), channel_id=1, source_target_pairs={{0,128},{128,0},{256,384},{384,256},{1,129},{129,1},{257,385},{385... | collective-permute-start | bytes 884744 | tf_op jit(solution)/shard_map/ppermute | solution.py:424
  89.3 4.8 %collective-permute-start.5 = (bf16[2,192,384]{2,1,0:T(8,128)(2,1)S(1)}, bf16[2,192,384]{2,1,0:T(8,128)(2,1)S(1)}, u32[]{:S(2)}, u32[]{:S(2)}) collective-permute-start(bf16[2,192,384]{2,1,0:T(8,128)(2,1)S(1)} %pad_maximum_fusion.refs_0_), channel_id=1, source_target_pairs={{0,256},{128,384},{256,0},{384,128},{1,257},{129,385},{257,1},{385... | collective-permute-start | bytes 884744 | tf_op jit(solution)/shard_map/ppermute | solution.py:424
  94.1 2.7 %collective-permute-start.6 = (bf16[2,192,384]{2,1,0:T(8,128)(2,1)S(1)}, bf16[2,192,384]{2,1,0:T(8,128)(2,1)S(1)}, u32[]{:S(2)}, u32[]{:S(2)}) collective-permute-start(bf16[2,192,384]{2,1,0:T(8,128)(2,1)S(1)} %pad_maximum_fusion.refs_0_), channel_id=1, source_target_pairs={{0,384},{128,256},{256,128},{384,0},{1,385},{129,257},{257,129},{3... | collective-permute-start | bytes 884744 | tf_op jit(solution)/shard_map/ppermute | solution.py:424
  96.8 8.5 %all-to-all-done.1 = bf16[64,2,640]{2,1,0:T(2,128)(2,1)S(1)} async-done(((bf16[64,2,640]{2,1,0:T(2,128)(2,1)}), bf16[64,2,640]{2,1,0:T(2,128)(2,1)S(1)}, u32[]{:S(2)}, u32[]{:S(2)}) %all-to-all-start.1) | async-done | bytes 163872 | tf_op jit(solution)/shard_map/all_to_all | solution.py:470
  105.3 0.2 convert_reduce_fusion
  105.5 3.0 %collective-permute-start.2 = (f32[2,640]{1,0:T(2,128)S(1)}, f32[2,640]{1,0:T(2,128)S(1)}, u32[]{:S(2)}, u32[]{:S(2)}) collective-permute-start(f32[2,640]{1,0:T(2,128)S(1)} %convert_reduce_fusion), channel_id=1, source_target_pairs={{0,1},{1,0},{2,3},{3,2},{4,5},{5,4},{6,7},{7,6},{8,9},{9,8},{10,11... | collective-permute-start | bytes 15368 | tf_op jit(solution)/shard_map/ppermute | solution.py:424
  108.5 2.9 %collective-permute-done.2 = f32[2,640]{1,0:T(2,128)S(1)} collective-permute-done((f32[2,640]{1,0:T(2,128)S(1)}, f32[2,640]{1,0:T(2,128)S(1)}, u32[]{:S(2)}, u32[]{:S(2)}) %collective-permute-start.2) | collective-permute-done | bytes 5152 | tf_op jit(solution)/shard_map/ppermute | solution.py:424
  111.3 0.6 add.25.sum_ref
  111.9 1.8 %expand.1 = (f32[8,256]{1,0:T(8,128)}, f32[64,1,256]{2,1,0:T(1,128)}) custom-call(bf16[2,256,128]{2,1,0:T(8,128)(2,1)} %copy-done.2, f32[2,640]{1,0:T(2,128)} %add.25.sum_ref), custom_call_target="tpu_custom_call" | custom-call | tf_op jit(solution)/shard_map/expand/pallas_call | solution.py:386
  113.7 7.2 %all-to-all-start.2 = ((f32[64,1,256]{2,1,0:T(1,128)}), f32[64,1,256]{2,1,0:T(1,128)S(1)}, u32[]{:S(2)}, u32[]{:S(2)}) async-start(f32[64,1,256]{2,1,0:T(1,128)} %get-tuple-element.25), calls=%async_computation.2 | async-start | bytes 131072 | tf_op jit(solution)/shard_map/all_to_all | solution.py:479
  120.9 0.0 collective-permute-done.4.refs_1_
  120.9 0.0 copy-start.4
  120.9 0.0 collective-permute-done.5.refs_2_
  120.9 0.0 copy-start.5
  120.9 0.0 collective-permute-done.6.refs_3_
  120.9 0.0 copy-done.3
  120.9 0.7 copy-done.4
  121.6 0.1 copy-done.5
  121.7 0.0 copy-start.6
  121.7 0.7 copy-done.6
  122.4 2.2 %finish.1 = (f32[576,128]{1,0:T(8,128)}, f32[576,128]{1,0:T(8,128)}) custom-call(bf16[2,192,384]{2,1,0:T(8,128)(2,1)} %copy-done.3, bf16[2,192,384]{2,1,0:T(8,128)(2,1)} %copy-done.4, bf16[2,192,384]{2,1,0:T(8,128)(2,1)} %copy-done.5, bf16[2,192,384]{2,1,0:T(8,128)(2,1)} %copy-done.6), custom_call_target="tpu_custom_call" | custom-call | flops 1 | bytes 1 | tf_op jit(solution)/shard_map/finish/pallas_call | solution.py:412
  124.6 10.9 %all-to-all-done.2 = f32[64,1,256]{2,1,0:T(1,128)S(1)} async-done(((f32[64,1,256]{2,1,0:T(1,128)}), f32[64,1,256]{2,1,0:T(1,128)S(1)}, u32[]{:S(2)}, u32[]{:S(2)}) %all-to-all-start.2) | async-done | bytes 65568 | tf_op jit(solution)/shard_map/all_to_all | solution.py:479
  135.5 0.7 reduce_max.11
  (7 shorter events, 0.2 us)
Async XLA Ops:
  5.5 60.0 %copy-start = (bf16[384,1536]{1,0:T(8,128)(2,1)S(1)}, bf16[384,1536]{1,0:T(8,128)(2,1)}, u32[]{:S(2)}) copy-start(bf16[384,1536]{1,0:T(8,128)(2,1)} %constant.47.clone.tabx_ref) | copy-start | bytes 3538948
  5.5 60.1 %copy-start.1 = (bf16[2,384,384]{2,1,0:T(8,128)(2,1)S(1)}, bf16[2,384,384]{2,1,0:T(8,128)(2,1)}, u32[]{:S(2)}) copy-start(bf16[2,384,384]{2,1,0:T(8,128)(2,1)} %constant.46.clone.back_ref) | copy-start | bytes 1769476
  59.6 6.0 %collective-permute-start = (bf16[64,24,128]{2,1,0:T(8,128)(2,1)S(1)}, bf16[64,24,128]{2,1,0:T(8,128)(2,1)S(1)}, u32[]{:S(2)}, u32[]{:S(2)}) collective-permute-start(bf16[64,24,128]{2,1,0:T(8,128)(2,1)S(1)} %slice.18.own_ref), channel_id=1, source_target_pairs={{0,2},{2,0},{4,6},{6,4},{8,10},{10,8},{12,14},{14,12},{16,18},{18,... | collective-permute-start | bytes 1179656 | tf_op jit(solution)/shard_map/ppermute | solution.py:424
  62.3 11.7 %collective-permute-start.1 = (bf16[64,16,128]{2,1,0:T(8,128)(2,1)}, bf16[64,16,128]{2,1,0:T(8,128)(2,1)}, u32[]{:S(2)}, u32[]{:S(2)}) collective-permute-start(bf16[64,16,128]{2,1,0:T(8,128)(2,1)} %slice.19), channel_id=1, source_target_pairs={{0,128},{128,0},{256,384},{384,256},{1,129},{129,1},{257,385},{385... | collective-permute-start | bytes 786440 | tf_op jit(solution)/shard_map/ppermute | solution.py:424
  69.6 17.4 %collective-permute-start.3 = (bf16[2,192,384]{2,1,0:T(8,128)(2,1)}, bf16[2,192,384]{2,1,0:T(8,128)(2,1)S(1)}, u32[]{:S(2)}, u32[]{:S(2)}) collective-permute-start(bf16[2,192,384]{2,1,0:T(8,128)(2,1)} %get-tuple-element.27), channel_id=1, source_target_pairs={{0,1},{1,0},{2,3},{3,2},{4,5},{5,4},{6,7},{7,6},{8,9},{9,8},{10,11... | collective-permute-start | bytes 884744 | tf_op jit(solution)/shard_map/ppermute | solution.py:424
  79.3 7.9 %copy-start.2 = (bf16[2,256,128]{2,1,0:T(8,128)(2,1)}, bf16[2,256,128]{2,1,0:T(8,128)(2,1)S(1)}, u32[]{:S(2)}) copy-start(bf16[2,256,128]{2,1,0:T(8,128)(2,1)S(1)} %get-tuple-element.23.place_ref) | copy-start | bytes 393220
  79.3 26.0 %all-to-all-start.1 = ((bf16[64,2,640]{2,1,0:T(2,128)(2,1)}), bf16[64,2,640]{2,1,0:T(2,128)(2,1)S(1)}, u32[]{:S(2)}, u32[]{:S(2)}) async-start(bf16[64,2,640]{2,1,0:T(2,128)(2,1)} %get-tuple-element.24), calls=%async_computation.1 | async-start | bytes 327680 | tf_op jit(solution)/shard_map/all_to_all | solution.py:470
  87.2 33.7 %copy-start.3 = (bf16[2,192,384]{2,1,0:T(8,128)(2,1)}, bf16[2,192,384]{2,1,0:T(8,128)(2,1)S(1)}, u32[]{:S(2)}) copy-start(bf16[2,192,384]{2,1,0:T(8,128)(2,1)S(1)} %pad_maximum_fusion.refs_0_) | copy-start | bytes 884740
  87.2 33.7 %collective-permute-start.4 = (bf16[2,192,384]{2,1,0:T(8,128)(2,1)S(1)}, bf16[2,192,384]{2,1,0:T(8,128)(2,1)S(1)}, u32[]{:S(2)}, u32[]{:S(2)}) collective-permute-start(bf16[2,192,384]{2,1,0:T(8,128)(2,1)S(1)} %pad_maximum_fusion.refs_0_), channel_id=1, source_target_pairs={{0,128},{128,0},{256,384},{384,256},{1,129},{129,1},{257,385},{385... | collective-permute-start | bytes 884744 | tf_op jit(solution)/shard_map/ppermute | solution.py:424
  89.3 31.6 %collective-permute-start.5 = (bf16[2,192,384]{2,1,0:T(8,128)(2,1)S(1)}, bf16[2,192,384]{2,1,0:T(8,128)(2,1)S(1)}, u32[]{:S(2)}, u32[]{:S(2)}) collective-permute-start(bf16[2,192,384]{2,1,0:T(8,128)(2,1)S(1)} %pad_maximum_fusion.refs_0_), channel_id=1, source_target_pairs={{0,256},{128,384},{256,0},{384,128},{1,257},{129,385},{257,1},{385... | collective-permute-start | bytes 884744 | tf_op jit(solution)/shard_map/ppermute | solution.py:424
  94.1 26.8 %collective-permute-start.6 = (bf16[2,192,384]{2,1,0:T(8,128)(2,1)S(1)}, bf16[2,192,384]{2,1,0:T(8,128)(2,1)S(1)}, u32[]{:S(2)}, u32[]{:S(2)}) collective-permute-start(bf16[2,192,384]{2,1,0:T(8,128)(2,1)S(1)} %pad_maximum_fusion.refs_0_), channel_id=1, source_target_pairs={{0,384},{128,256},{256,128},{384,0},{1,385},{129,257},{257,129},{3... | collective-permute-start | bytes 884744 | tf_op jit(solution)/shard_map/ppermute | solution.py:424
  105.5 5.9 %collective-permute-start.2 = (f32[2,640]{1,0:T(2,128)S(1)}, f32[2,640]{1,0:T(2,128)S(1)}, u32[]{:S(2)}, u32[]{:S(2)}) collective-permute-start(f32[2,640]{1,0:T(2,128)S(1)} %convert_reduce_fusion), channel_id=1, source_target_pairs={{0,1},{1,0},{2,3},{3,2},{4,5},{5,4},{6,7},{7,6},{8,9},{9,8},{10,11... | collective-permute-start | bytes 15368 | tf_op jit(solution)/shard_map/ppermute | solution.py:424
  113.7 21.8 %all-to-all-start.2 = ((f32[64,1,256]{2,1,0:T(1,128)}), f32[64,1,256]{2,1,0:T(1,128)S(1)}, u32[]{:S(2)}, u32[]{:S(2)}) async-start(f32[64,1,256]{2,1,0:T(1,128)} %get-tuple-element.25), calls=%async_computation.2 | async-start | bytes 131072 | tf_op jit(solution)/shard_map/all_to_all | solution.py:479
  120.9 0.7 copy-start.4
  120.9 0.8 copy-start.5
  121.7 0.7 copy-start.6

commit v5 on v4

--- a/solution.py
+++ b/solution.py
@@ -27,7 +27,7 @@
 ORIENTS = 8
 REST = SHARE + 2 * BLOCKS
 META = REST + 4 * BLOCKS - 2 * SHARE
-VMEM_LIMIT = 48 * 1024 * 1024
+VMEM_LIMIT = 16 * 1024 * 1024
 
 VM = pl.BlockSpec(memory_space=pltpu.VMEM)
 SM = pl.BlockSpec(memory_space=pltpu.SMEM)
@@ -38,11 +38,6 @@
 
 def bf(x):
     return np.asarray(x, np.float32).astype(jnp.bfloat16)
-
-
-def split(x):
-    high = bf(x)
-    return high, bf(np.asarray(x, np.float64) - high.astype(np.float64))
 
 
 def tables():
@@ -55,9 +50,7 @@
     for n in range(2):
         back[n, :, :HALF] = cosv[rows][:, n * HALF + order]
         back[n, :, HALF:] = -sinv[rows][:, n * HALF + order]
-    ch, cl = split(cosv)
-    sh, sl = split(sinv)
-    return bf(back), np.concatenate([ch, cl, sh, sl], 1)
+    return bf(back), bf(np.concatenate([cosv, sinv], 1))
 
 
 def stay(x):
@@ -183,33 +176,58 @@
     )(rot, count, *[stay(x) for x in (index, weight, table, spectrum, grid, orient, row, col)])
 
 
-def correlate(place, own, other, spectrum, filt, tabx, back):
-    def kernel(
-        at_ref, own_ref, other_ref, spec_hbm, filt_hbm, tabx_ref, back_ref, keep_ref, send_ref,
-        sl_s, spec_s, spec_ref, filt_ref, sems,
-    ):
-        copies = [
-            pltpu.make_async_copy(spec_hbm, spec_ref, sems.at[0]),
-            pltpu.make_async_copy(filt_hbm, filt_ref, sems.at[1]),
-        ]
+def arrange(spectrum, filt, tabx):
+    def kernel(spec_hbm, filt_hbm, tabx_hbm, out_ref, wide_ref, spec_ref, filt_ref, tabx_ref, spec_s, sems):
+        pairs = ((spec_hbm, spec_ref), (filt_hbm, filt_ref), (tabx_hbm, tabx_ref))
+        copies = [pltpu.make_async_copy(a, b, sems.at[i]) for i, (a, b) in enumerate(pairs)]
         for copy in copies:
             copy.start()
+        for copy in copies:
+            copy.wait()
+        for b in range(ROWS):
+            cols = slice(b * LANES, (b + 1) * LANES)
+            for c, value in enumerate((spec_ref[0, :, cols], spec_ref[1, :, cols], filt_ref[:, cols])):
+                spec_s[c * ROWS + b] = value.astype(F32)
+        for c in range(3):
+            for j in range(ROWS):
+                for b in range(ROWS):
+                    out_ref[c * BLOCKS + j * ROWS + b] = every(spec_s.at[c * ROWS + b], j, ROWS)
+        cosv, sinv = tabx_ref[:, :DFT], tabx_ref[:, DFT:]
+        wide_ref[:DFT, :DFT] = cosv
+        wide_ref[:DFT, DFT:] = sinv
+        wide_ref[DFT:, :DFT] = -sinv
+        wide_ref[DFT:, DFT:] = cosv
+
+    return pl.pallas_call(
+        kernel,
+        out_shape=(
+            jax.ShapeDtypeStruct((3 * BLOCKS, TILES, LANES), F32),
+            jax.ShapeDtypeStruct((2 * DFT, 2 * DFT), BF),
+        ),
+        in_specs=[HB] * 3,
+        out_specs=(VM, VM),
+        scratch_shapes=[pltpu.VMEM(x.shape, BF) for x in (spectrum, filt, tabx)]
+        + [pltpu.VMEM((3 * ROWS, HALF, LANES), F32), pltpu.SemaphoreType.DMA((3,))],
+        compiler_params=pltpu.CompilerParams(vmem_limit_bytes=VMEM_LIMIT),
+        name="arrange",
+    )(*[stay(x) for x in (spectrum, filt, tabx)])
+
+
+def correlate(place, own, other, blocks, wide, back):
+    def kernel(
+        at_ref, own_ref, other_ref, block_ref, wide_ref, back_hbm, keep_hbm, send_ref,
+        sl_s, back_ref, keep_ref, sems,
+    ):
+        fetch = pltpu.make_async_copy(back_hbm.at[at_ref[0]], back_ref, sems.at[2])
+        fetch.start()
+        leave = [pltpu.make_async_copy(keep_ref.at[o], keep_hbm.at[o], sems.at[o]) for o in range(2)]
         sl_s[at_ref[1]] = own_ref[...].astype(F32).reshape(TILES * SROWS, LANES)
         sl_s[1 - at_ref[1]] = other_ref[...].astype(F32).reshape(TILES * SROWS, LANES)
-        for copy in copies:
-            copy.wait()
-        for c in range(2):
-            for b in range(ROWS):
-                spec_s[c * ROWS + b] = spec_ref[c, :, b * LANES : (b + 1) * LANES].astype(F32)
-        for b in range(ROWS):
-            spec_s[2 * ROWS + b] = filt_ref[:, b * LANES : (b + 1) * LANES].astype(F32)
         real = [[None] * (ROWS * ROWS) for _ in range(2)]
         imag = [[None] * (ROWS * ROWS) for _ in range(2)]
         for j in range(ROWS):
             for b in range(ROWS):
-                mr = every(spec_s.at[b], j, ROWS)
-                mi = every(spec_s.at[ROWS + b], j, ROWS)
-                c = every(spec_s.at[2 * ROWS + b], j, ROWS)
+                mr, mi, c = [block_ref[k * BLOCKS + j * ROWS + b] for k in range(3)]
                 for o in range(2):
                     row = o * BLOCKS + j * ROWS + b
                     cr = c * every(sl_s.at[0], row, SROWS)
@@ -224,12 +242,9 @@
             ],
             axis=0,
         )
-        cosv, sinv = tabx_ref[:, :DFT], tabx_ref[:, 2 * DFT : 3 * DFT]
-        wide = jnp.concatenate(
-            [jnp.concatenate([cosv, sinv], axis=1), jnp.concatenate([-sinv, cosv], axis=1)], axis=0
-        )
-        halfimg = lax.dot_general(cross, wide, NN, preferred_element_type=F32).astype(BF)
-        table = back_ref[at_ref[0]]
+        halfimg = lax.dot_general(cross, wide_ref[...], NN, preferred_element_type=F32).astype(BF)
+        fetch.wait()
+        table = back_ref[...]
         low = at_ref[0] == 0
         for o in range(2):
             rows = halfimg[o * HALF : (o + 1) * HALF]
@@ -238,33 +253,35 @@
             left = jnp.concatenate([sums[:HALF, :HALF], sums[HALF:, :HALF]], axis=1)
             right = jnp.concatenate([sums[:HALF, HALF:], sums[HALF:, HALF:]], axis=1)
             keep_ref[o] = jnp.where(low, left, right).astype(BF)
+            leave[o].start()
             send_ref[o] = jnp.where(low, right, left).astype(BF)
+        for copy in leave:
+            copy.wait()
 
     shape = jax.ShapeDtypeStruct((2, HALF, DFT), BF)
     return pl.pallas_call(
         kernel,
         out_shape=(shape, shape),
-        in_specs=[SM, VM, VM, HB, HB, VM, VM],
-        out_specs=(VM, VM),
+        in_specs=[SM] + [VM] * 4 + [HB],
+        out_specs=(HB, VM),
         scratch_shapes=[
             pltpu.VMEM((2, TILES * SROWS, LANES), F32),
-            pltpu.VMEM((3 * ROWS, HALF, LANES), F32),
-            pltpu.VMEM(spectrum.shape, BF),
-            pltpu.VMEM(filt.shape, BF),
-            pltpu.SemaphoreType.DMA((2,)),
+            pltpu.VMEM((DFT, DFT), BF),
+            pltpu.VMEM((2, HALF, DFT), BF),
+            pltpu.SemaphoreType.DMA((3,)),
         ],
         compiler_params=pltpu.CompilerParams(vmem_limit_bytes=VMEM_LIMIT),
         name="correlate",
-    )(place, own, other, stay(spectrum), stay(filt), tabx, back)
-
-
-def score(rot, got, share, slices, tabx, taby):
+    )(place, own, other, blocks, wide, stay(back))
+
+
+def score(place, got, share, slices, tabx):
     def kernel(
-        rot_ref, got_ref, share_ref, slice_ref, tabx_ref, taby_ref,
+        at_ref, got_ref, share_ref, slice_ref, tabx_ref,
         out_ref, place_hbm, got_s, share_s, place_s, place_ref, sem, out_s,
     ):
         got_s[...] = got_ref[...].astype(F32).reshape(got_s.shape)
-        side = rot_ref[0] & 1
+        side = at_ref[2] & 1
         share_s[1 - side] = share_ref[...].astype(F32).reshape(TILES * SHARE, LANES)
         for r in range(SHARE):
             share_s[side, pl.ds(r, TILES, stride=SHARE), :] = every(got_s, r, XROWS)
@@ -300,14 +317,17 @@
         hot_y = jnp.concatenate(hot_y, axis=0)
         place = jnp.concatenate(place, axis=0)
         wave = lax.dot_general(hot_x, tabx_ref[...], NN, preferred_element_type=F32)
-        cx = wave[:, :DFT] + wave[:, DFT : 2 * DFT]
-        sx = wave[:, 2 * DFT : 3 * DFT] + wave[:, 3 * DFT :]
-        tilt = lax.dot_general(hot_y, taby_ref[...], NT, preferred_element_type=F32)
+        cx, sx = wave[:, :DFT], wave[:, DFT:]
+        line = lax.broadcasted_iota(I32, (16, DFT), 0) + at_ref[3]
+        pick = jnp.where(lax.broadcasted_iota(I32, (16, DFT), 1) == line, 1.0, 0.0).astype(BF)
+        taby = lax.dot_general(pick, tabx_ref[...], NN, preferred_element_type=F32).astype(BF)
+        tilt_c = lax.dot_general(hot_y, taby[:, :DFT], NT, preferred_element_type=F32)
+        tilt_s = lax.dot_general(hot_y, taby[:, DFT:], NT, preferred_element_type=F32)
         pieces = [[] for _ in range(SLOTS)]
         second = [jnp.broadcast_to(meta[:, 5 * i : 5 * i + 1], (TILES, LANES)) > 0.5 for i in range(SLOTS)]
         for j in range(ROWS):
-            cosines = jnp.broadcast_to(tilt[:, j : j + 1] + tilt[:, 3 + j : 4 + j], (SLOTS * TILES, LANES))
-            sines = jnp.broadcast_to(tilt[:, 6 + j : 7 + j] + tilt[:, 9 + j : 10 + j], (SLOTS * TILES, LANES))
+            cosines = jnp.broadcast_to(tilt_c[:, j : j + 1], (SLOTS * TILES, LANES))
+            sines = jnp.broadcast_to(tilt_s[:, j : j + 1], (SLOTS * TILES, LANES))
             for b in range(ROWS):
                 r = j * ROWS + b
                 cols = slice(b * LANES, (b + 1) * LANES)
@@ -326,12 +346,9 @@
                     wx, vx = cx[at, cols], sx[at, cols]
                     pieces[i].append(cy * (pr * wx - pi * vx) - sy * (pr * vx + pi * wx))
         shifted = jnp.concatenate([jnp.concatenate(p, axis=1) for p in pieces], axis=0)
-        high = shifted.astype(BF)
         bin_of = lax.shift_right_logical(lax.broadcasted_iota(I32, (WIDE, DFT), 0), 2)
         group = jnp.where(bin_of == lax.broadcasted_iota(I32, (WIDE, DFT), 1), 1.0, 0.0).astype(BF)
-        low = (shifted - high.astype(F32)).astype(BF)
-        binned = lax.dot_general(high, group, NN, preferred_element_type=F32)
-        binned = binned + lax.dot_general(low, group, NN, preferred_element_type=F32)
+        binned = lax.dot_general(shifted.astype(BF), group, NN, preferred_element_type=F32)
         binned = binned.astype(BF)[:, :BINS]
         grid = jnp.concatenate([sent(2 * BLOCKS + r).astype(BF) for r in range(2 * BLOCKS)], axis=1)
         values = jnp.concatenate([grid[:, q * BINS : (q + 1) * BINS] for q in range(GRID)], axis=0)
@@ -354,21 +371,22 @@
             jax.ShapeDtypeStruct((TILES, 2, SPAN * LANES), BF),
             jax.ShapeDtypeStruct((2, SLOTS * TILES, LANES), BF),
         ),
-        in_specs=[SM] + [VM] * 5,
+        in_specs=[SM] + [VM] * 4,
         out_specs=(VM, HB),
         scratch_shapes=[pltpu.VMEM((TILES * XROWS, LANES), F32), pltpu.VMEM((2, TILES * SHARE, LANES), F32), pltpu.VMEM((2, SLOTS * TILES, LANES), F32), pltpu.VMEM((2, SLOTS * TILES, LANES), BF), pltpu.SemaphoreType.DMA, pltpu.VMEM((TILES, 2, SPAN * LANES), F32)],
         compiler_params=pltpu.CompilerParams(vmem_limit_bytes=VMEM_LIMIT),
         cost_estimate=pl.CostEstimate(flops=6_000_000_000, transcendentals=0, bytes_accessed=8_000_000),
         name="score",
-    )(rot, got, share, slices, tabx, taby)
-
-
-def expand(place, sums):
-    def kernel(place_ref, sum_ref, refined_ref, top_ref):
+    )(place, got, share, slices, tabx)
+
+
+def expand(place, mine, other):
+    def kernel(place_ref, mine_ref, other_ref, refined_ref, top_ref):
+        both = mine_ref[...] + other_ref[...]
         place = jnp.concatenate([place_ref[0], place_ref[1]], axis=1)
         lane = lax.broadcasted_iota(I32, (GRID, LANES), 1)
         row = lax.broadcasted_iota(I32, (GRID, LANES), 0)
-        sums = [sum_ref[r // SPAN : r // SPAN + 1, r % SPAN * LANES : (r % SPAN + 1) * LANES] for r in range(GRID + 1)]
+        sums = [both[r // SPAN : r // SPAN + 1, r % SPAN * LANES : (r % SPAN + 1) * LANES] for r in range(GRID + 1)]
         last = jnp.broadcast_to(sums[GRID], (GRID, LANES))
         last = jnp.sum(jnp.where(lane == row, last, 0.0), axis=1, keepdims=True)
         rest = jnp.concatenate([jnp.concatenate(sums[:GRID], axis=0), jnp.where(lane == 0, last, 0.0)], axis=1) * (1.0 / DFT)
@@ -389,10 +407,11 @@
             jax.ShapeDtypeStruct((GRID, SLOTS * TILES), F32),
             jax.ShapeDtypeStruct((TILES, 1, SLOTS * TILES), F32),
         ),
-        in_specs=[VM] * 2,
+        in_specs=[VM] * 3,
         out_specs=(VM, VM),
+        compiler_params=pltpu.CompilerParams(vmem_limit_bytes=VMEM_LIMIT),
         name="expand",
-    )(place, sums)
+    )(place, mine, other)
 
 
 def finish(parts):
@@ -415,6 +434,7 @@
         in_specs=[VM] * 4,
         out_specs=(VM, VM),
         cost_estimate=pl.CostEstimate(flops=1, transcendentals=0, bytes_accessed=1),
+        compiler_params=pltpu.CompilerParams(vmem_limit_bytes=VMEM_LIMIT),
         name="finish",
     )(*parts)
 
@@ -439,10 +459,6 @@
     back, tabx = [jnp.asarray(t) for t in tables()]
     nar = lax.axis_index("nar")
     tile = lax.axis_index("tile")
-
-    taby = lax.dynamic_slice_in_dim(tabx, (nar * TILES + tile) * ROWS, ROWS, 0)
-    taby = taby.reshape(ROWS, 4, DFT).transpose(1, 0, 2).reshape(4 * ROWS, DFT)
-    taby = jnp.pad(taby, ((0, 16 - 4 * ROWS), (0, 0)))
 
     grid = ctf_grid.reshape(GRID, TILES * BINS)
     spec = spectrum.reshape(2, HALF, DFT)
@@ -460,13 +476,17 @@
         peak_col,
         peak_count,
     )
+    slices, nar, tile = lax.optimization_barrier((slices, nar, tile))
+    place_at = jnp.stack([nar, tile % 2, rot[0], (nar * TILES + tile) * ROWS])
+    rows, wide = arrange(spec, filt, tabx)
     got = lax.all_to_all(blocks, "tile", 0, 0, tiled=True)
+    got, rows, wide, place_at = lax.optimization_barrier((got, rows, wide, place_at))
     share, mine = exchange(got[:, :SHARE], "rot", 1), got[:, SHARE:]
     other = exchange(mine, "tile", 1)
-    keep, send = correlate(jnp.stack([nar, tile % 2]), mine, other, spec, filt, tabx, back)
+    keep, send = correlate(place_at, mine, other, rows, wide, back)
     got, send = lax.optimization_barrier((got, send))
     extra_rows = exchange(send, "nar", 1)
-    packed, place = score(rot, got, share, slices, tabx, taby)
+    packed, place = score(place_at, got, share, slices, tabx)
     sums = lax.all_to_all(packed, "tile", 0, 0, tiled=True)
 
     corr = (keep.astype(F32) + extra_rows.astype(F32)) * (1.0 / DFT)
@@ -474,8 +494,7 @@
     others = [exchange(stats, "rot", bit) for bit in (1, 2, 3)]
 
     sums = jnp.sum(sums.astype(F32), axis=0)
-    sums = sums + exchange(sums, "nar", 1)
-    refined, tops = expand(place, sums)
+    refined, tops = expand(place, sums, exchange(sums, "nar", 1))
     tops = lax.all_to_all(tops, "tile", 0, 0)
     peak, mean = finish([stats] + others)
     tops, peak, mean = lax.optimization_barrier((tops, peak, mean))

time: 137 us -> 134 us (0.978)
  blocking collectives: 54 us -> 0 us
  waiting for transfers between devices: 22.2 us -> 59.3 us
  starting transfers between devices: 36.9 us -> 55.3 us
  local copies, waits for them, and re-layouts: 2.32 us -> 0.07 us
    all_to_all x1 -> x0, blocking collectives: 54 us -> none  [shards(): got = lax.all_to_all(blocks, 'tile', 0, 0, tiled=True)]
    all_to_all x0 -> x1, waiting for transfers between devices: none -> 34.5 us  [shards(): got = lax.all_to_all(blocks, 'tile', 0, 0, tiled=True)]
    all_to_all x0 -> x1, starting transfers between devices: none -> 18.1 us  [shards(): got = lax.all_to_all(blocks, 'tile', 0, 0, tiled=True)]
    all_to_all x1, waiting for transfers between devices: 10.9 us -> 13.6 us  [shards(): tops = lax.all_to_all(tops, 'tile', 0, 0)]
    unnamed x14 -> x2, local copies, waits for them, and re-layouts: 1.5 us -> 0.01 us
    pallas_call x1 -> x2, Pallas kernels: 3.94 us -> 5.11 us  [the longest x1 3.63 us: correlate(): pl.pallas_call(kernel, out_shape=(shape, shape), in_specs=[SM] + [VM] * 4...]
  transfers between devices with their start and end apart: 9 -> 10, of which waited for: 3 -> 4; matrix products, arithmetic and copies ran while one was open for 1% -> 0% of each run, Pallas kernels for 10% -> 8%
where the time goes in v5:
time: 134 us
  waiting for transfers between devices  59.3 us (44%)
  starting transfers between devices  55.3 us (41%)
  Pallas kernels  16.3 us (12%)
  between operations  1.52 us (1%)
    all_to_all x1, waiting for transfers between devices, shards(): got = lax.all_to_all(blocks, 'tile', 0, 0, tiled=True)  34.5 us
    ppermute x7, starting transfers between devices, exchange(): return lax.ppermute(x, axis, [(k, k ^ bit) for k in range(size)])  22.3 us
    all_to_all x1, starting transfers between devices, shards(): got = lax.all_to_all(blocks, 'tile', 0, 0, tiled=True)  18.1 us
    all_to_all x1, waiting for transfers between devices, shards(): tops = lax.all_to_all(tops, 'tile', 0, 0)  13.6 us
    all_to_all x1, waiting for transfers between devices, shards(): sums = lax.all_to_all(packed, 'tile', 0, 0, tiled=True)  8.52 us
    all_to_all x1, starting transfers between devices, shards(): sums = lax.all_to_all(packed, 'tile', 0, 0, tiled=True)  7.68 us
    all_to_all x1, starting transfers between devices, shards(): tops = lax.all_to_all(tops, 'tile', 0, 0)  7.16 us
    pallas_call x1, Pallas kernels, prepare(): pl.pallas_call(kernel, out_shape=(jax.ShapeDtypeStruct((TILES, XROWS, LAN...  5.04 us
  transfers between devices with their start and end apart: 10, of which 4 were waited for; matrix products, arithmetic and copies ran while one was open for 0% of the time, Pallas kernels for 8%

profile of v5, /device:TPU:1, one launch (start us, length us, event | category | flops | bytes accessed | tf_op | source)
XLA Modules:
  0.0 133.6 jit_solution(279252584209808696)
XLA Ops:
  1.3 5.0 %prepare.1 = (bf16[64,40,128]{2,1,0:T(8,128)(2,1)}, f32[2,18,128]{2,1,0:T(8,128)S(1)}) custom-call(s32[1]{0:T(128)} %bitcast.rot_ref, s32[1,1]{1,0:T(1,128)S(6)} %copy.16.count_ref, s32[144,128]{1,0:T(8,128)} %bitcast.20, bf16[8,1,3,2,384]{4,3,2,1,0:T(2,128)(2,1)} %bitcast.21, bf16[2,4096]{1,0:T(2,128)(2,1)} %bitcast.22, bf16[2,192,384]{2,1,0:T(8,128)(2,1)} %bitcast.16, ...), custom_call_target="tpu_custom_call" | custom-call | tf_op jit(solution)/shard_map/prepare/pallas_call | solution.py:154
  6.3 18.1 %all-to-all-start = ((bf16[64,40,128]{2,1,0:T(8,128)(2,1)}), bf16[64,40,128]{2,1,0:T(8,128)(2,1)S(1)}, u32[]{:S(2)}, u32[]{:S(2)}) async-start(bf16[64,40,128]{2,1,0:T(8,128)(2,1)} %get-tuple-element.28), calls=%async_computation | async-start | bytes 1310720 | tf_op jit(solution)/shard_map/all_to_all | solution.py:482
  24.4 1.5 %arrange.1 = (f32[27,64,128]{2,1,0:T(8,128)S(1)}, bf16[768,768]{1,0:T(8,128)(2,1)S(1)}) custom-call(bf16[2,192,384]{2,1,0:T(8,128)(2,1)} %bitcast.17, bf16[192,384]{1,0:T(8,128)(2,1)} %bitcast.19, bf16[384,768]{1,0:T(8,128)(2,1)} %constant.42.clone.tabx_hbm.tabx_ref), custom_call_target="tpu_custom_call" | custom-call | tf_op jit(solution)/shard_map/arrange/pallas_call | solution.py:201
  25.9 0.1 pad_add_fusion.at_ref
  26.0 34.5 %all-to-all-done.got_ref = bf16[64,40,128]{2,1,0:T(8,128)(2,1)S(1)} async-done(((bf16[64,40,128]{2,1,0:T(8,128)(2,1)}), bf16[64,40,128]{2,1,0:T(8,128)(2,1)S(1)}, u32[]{:S(2)}, u32[]{:S(2)}) %all-to-all-start) | async-done | bytes 655392 | tf_op jit(solution)/shard_map/all_to_all | solution.py:482
  60.5 1.9 %collective-permute-start = (bf16[64,24,128]{2,1,0:T(8,128)(2,1)S(1)}, bf16[64,24,128]{2,1,0:T(8,128)(2,1)S(1)}, u32[]{:S(2)}, u32[]{:S(2)}) collective-permute-start(bf16[64,24,128]{2,1,0:T(8,128)(2,1)S(1)} %slice.14.own_ref), channel_id=1, source_target_pairs={{0,2},{2,0},{4,6},{6,4},{8,10},{10,8},{12,14},{14,12},{16,18},{18,... | collective-permute-start | bytes 1179656 | tf_op jit(solution)/shard_map/ppermute | solution.py:444
  62.5 0.0 copy-start
  62.5 3.3 %collective-permute-start.1 = (bf16[64,16,128]{2,1,0:T(8,128)(2,1)S(1)}, bf16[64,16,128]{2,1,0:T(8,128)(2,1)S(1)}, u32[]{:S(2)}, u32[]{:S(2)}) collective-permute-start(bf16[64,16,128]{2,1,0:T(8,128)(2,1)S(1)} %slice.15), channel_id=1, source_target_pairs={{0,128},{128,0},{256,384},{384,256},{1,129},{129,1},{257,385},{385... | collective-permute-start | bytes 786440 | tf_op jit(solution)/shard_map/ppermute | solution.py:444
  65.8 0.0 collective-permute-done.other_ref
  65.8 3.6 %correlate.1 = (bf16[2,192,384]{2,1,0:T(8,128)(2,1)S(1)}, bf16[2,192,384]{2,1,0:T(8,128)(2,1)S(1)}) custom-call(s32[4]{0:T(128)S(1)} %pad_add_fusion.at_ref, bf16[64,24,128]{2,1,0:T(8,128)(2,1)S(1)} %slice.14.own_ref, bf16[64,24,128]{2,1,0:T(8,128)(2,1)S(1)} %collective-permute-done.other_ref, f32[27,64,128]{2,1,0:T(8,128)S(1)} %get-tuple-element.36.block_ref, ...), custom_call_target="tpu_custom_call" | custom-call | tf_op jit(solution)/shard_map/correlate/pallas_call | solution.py:262
  69.5 4.4 %collective-permute-start.3 = (bf16[2,192,384]{2,1,0:T(8,128)(2,1)S(1)}, bf16[2,192,384]{2,1,0:T(8,128)(2,1)S(1)}, u32[]{:S(2)}, u32[]{:S(2)}) collective-permute-start(bf16[2,192,384]{2,1,0:T(8,128)(2,1)S(1)} %get-tuple-element.45), channel_id=1, source_target_pairs={{0,1},{1,0},{2,3},{3,2},{4,5},{5,4},{6,7},{7,6},{8,9},{9,8},{10,11... | collective-permute-start | bytes 884744 | tf_op jit(solution)/shard_map/ppermute | solution.py:444
  73.8 0.0 collective-permute-done.1.share_ref
  73.8 0.0 copy-done
  73.8 4.4 %score.1 = (bf16[64,2,640]{2,1,0:T(2,128)(2,1)}, bf16[2,256,128]{2,1,0:T(8,128)(2,1)S(1)}) custom-call(s32[4]{0:T(128)S(1)} %pad_add_fusion.at_ref, bf16[64,40,128]{2,1,0:T(8,128)(2,1)S(1)} %all-to-all-done.got_ref, bf16[64,16,128]{2,1,0:T(8,128)(2,1)S(1)} %collective-permute-done.1.share_ref, f32[2,18,128]{2,1,0:T(8,128)S(1)} %get-tuple-element.40.slice_ref, ...), custom_call_target="tpu_custom_call" | custom-call | flops 6000000000 | bytes 8000000 | tf_op jit(solution)/shard_map/score/pallas_call | solution.py:368
  78.3 7.7 %all-to-all-start.1 = ((bf16[64,2,640]{2,1,0:T(2,128)(2,1)}), bf16[64,2,640]{2,1,0:T(2,128)(2,1)S(1)}, u32[]{:S(2)}, u32[]{:S(2)}) async-start(bf16[64,2,640]{2,1,0:T(2,128)(2,1)} %get-tuple-element.42), calls=%async_computation.1 | async-start | bytes 327680 | tf_op jit(solution)/shard_map/all_to_all | solution.py:490
  86.0 0.0 collective-permute-done.3
  86.0 0.1 add_multiply_fusion
  86.2 2.1 %collective-permute-start.4 = (bf16[2,192,384]{2,1,0:T(8,128)(2,1)S(1)}, bf16[2,192,384]{2,1,0:T(8,128)(2,1)S(1)}, u32[]{:S(2)}, u32[]{:S(2)}) collective-permute-start(bf16[2,192,384]{2,1,0:T(8,128)(2,1)S(1)} %pad_maximum_fusion.refs_0_), channel_id=1, source_target_pairs={{0,128},{128,0},{256,384},{384,256},{1,129},{129,1},{257,385},{385... | collective-permute-start | bytes 884744 | tf_op jit(solution)/shard_map/ppermute | solution.py:444
  88.3 4.8 %collective-permute-start.5 = (bf16[2,192,384]{2,1,0:T(8,128)(2,1)S(1)}, bf16[2,192,384]{2,1,0:T(8,128)(2,1)S(1)}, u32[]{:S(2)}, u32[]{:S(2)}) collective-permute-start(bf16[2,192,384]{2,1,0:T(8,128)(2,1)S(1)} %pad_maximum_fusion.refs_0_), channel_id=1, source_target_pairs={{0,256},{128,384},{256,0},{384,128},{1,257},{129,385},{257,1},{385... | collective-permute-start | bytes 884744 | tf_op jit(solution)/shard_map/ppermute | solution.py:444
  93.1 2.7 %collective-permute-start.6 = (bf16[2,192,384]{2,1,0:T(8,128)(2,1)S(1)}, bf16[2,192,384]{2,1,0:T(8,128)(2,1)S(1)}, u32[]{:S(2)}, u32[]{:S(2)}) collective-permute-start(bf16[2,192,384]{2,1,0:T(8,128)(2,1)S(1)} %pad_maximum_fusion.refs_0_), channel_id=1, source_target_pairs={{0,384},{128,256},{256,128},{384,0},{1,385},{129,257},{257,129},{3... | collective-permute-start | bytes 884744 | tf_op jit(solution)/shard_map/ppermute | solution.py:444
  95.8 8.5 %all-to-all-done.1 = bf16[64,2,640]{2,1,0:T(2,128)(2,1)S(1)} async-done(((bf16[64,2,640]{2,1,0:T(2,128)(2,1)}), bf16[64,2,640]{2,1,0:T(2,128)(2,1)S(1)}, u32[]{:S(2)}, u32[]{:S(2)}) %all-to-all-start.1) | async-done | bytes 163872 | tf_op jit(solution)/shard_map/all_to_all | solution.py:490
  104.3 0.2 convert_reduce_fusion.mine_ref
  104.5 3.1 %collective-permute-start.2 = (f32[2,640]{1,0:T(2,128)S(1)}, f32[2,640]{1,0:T(2,128)S(1)}, u32[]{:S(2)}, u32[]{:S(2)}) collective-permute-start(f32[2,640]{1,0:T(2,128)S(1)} %convert_reduce_fusion.mine_ref), channel_id=1, source_target_pairs={{0,1},{1,0},{2,3},{3,2},{4,5},{5,4},{6,7},{7,6},{8,9},{9,8},{10,11... | collective-permute-start | bytes 15368 | tf_op jit(solution)/shard_map/ppermute | solution.py:444
  107.6 2.7 %collective-permute-done.2.other_ref = f32[2,640]{1,0:T(2,128)S(1)} collective-permute-done((f32[2,640]{1,0:T(2,128)S(1)}, f32[2,640]{1,0:T(2,128)S(1)}, u32[]{:S(2)}, u32[]{:S(2)}) %collective-permute-start.2) | collective-permute-done | bytes 5152 | tf_op jit(solution)/shard_map/ppermute | solution.py:444
  110.3 0.8 expand.1
  111.2 7.2 %all-to-all-start.2 = ((f32[64,1,256]{2,1,0:T(1,128)}), f32[64,1,256]{2,1,0:T(1,128)S(1)}, u32[]{:S(2)}, u32[]{:S(2)}) async-start(f32[64,1,256]{2,1,0:T(1,128)} %get-tuple-element.43), calls=%async_computation.2 | async-start | bytes 131072 | tf_op jit(solution)/shard_map/all_to_all | solution.py:498
  118.3 0.0 collective-permute-done.4.refs_1_
  118.4 0.0 collective-permute-done.5.refs_2_
  118.4 0.0 collective-permute-done.6.refs_3_
  118.4 0.9 finish.1
  119.3 13.6 %all-to-all-done.2 = f32[64,1,256]{2,1,0:T(1,128)S(1)} async-done(((f32[64,1,256]{2,1,0:T(1,128)}), f32[64,1,256]{2,1,0:T(1,128)S(1)}, u32[]{:S(2)}, u32[]{:S(2)}) %all-to-all-start.2) | async-done | bytes 65568 | tf_op jit(solution)/shard_map/all_to_all | solution.py:498
  132.9 0.7 reduce_max.11
  (5 shorter events, 0.2 us)
Async XLA Ops:
  6.3 54.1 %all-to-all-start = ((bf16[64,40,128]{2,1,0:T(8,128)(2,1)}), bf16[64,40,128]{2,1,0:T(8,128)(2,1)S(1)}, u32[]{:S(2)}, u32[]{:S(2)}) async-start(bf16[64,40,128]{2,1,0:T(8,128)(2,1)} %get-tuple-element.28), calls=%async_computation | async-start | bytes 1310720 | tf_op jit(solution)/shard_map/all_to_all | solution.py:482
  60.5 5.3 %collective-permute-start = (bf16[64,24,128]{2,1,0:T(8,128)(2,1)S(1)}, bf16[64,24,128]{2,1,0:T(8,128)(2,1)S(1)}, u32[]{:S(2)}, u32[]{:S(2)}) collective-permute-start(bf16[64,24,128]{2,1,0:T(8,128)(2,1)S(1)} %slice.14.own_ref), channel_id=1, source_target_pairs={{0,2},{2,0},{4,6},{6,4},{8,10},{10,8},{12,14},{14,12},{16,18},{18,... | collective-permute-start | bytes 1179656 | tf_op jit(solution)/shard_map/ppermute | solution.py:444
  62.5 11.4 %copy-start = (bf16[384,768]{1,0:T(8,128)(2,1)S(1)}, bf16[384,768]{1,0:T(8,128)(2,1)}, u32[]{:S(2)}) copy-start(bf16[384,768]{1,0:T(8,128)(2,1)} %constant.42.clone.tabx_hbm.tabx_ref) | copy-start | bytes 1769476
  62.5 11.4 %collective-permute-start.1 = (bf16[64,16,128]{2,1,0:T(8,128)(2,1)S(1)}, bf16[64,16,128]{2,1,0:T(8,128)(2,1)S(1)}, u32[]{:S(2)}, u32[]{:S(2)}) collective-permute-start(bf16[64,16,128]{2,1,0:T(8,128)(2,1)S(1)} %slice.15), channel_id=1, source_target_pairs={{0,128},{128,0},{256,384},{384,256},{1,129},{129,1},{257,385},{385... | collective-permute-start | bytes 786440 | tf_op jit(solution)/shard_map/ppermute | solution.py:444
  69.5 16.5 %collective-permute-start.3 = (bf16[2,192,384]{2,1,0:T(8,128)(2,1)S(1)}, bf16[2,192,384]{2,1,0:T(8,128)(2,1)S(1)}, u32[]{:S(2)}, u32[]{:S(2)}) collective-permute-start(bf16[2,192,384]{2,1,0:T(8,128)(2,1)S(1)} %get-tuple-element.45), channel_id=1, source_target_pairs={{0,1},{1,0},{2,3},{3,2},{4,5},{5,4},{6,7},{7,6},{8,9},{9,8},{10,11... | collective-permute-start | bytes 884744 | tf_op jit(solution)/shard_map/ppermute | solution.py:444
  78.3 26.0 %all-to-all-start.1 = ((bf16[64,2,640]{2,1,0:T(2,128)(2,1)}), bf16[64,2,640]{2,1,0:T(2,128)(2,1)S(1)}, u32[]{:S(2)}, u32[]{:S(2)}) async-start(bf16[64,2,640]{2,1,0:T(2,128)(2,1)} %get-tuple-element.42), calls=%async_computation.1 | async-start | bytes 327680 | tf_op jit(solution)/shard_map/all_to_all | solution.py:490
  86.2 32.2 %collective-permute-start.4 = (bf16[2,192,384]{2,1,0:T(8,128)(2,1)S(1)}, bf16[2,192,384]{2,1,0:T(8,128)(2,1)S(1)}, u32[]{:S(2)}, u32[]{:S(2)}) collective-permute-start(bf16[2,192,384]{2,1,0:T(8,128)(2,1)S(1)} %pad_maximum_fusion.refs_0_), channel_id=1, source_target_pairs={{0,128},{128,0},{256,384},{384,256},{1,129},{129,1},{257,385},{385... | collective-permute-start | bytes 884744 | tf_op jit(solution)/shard_map/ppermute | solution.py:444
  88.3 30.1 %collective-permute-start.5 = (bf16[2,192,384]{2,1,0:T(8,128)(2,1)S(1)}, bf16[2,192,384]{2,1,0:T(8,128)(2,1)S(1)}, u32[]{:S(2)}, u32[]{:S(2)}) collective-permute-start(bf16[2,192,384]{2,1,0:T(8,128)(2,1)S(1)} %pad_maximum_fusion.refs_0_), channel_id=1, source_target_pairs={{0,256},{128,384},{256,0},{384,128},{1,257},{129,385},{257,1},{385... | collective-permute-start | bytes 884744 | tf_op jit(solution)/shard_map/ppermute | solution.py:444
  93.1 25.3 %collective-permute-start.6 = (bf16[2,192,384]{2,1,0:T(8,128)(2,1)S(1)}, bf16[2,192,384]{2,1,0:T(8,128)(2,1)S(1)}, u32[]{:S(2)}, u32[]{:S(2)}) collective-permute-start(bf16[2,192,384]{2,1,0:T(8,128)(2,1)S(1)} %pad_maximum_fusion.refs_0_), channel_id=1, source_target_pairs={{0,384},{128,256},{256,128},{384,0},{1,385},{129,257},{257,129},{3... | collective-permute-start | bytes 884744 | tf_op jit(solution)/shard_map/ppermute | solution.py:444
  104.5 5.9 %collective-permute-start.2 = (f32[2,640]{1,0:T(2,128)S(1)}, f32[2,640]{1,0:T(2,128)S(1)}, u32[]{:S(2)}, u32[]{:S(2)}) collective-permute-start(f32[2,640]{1,0:T(2,128)S(1)} %convert_reduce_fusion.mine_ref), channel_id=1, source_target_pairs={{0,1},{1,0},{2,3},{3,2},{4,5},{5,4},{6,7},{7,6},{8,9},{9,8},{10,11... | collective-permute-start | bytes 15368 | tf_op jit(solution)/shard_map/ppermute | solution.py:444
  111.2 21.8 %all-to-all-start.2 = ((f32[64,1,256]{2,1,0:T(1,128)}), f32[64,1,256]{2,1,0:T(1,128)S(1)}, u32[]{:S(2)}, u32[]{:S(2)}) async-start(f32[64,1,256]{2,1,0:T(1,128)} %get-tuple-element.43), calls=%async_computation.2 | async-start | bytes 131072 | tf_op jit(solution)/shard_map/all_to_all | solution.py:498

commit v6 on v5

--- a/solution.py
+++ b/solution.py
@@ -65,8 +65,8 @@
     def kernel(
         rot_ref, count_ref, *refs,
     ):
-        sources, (out_ref, own_ref), scratch = refs[:8], refs[8:10], refs[10:]
-        targets, (sems, table_s, weight_s, value_s, spec_s, grid_s, all_s, out_s) = scratch[:8], scratch[8:]
+        sources, (out_hbm, own_ref), scratch = refs[:8], refs[8:10], refs[10:]
+        targets, (sems, table_s, weight_s, value_s, spec_s, grid_s, all_s, out_s, out_ref) = scratch[:8], scratch[8:]
         copies = [pltpu.make_async_copy(a, b, sems.at[i]) for i, (a, b) in enumerate(zip(sources, targets))]
         for copy in copies:
             copy.start()
@@ -102,7 +102,7 @@
                 value_s[c, rows, :] = pick(c, 4, 0) * weight_s[rows, :]
             return carry
 
-        lax.fori_loop(0, 2 * BLOCKS, step, 0)
+        lax.fori_loop(0, 2 * BLOCKS, step, 0, unroll=3)
         for c in range(2):
             total = value_s[c, 0 : 2 * BLOCKS, :]
             for k in range(1, 8):
@@ -149,7 +149,16 @@
         fields = jnp.broadcast_to(fields.astype(F32), (TILES, LANES))
         for r in range(META, XROWS):
             out_s[pl.ds(r, TILES, stride=XROWS), :] = fields
-        out_ref[...] = out_s[...].astype(BF).reshape(out_ref.shape)
+        piece = TILES // 4
+        leave = []
+        for k in range(4):
+            rows = out_s[k * piece * XROWS : (k + 1) * piece * XROWS, :]
+            out_ref[k * piece : (k + 1) * piece] = rows.astype(BF).reshape(piece, XROWS, LANES)
+            at = pl.ds(k * piece, piece)
+            leave.append(pltpu.make_async_copy(out_ref.at[at], out_hbm.at[at], sems.at[8 + k]))
+            leave[-1].start()
+        for copy in leave:
+            copy.wait()
 
     return pl.pallas_call(
         kernel,
@@ -158,11 +167,11 @@
             jax.ShapeDtypeStruct((2, 2 * BLOCKS, LANES), F32),
         ),
         in_specs=[SM, SM] + [HB] * 8,
-        out_specs=(VM, VM),
+        out_specs=(HB, VM),
         scratch_shapes=[pltpu.VMEM(x.shape, x.dtype) for x in (index, weight, table, spectrum, grid)]
         + [pltpu.SMEM(x.shape, x.dtype) for x in (orient, row, col)]
         + [
-            pltpu.SemaphoreType.DMA((8,)),
+            pltpu.SemaphoreType.DMA((12,)),
             pltpu.VMEM(table.shape, F32),
             pltpu.VMEM(index.shape, F32),
             pltpu.VMEM((2,) + index.shape, F32),
@@ -170,6 +179,7 @@
             pltpu.VMEM((GRID * TILES * BINS // LANES, LANES), F32),
             pltpu.VMEM((4 * BLOCKS, TILES, LANES), F32),
             pltpu.VMEM((TILES * XROWS, LANES), F32),
+            pltpu.VMEM((TILES, XROWS, LANES), BF),
         ],
         compiler_params=pltpu.CompilerParams(vmem_limit_bytes=VMEM_LIMIT),
         name="prepare",

time: 134 us -> 133 us (level)
  transfers between devices with their start and end apart: 10 -> 10, of which waited for: 4 -> 4; matrix products, arithmetic and copies ran while one was open for 0% -> 0% of each run, Pallas kernels for 8% -> 9%
where the time goes in v6:
time: 133 us
  waiting for transfers between devices  59.3 us (45%)
  starting transfers between devices  55.3 us (42%)
  Pallas kernels  15.4 us (12%)
  between operations  1.52 us (1%)
    all_to_all x1, waiting for transfers between devices, shards(): got = lax.all_to_all(blocks, 'tile', 0, 0, tiled=True)  34.5 us
    ppermute x7, starting transfers between devices, exchange(): return lax.ppermute(x, axis, [(k, k ^ bit) for k in range(size)])  22.4 us
    all_to_all x1, starting transfers between devices, shards(): got = lax.all_to_all(blocks, 'tile', 0, 0, tiled=True)  18.1 us
    all_to_all x1, waiting for transfers between devices, shards(): tops = lax.all_to_all(tops, 'tile', 0, 0)  13.6 us
    all_to_all x1, waiting for transfers between devices, shards(): sums = lax.all_to_all(packed, 'tile', 0, 0, tiled=True)  8.52 us
    all_to_all x1, starting transfers between devices, shards(): sums = lax.all_to_all(packed, 'tile', 0, 0, tiled=True)  7.68 us
    all_to_all x1, starting transfers between devices, shards(): tops = lax.all_to_all(tops, 'tile', 0, 0)  7.16 us
    pallas_call x1, Pallas kernels, score(): pl.pallas_call(kernel, out_shape=(jax.ShapeDtypeStruct((TILES, 2, SPAN *...  4.41 us
  transfers between devices with their start and end apart: 10, of which 4 were waited for; matrix products, arithmetic and copies ran while one was open for 0% of the time, Pallas kernels for 9%

profile of v6, /device:TPU:1, one launch (start us, length us, event | category | flops | bytes accessed | tf_op | source)
XLA Modules:
  0.0 132.7 jit_solution(17767400042881249767)
XLA Ops:
  1.3 4.1 %prepare.1 = (bf16[64,40,128]{2,1,0:T(8,128)(2,1)}, f32[2,18,128]{2,1,0:T(8,128)S(1)}) custom-call(s32[1]{0:T(128)} %bitcast.rot_ref, s32[1,1]{1,0:T(1,128)S(6)} %copy.16.count_ref, s32[144,128]{1,0:T(8,128)} %bitcast.20, bf16[8,1,3,2,384]{4,3,2,1,0:T(2,128)(2,1)} %bitcast.21, bf16[2,4096]{1,0:T(2,128)(2,1)} %bitcast.22, bf16[2,192,384]{2,1,0:T(8,128)(2,1)} %bitcast.16, ...), custom_call_target="tpu_custom_call" | custom-call | tf_op jit(solution)/shard_map/prepare/pallas_call | solution.py:163
  5.4 18.1 %all-to-all-start = ((bf16[64,40,128]{2,1,0:T(8,128)(2,1)}), bf16[64,40,128]{2,1,0:T(8,128)(2,1)S(1)}, u32[]{:S(2)}, u32[]{:S(2)}) async-start(bf16[64,40,128]{2,1,0:T(8,128)(2,1)} %get-tuple-element.28), calls=%async_computation | async-start | bytes 1310720 | tf_op jit(solution)/shard_map/all_to_all | solution.py:492
  23.5 1.5 %arrange.1 = (f32[27,64,128]{2,1,0:T(8,128)S(1)}, bf16[768,768]{1,0:T(8,128)(2,1)S(1)}) custom-call(bf16[2,192,384]{2,1,0:T(8,128)(2,1)} %bitcast.17, bf16[192,384]{1,0:T(8,128)(2,1)} %bitcast.19, bf16[384,768]{1,0:T(8,128)(2,1)} %constant.42.clone.tabx_hbm.tabx_ref), custom_call_target="tpu_custom_call" | custom-call | tf_op jit(solution)/shard_map/arrange/pallas_call | solution.py:211
  25.0 0.1 pad_add_fusion.at_ref
  25.1 34.5 %all-to-all-done.got_ref = bf16[64,40,128]{2,1,0:T(8,128)(2,1)S(1)} async-done(((bf16[64,40,128]{2,1,0:T(8,128)(2,1)}), bf16[64,40,128]{2,1,0:T(8,128)(2,1)S(1)}, u32[]{:S(2)}, u32[]{:S(2)}) %all-to-all-start) | async-done | bytes 655392 | tf_op jit(solution)/shard_map/all_to_all | solution.py:492
  59.6 1.9 %collective-permute-start = (bf16[64,24,128]{2,1,0:T(8,128)(2,1)S(1)}, bf16[64,24,128]{2,1,0:T(8,128)(2,1)S(1)}, u32[]{:S(2)}, u32[]{:S(2)}) collective-permute-start(bf16[64,24,128]{2,1,0:T(8,128)(2,1)S(1)} %slice.14.own_ref), channel_id=1, source_target_pairs={{0,2},{2,0},{4,6},{6,4},{8,10},{10,8},{12,14},{14,12},{16,18},{18,... | collective-permute-start | bytes 1179656 | tf_op jit(solution)/shard_map/ppermute | solution.py:454
  61.5 0.0 copy-start
  61.5 3.3 %collective-permute-start.1 = (bf16[64,16,128]{2,1,0:T(8,128)(2,1)S(1)}, bf16[64,16,128]{2,1,0:T(8,128)(2,1)S(1)}, u32[]{:S(2)}, u32[]{:S(2)}) collective-permute-start(bf16[64,16,128]{2,1,0:T(8,128)(2,1)S(1)} %slice.15), channel_id=1, source_target_pairs={{0,128},{128,0},{256,384},{384,256},{1,129},{129,1},{257,385},{385... | collective-permute-start | bytes 786440 | tf_op jit(solution)/shard_map/ppermute | solution.py:454
  64.9 0.0 collective-permute-done.other_ref
  64.9 3.6 %correlate.1 = (bf16[2,192,384]{2,1,0:T(8,128)(2,1)S(1)}, bf16[2,192,384]{2,1,0:T(8,128)(2,1)S(1)}) custom-call(s32[4]{0:T(128)S(1)} %pad_add_fusion.at_ref, bf16[64,24,128]{2,1,0:T(8,128)(2,1)S(1)} %slice.14.own_ref, bf16[64,24,128]{2,1,0:T(8,128)(2,1)S(1)} %collective-permute-done.other_ref, f32[27,64,128]{2,1,0:T(8,128)S(1)} %get-tuple-element.36.block_ref, ...), custom_call_target="tpu_custom_call" | custom-call | tf_op jit(solution)/shard_map/correlate/pallas_call | solution.py:272
  68.5 4.4 %collective-permute-start.3 = (bf16[2,192,384]{2,1,0:T(8,128)(2,1)S(1)}, bf16[2,192,384]{2,1,0:T(8,128)(2,1)S(1)}, u32[]{:S(2)}, u32[]{:S(2)}) collective-permute-start(bf16[2,192,384]{2,1,0:T(8,128)(2,1)S(1)} %get-tuple-element.45), channel_id=1, source_target_pairs={{0,1},{1,0},{2,3},{3,2},{4,5},{5,4},{6,7},{7,6},{8,9},{9,8},{10,11... | collective-permute-start | bytes 884744 | tf_op jit(solution)/shard_map/ppermute | solution.py:454
  72.9 0.0 collective-permute-done.1.share_ref
  72.9 0.0 copy-done
  72.9 4.4 %score.1 = (bf16[64,2,640]{2,1,0:T(2,128)(2,1)}, bf16[2,256,128]{2,1,0:T(8,128)(2,1)S(1)}) custom-call(s32[4]{0:T(128)S(1)} %pad_add_fusion.at_ref, bf16[64,40,128]{2,1,0:T(8,128)(2,1)S(1)} %all-to-all-done.got_ref, bf16[64,16,128]{2,1,0:T(8,128)(2,1)S(1)} %collective-permute-done.1.share_ref, f32[2,18,128]{2,1,0:T(8,128)S(1)} %get-tuple-element.40.slice_ref, ...), custom_call_target="tpu_custom_call" | custom-call | flops 6000000000 | bytes 8000000 | tf_op jit(solution)/shard_map/score/pallas_call | solution.py:378
  77.3 7.7 %all-to-all-start.1 = ((bf16[64,2,640]{2,1,0:T(2,128)(2,1)}), bf16[64,2,640]{2,1,0:T(2,128)(2,1)S(1)}, u32[]{:S(2)}, u32[]{:S(2)}) async-start(bf16[64,2,640]{2,1,0:T(2,128)(2,1)} %get-tuple-element.42), calls=%async_computation.1 | async-start | bytes 327680 | tf_op jit(solution)/shard_map/all_to_all | solution.py:500
  85.0 0.0 collective-permute-done.3
  85.0 0.1 add_multiply_fusion
  85.2 2.1 %collective-permute-start.4 = (bf16[2,192,384]{2,1,0:T(8,128)(2,1)S(1)}, bf16[2,192,384]{2,1,0:T(8,128)(2,1)S(1)}, u32[]{:S(2)}, u32[]{:S(2)}) collective-permute-start(bf16[2,192,384]{2,1,0:T(8,128)(2,1)S(1)} %pad_maximum_fusion.refs_0_), channel_id=1, source_target_pairs={{0,128},{128,0},{256,384},{384,256},{1,129},{129,1},{257,385},{385... | collective-permute-start | bytes 884744 | tf_op jit(solution)/shard_map/ppermute | solution.py:454
  87.3 4.8 %collective-permute-start.5 = (bf16[2,192,384]{2,1,0:T(8,128)(2,1)S(1)}, bf16[2,192,384]{2,1,0:T(8,128)(2,1)S(1)}, u32[]{:S(2)}, u32[]{:S(2)}) collective-permute-start(bf16[2,192,384]{2,1,0:T(8,128)(2,1)S(1)} %pad_maximum_fusion.refs_0_), channel_id=1, source_target_pairs={{0,256},{128,384},{256,0},{384,128},{1,257},{129,385},{257,1},{385... | collective-permute-start | bytes 884744 | tf_op jit(solution)/shard_map/ppermute | solution.py:454
  92.2 2.7 %collective-permute-start.6 = (bf16[2,192,384]{2,1,0:T(8,128)(2,1)S(1)}, bf16[2,192,384]{2,1,0:T(8,128)(2,1)S(1)}, u32[]{:S(2)}, u32[]{:S(2)}) collective-permute-start(bf16[2,192,384]{2,1,0:T(8,128)(2,1)S(1)} %pad_maximum_fusion.refs_0_), channel_id=1, source_target_pairs={{0,384},{128,256},{256,128},{384,0},{1,385},{129,257},{257,129},{3... | collective-permute-start | bytes 884744 | tf_op jit(solution)/shard_map/ppermute | solution.py:454
  94.8 8.5 %all-to-all-done.1 = bf16[64,2,640]{2,1,0:T(2,128)(2,1)S(1)} async-done(((bf16[64,2,640]{2,1,0:T(2,128)(2,1)}), bf16[64,2,640]{2,1,0:T(2,128)(2,1)S(1)}, u32[]{:S(2)}, u32[]{:S(2)}) %all-to-all-start.1) | async-done | bytes 163872 | tf_op jit(solution)/shard_map/all_to_all | solution.py:500
  103.4 0.2 convert_reduce_fusion.mine_ref
  103.5 3.2 %collective-permute-start.2 = (f32[2,640]{1,0:T(2,128)S(1)}, f32[2,640]{1,0:T(2,128)S(1)}, u32[]{:S(2)}, u32[]{:S(2)}) collective-permute-start(f32[2,640]{1,0:T(2,128)S(1)} %convert_reduce_fusion.mine_ref), channel_id=1, source_target_pairs={{0,1},{1,0},{2,3},{3,2},{4,5},{5,4},{6,7},{7,6},{8,9},{9,8},{10,11... | collective-permute-start | bytes 15368 | tf_op jit(solution)/shard_map/ppermute | solution.py:454
  106.7 2.7 %collective-permute-done.2.other_ref = f32[2,640]{1,0:T(2,128)S(1)} collective-permute-done((f32[2,640]{1,0:T(2,128)S(1)}, f32[2,640]{1,0:T(2,128)S(1)}, u32[]{:S(2)}, u32[]{:S(2)}) %collective-permute-start.2) | collective-permute-done | bytes 5152 | tf_op jit(solution)/shard_map/ppermute | solution.py:454
  109.4 0.8 expand.1
  110.2 7.2 %all-to-all-start.2 = ((f32[64,1,256]{2,1,0:T(1,128)}), f32[64,1,256]{2,1,0:T(1,128)S(1)}, u32[]{:S(2)}, u32[]{:S(2)}) async-start(f32[64,1,256]{2,1,0:T(1,128)} %get-tuple-element.43), calls=%async_computation.2 | async-start | bytes 131072 | tf_op jit(solution)/shard_map/all_to_all | solution.py:508
  117.4 0.0 collective-permute-done.4.refs_1_
  117.4 0.0 collective-permute-done.5.refs_2_
  117.4 0.0 collective-permute-done.6.refs_3_
  117.4 0.9 finish.1
  118.4 13.6 %all-to-all-done.2 = f32[64,1,256]{2,1,0:T(1,128)S(1)} async-done(((f32[64,1,256]{2,1,0:T(1,128)}), f32[64,1,256]{2,1,0:T(1,128)S(1)}, u32[]{:S(2)}, u32[]{:S(2)}) %all-to-all-start.2) | async-done | bytes 65568 | tf_op jit(solution)/shard_map/all_to_all | solution.py:508
  132.0 0.7 reduce_max.11
  (5 shorter events, 0.2 us)
Async XLA Ops:
  5.4 54.1 %all-to-all-start = ((bf16[64,40,128]{2,1,0:T(8,128)(2,1)}), bf16[64,40,128]{2,1,0:T(8,128)(2,1)S(1)}, u32[]{:S(2)}, u32[]{:S(2)}) async-start(bf16[64,40,128]{2,1,0:T(8,128)(2,1)} %get-tuple-element.28), calls=%async_computation | async-start | bytes 1310720 | tf_op jit(solution)/shard_map/all_to_all | solution.py:492
  59.6 5.3 %collective-permute-start = (bf16[64,24,128]{2,1,0:T(8,128)(2,1)S(1)}, bf16[64,24,128]{2,1,0:T(8,128)(2,1)S(1)}, u32[]{:S(2)}, u32[]{:S(2)}) collective-permute-start(bf16[64,24,128]{2,1,0:T(8,128)(2,1)S(1)} %slice.14.own_ref), channel_id=1, source_target_pairs={{0,2},{2,0},{4,6},{6,4},{8,10},{10,8},{12,14},{14,12},{16,18},{18,... | collective-permute-start | bytes 1179656 | tf_op jit(solution)/shard_map/ppermute | solution.py:454
  61.5 11.4 %copy-start = (bf16[384,768]{1,0:T(8,128)(2,1)S(1)}, bf16[384,768]{1,0:T(8,128)(2,1)}, u32[]{:S(2)}) copy-start(bf16[384,768]{1,0:T(8,128)(2,1)} %constant.42.clone.tabx_hbm.tabx_ref) | copy-start | bytes 1769476
  61.5 11.4 %collective-permute-start.1 = (bf16[64,16,128]{2,1,0:T(8,128)(2,1)S(1)}, bf16[64,16,128]{2,1,0:T(8,128)(2,1)S(1)}, u32[]{:S(2)}, u32[]{:S(2)}) collective-permute-start(bf16[64,16,128]{2,1,0:T(8,128)(2,1)S(1)} %slice.15), channel_id=1, source_target_pairs={{0,128},{128,0},{256,384},{384,256},{1,129},{129,1},{257,385},{385... | collective-permute-start | bytes 786440 | tf_op jit(solution)/shard_map/ppermute | solution.py:454
  68.5 16.5 %collective-permute-start.3 = (bf16[2,192,384]{2,1,0:T(8,128)(2,1)S(1)}, bf16[2,192,384]{2,1,0:T(8,128)(2,1)S(1)}, u32[]{:S(2)}, u32[]{:S(2)}) collective-permute-start(bf16[2,192,384]{2,1,0:T(8,128)(2,1)S(1)} %get-tuple-element.45), channel_id=1, source_target_pairs={{0,1},{1,0},{2,3},{3,2},{4,5},{5,4},{6,7},{7,6},{8,9},{9,8},{10,11... | collective-permute-start | bytes 884744 | tf_op jit(solution)/shard_map/ppermute | solution.py:454
  77.3 26.0 %all-to-all-start.1 = ((bf16[64,2,640]{2,1,0:T(2,128)(2,1)}), bf16[64,2,640]{2,1,0:T(2,128)(2,1)S(1)}, u32[]{:S(2)}, u32[]{:S(2)}) async-start(bf16[64,2,640]{2,1,0:T(2,128)(2,1)} %get-tuple-element.42), calls=%async_computation.1 | async-start | bytes 327680 | tf_op jit(solution)/shard_map/all_to_all | solution.py:500
  85.2 32.2 %collective-permute-start.4 = (bf16[2,192,384]{2,1,0:T(8,128)(2,1)S(1)}, bf16[2,192,384]{2,1,0:T(8,128)(2,1)S(1)}, u32[]{:S(2)}, u32[]{:S(2)}) collective-permute-start(bf16[2,192,384]{2,1,0:T(8,128)(2,1)S(1)} %pad_maximum_fusion.refs_0_), channel_id=1, source_target_pairs={{0,128},{128,0},{256,384},{384,256},{1,129},{129,1},{257,385},{385... | collective-permute-start | bytes 884744 | tf_op jit(solution)/shard_map/ppermute | solution.py:454
  87.3 30.1 %collective-permute-start.5 = (bf16[2,192,384]{2,1,0:T(8,128)(2,1)S(1)}, bf16[2,192,384]{2,1,0:T(8,128)(2,1)S(1)}, u32[]{:S(2)}, u32[]{:S(2)}) collective-permute-start(bf16[2,192,384]{2,1,0:T(8,128)(2,1)S(1)} %pad_maximum_fusion.refs_0_), channel_id=1, source_target_pairs={{0,256},{128,384},{256,0},{384,128},{1,257},{129,385},{257,1},{385... | collective-permute-start | bytes 884744 | tf_op jit(solution)/shard_map/ppermute | solution.py:454
  92.2 25.3 %collective-permute-start.6 = (bf16[2,192,384]{2,1,0:T(8,128)(2,1)S(1)}, bf16[2,192,384]{2,1,0:T(8,128)(2,1)S(1)}, u32[]{:S(2)}, u32[]{:S(2)}) collective-permute-start(bf16[2,192,384]{2,1,0:T(8,128)(2,1)S(1)} %pad_maximum_fusion.refs_0_), channel_id=1, source_target_pairs={{0,384},{128,256},{256,128},{384,0},{1,385},{129,257},{257,129},{3... | collective-permute-start | bytes 884744 | tf_op jit(solution)/shard_map/ppermute | solution.py:454
  103.5 5.9 %collective-permute-start.2 = (f32[2,640]{1,0:T(2,128)S(1)}, f32[2,640]{1,0:T(2,128)S(1)}, u32[]{:S(2)}, u32[]{:S(2)}) collective-permute-start(f32[2,640]{1,0:T(2,128)S(1)} %convert_reduce_fusion.mine_ref), channel_id=1, source_target_pairs={{0,1},{1,0},{2,3},{3,2},{4,5},{5,4},{6,7},{7,6},{8,9},{9,8},{10,11... | collective-permute-start | bytes 15368 | tf_op jit(solution)/shard_map/ppermute | solution.py:454
  110.2 21.8 %all-to-all-start.2 = ((f32[64,1,256]{2,1,0:T(1,128)}), f32[64,1,256]{2,1,0:T(1,128)S(1)}, u32[]{:S(2)}, u32[]{:S(2)}) async-start(f32[64,1,256]{2,1,0:T(1,128)} %get-tuple-element.43), calls=%async_computation.2 | async-start | bytes 131072 | tf_op jit(solution)/shard_map/all_to_all | solution.py:508

commit v7 on v6

--- a/solution.py
+++ b/solution.py
@@ -102,7 +102,7 @@
                 value_s[c, rows, :] = pick(c, 4, 0) * weight_s[rows, :]
             return carry
 
-        lax.fori_loop(0, 2 * BLOCKS, step, 0, unroll=3)
+        lax.fori_loop(0, 2 * BLOCKS, step, 0, unroll=6)
         for c in range(2):
             total = value_s[c, 0 : 2 * BLOCKS, :]
             for k in range(1, 8):
@@ -355,11 +355,21 @@
                     cy, sy = cosines[at], sines[at]
                     wx, vx = cx[at, cols], sx[at, cols]
                     pieces[i].append(cy * (pr * wx - pi * vx) - sy * (pr * vx + pi * wx))
-        shifted = jnp.concatenate([jnp.concatenate(p, axis=1) for p in pieces], axis=0)
-        bin_of = lax.shift_right_logical(lax.broadcasted_iota(I32, (WIDE, DFT), 0), 2)
-        group = jnp.where(bin_of == lax.broadcasted_iota(I32, (WIDE, DFT), 1), 1.0, 0.0).astype(BF)
-        binned = lax.dot_general(shifted.astype(BF), group, NN, preferred_element_type=F32)
-        binned = binned.astype(BF)[:, :BINS]
+        shifted = jnp.concatenate(
+            [
+                jnp.concatenate(pieces[i][j * ROWS : (j + 1) * ROWS], axis=1).astype(BF)
+                for j in range(ROWS)
+                for i in range(SLOTS)
+            ],
+            axis=0,
+        )
+        bin_of = lax.shift_right_logical(lax.broadcasted_iota(I32, (DFT, LANES), 0), 2)
+        group = jnp.where(bin_of == lax.broadcasted_iota(I32, (DFT, LANES), 1), 1.0, 0.0).astype(BF)
+        sums = lax.dot_general(shifted, group, NN, preferred_element_type=F32)
+        count_rows = SLOTS * TILES
+        binned = jnp.concatenate(
+            [sums[j * count_rows : (j + 1) * count_rows, : DFT // 4] for j in range(ROWS)], axis=1
+        ).astype(BF)
         grid = jnp.concatenate([sent(2 * BLOCKS + r).astype(BF) for r in range(2 * BLOCKS)], axis=1)
         values = jnp.concatenate([grid[:, q * BINS : (q + 1) * BINS] for q in range(GRID)], axis=0)
         scores = lax.dot_general(values, binned, NT, preferred_element_type=F32).astype(BF)

time: 133 us -> 133 us (level)
  transfers between devices with their start and end apart: 10 -> 10, of which waited for: 4 -> 4; matrix products, arithmetic and copies ran while one was open for 0% -> 0% of each run, Pallas kernels for 9% -> 8%
where the time goes in v7:
time: 133 us; the launch traced here: 132 us
  waiting for transfers between devices  59.3 us (45%)
  starting transfers between devices  55.3 us (42%)
  Pallas kernels  14.9 us (11%)
  between operations  1.52 us (1%)
    all_to_all x1, waiting for transfers between devices, shards(): got = lax.all_to_all(blocks, 'tile', 0, 0, tiled=True)  34.5 us
    ppermute x7, starting transfers between devices, exchange(): return lax.ppermute(x, axis, [(k, k ^ bit) for k in range(size)])  22.3 us
    all_to_all x1, starting transfers between devices, shards(): got = lax.all_to_all(blocks, 'tile', 0, 0, tiled=True)  18.1 us
    all_to_all x1, waiting for transfers between devices, shards(): tops = lax.all_to_all(tops, 'tile', 0, 0)  13.6 us
    all_to_all x1, waiting for transfers between devices, shards(): sums = lax.all_to_all(packed, 'tile', 0, 0, tiled=True)  8.52 us
    all_to_all x1, starting transfers between devices, shards(): sums = lax.all_to_all(packed, 'tile', 0, 0, tiled=True)  7.68 us
    all_to_all x1, starting transfers between devices, shards(): tops = lax.all_to_all(tops, 'tile', 0, 0)  7.16 us
    pallas_call x1, Pallas kernels, score(): pl.pallas_call(kernel, out_shape=(jax.ShapeDtypeStruct((TILES, 2, SPAN *...  4.14 us
  transfers between devices with their start and end apart: 10, of which 4 were waited for; matrix products, arithmetic and copies ran while one was open for 0% of the time, Pallas kernels for 8%

profile of v7, /device:TPU:1, one launch (start us, length us, event | category | flops | bytes accessed | tf_op | source)
XLA Modules:
  0.0 132.2 jit_solution(4259310993530974266)
XLA Ops:
  1.3 3.9 %prepare.1 = (bf16[64,40,128]{2,1,0:T(8,128)(2,1)}, f32[2,18,128]{2,1,0:T(8,128)S(1)}) custom-call(s32[1]{0:T(128)} %bitcast.rot_ref, s32[1,1]{1,0:T(1,128)S(6)} %copy.16.count_ref, s32[144,128]{1,0:T(8,128)} %bitcast.20, bf16[8,1,3,2,384]{4,3,2,1,0:T(2,128)(2,1)} %bitcast.21, bf16[2,4096]{1,0:T(2,128)(2,1)} %bitcast.22, bf16[2,192,384]{2,1,0:T(8,128)(2,1)} %bitcast.16, ...), custom_call_target="tpu_custom_call" | custom-call | tf_op jit(solution)/shard_map/prepare/pallas_call | solution.py:163
  5.2 18.1 %all-to-all-start = ((bf16[64,40,128]{2,1,0:T(8,128)(2,1)}), bf16[64,40,128]{2,1,0:T(8,128)(2,1)S(1)}, u32[]{:S(2)}, u32[]{:S(2)}) async-start(bf16[64,40,128]{2,1,0:T(8,128)(2,1)} %get-tuple-element.28), calls=%async_computation | async-start | bytes 1310720 | tf_op jit(solution)/shard_map/all_to_all | solution.py:502
  23.3 1.5 %arrange.1 = (f32[27,64,128]{2,1,0:T(8,128)S(1)}, bf16[768,768]{1,0:T(8,128)(2,1)S(1)}) custom-call(bf16[2,192,384]{2,1,0:T(8,128)(2,1)} %bitcast.17, bf16[192,384]{1,0:T(8,128)(2,1)} %bitcast.19, bf16[384,768]{1,0:T(8,128)(2,1)} %constant.42.clone.tabx_hbm.tabx_ref), custom_call_target="tpu_custom_call" | custom-call | tf_op jit(solution)/shard_map/arrange/pallas_call | solution.py:211
  24.8 0.1 pad_add_fusion.at_ref
  24.8 34.5 %all-to-all-done.got_ref = bf16[64,40,128]{2,1,0:T(8,128)(2,1)S(1)} async-done(((bf16[64,40,128]{2,1,0:T(8,128)(2,1)}), bf16[64,40,128]{2,1,0:T(8,128)(2,1)S(1)}, u32[]{:S(2)}, u32[]{:S(2)}) %all-to-all-start) | async-done | bytes 655392 | tf_op jit(solution)/shard_map/all_to_all | solution.py:502
  59.3 1.9 %collective-permute-start = (bf16[64,24,128]{2,1,0:T(8,128)(2,1)S(1)}, bf16[64,24,128]{2,1,0:T(8,128)(2,1)S(1)}, u32[]{:S(2)}, u32[]{:S(2)}) collective-permute-start(bf16[64,24,128]{2,1,0:T(8,128)(2,1)S(1)} %slice.14.own_ref), channel_id=1, source_target_pairs={{0,2},{2,0},{4,6},{6,4},{8,10},{10,8},{12,14},{14,12},{16,18},{18,... | collective-permute-start | bytes 1179656 | tf_op jit(solution)/shard_map/ppermute | solution.py:464
  61.3 0.0 copy-start
  61.3 3.3 %collective-permute-start.1 = (bf16[64,16,128]{2,1,0:T(8,128)(2,1)S(1)}, bf16[64,16,128]{2,1,0:T(8,128)(2,1)S(1)}, u32[]{:S(2)}, u32[]{:S(2)}) collective-permute-start(bf16[64,16,128]{2,1,0:T(8,128)(2,1)S(1)} %slice.15), channel_id=1, source_target_pairs={{0,128},{128,0},{256,384},{384,256},{1,129},{129,1},{257,385},{385... | collective-permute-start | bytes 786440 | tf_op jit(solution)/shard_map/ppermute | solution.py:464
  64.7 0.0 collective-permute-done.other_ref
  64.7 3.6 %correlate.1 = (bf16[2,192,384]{2,1,0:T(8,128)(2,1)S(1)}, bf16[2,192,384]{2,1,0:T(8,128)(2,1)S(1)}) custom-call(s32[4]{0:T(128)S(1)} %pad_add_fusion.at_ref, bf16[64,24,128]{2,1,0:T(8,128)(2,1)S(1)} %slice.14.own_ref, bf16[64,24,128]{2,1,0:T(8,128)(2,1)S(1)} %collective-permute-done.other_ref, f32[27,64,128]{2,1,0:T(8,128)S(1)} %get-tuple-element.36.block_ref, ...), custom_call_target="tpu_custom_call" | custom-call | tf_op jit(solution)/shard_map/correlate/pallas_call | solution.py:272
  68.3 4.4 %collective-permute-start.3 = (bf16[2,192,384]{2,1,0:T(8,128)(2,1)S(1)}, bf16[2,192,384]{2,1,0:T(8,128)(2,1)S(1)}, u32[]{:S(2)}, u32[]{:S(2)}) collective-permute-start(bf16[2,192,384]{2,1,0:T(8,128)(2,1)S(1)} %get-tuple-element.45), channel_id=1, source_target_pairs={{0,1},{1,0},{2,3},{3,2},{4,5},{5,4},{6,7},{7,6},{8,9},{9,8},{10,11... | collective-permute-start | bytes 884744 | tf_op jit(solution)/shard_map/ppermute | solution.py:464
  72.7 0.0 collective-permute-done.1.share_ref
  72.7 0.0 copy-done
  72.7 4.1 %score.1 = (bf16[64,2,640]{2,1,0:T(2,128)(2,1)}, bf16[2,256,128]{2,1,0:T(8,128)(2,1)S(1)}) custom-call(s32[4]{0:T(128)S(1)} %pad_add_fusion.at_ref, bf16[64,40,128]{2,1,0:T(8,128)(2,1)S(1)} %all-to-all-done.got_ref, bf16[64,16,128]{2,1,0:T(8,128)(2,1)S(1)} %collective-permute-done.1.share_ref, f32[2,18,128]{2,1,0:T(8,128)S(1)} %get-tuple-element.40.slice_ref, ...), custom_call_target="tpu_custom_call" | custom-call | flops 6000000000 | bytes 8000000 | tf_op jit(solution)/shard_map/score/pallas_call | solution.py:388
  76.8 7.7 %all-to-all-start.1 = ((bf16[64,2,640]{2,1,0:T(2,128)(2,1)}), bf16[64,2,640]{2,1,0:T(2,128)(2,1)S(1)}, u32[]{:S(2)}, u32[]{:S(2)}) async-start(bf16[64,2,640]{2,1,0:T(2,128)(2,1)} %get-tuple-element.42), calls=%async_computation.1 | async-start | bytes 327680 | tf_op jit(solution)/shard_map/all_to_all | solution.py:510
  84.5 0.0 collective-permute-done.3
  84.5 0.1 add_multiply_fusion
  84.7 2.1 %collective-permute-start.4 = (bf16[2,192,384]{2,1,0:T(8,128)(2,1)S(1)}, bf16[2,192,384]{2,1,0:T(8,128)(2,1)S(1)}, u32[]{:S(2)}, u32[]{:S(2)}) collective-permute-start(bf16[2,192,384]{2,1,0:T(8,128)(2,1)S(1)} %pad_maximum_fusion.refs_0_), channel_id=1, source_target_pairs={{0,128},{128,0},{256,384},{384,256},{1,129},{129,1},{257,385},{385... | collective-permute-start | bytes 884744 | tf_op jit(solution)/shard_map/ppermute | solution.py:464
  86.8 4.8 %collective-permute-start.5 = (bf16[2,192,384]{2,1,0:T(8,128)(2,1)S(1)}, bf16[2,192,384]{2,1,0:T(8,128)(2,1)S(1)}, u32[]{:S(2)}, u32[]{:S(2)}) collective-permute-start(bf16[2,192,384]{2,1,0:T(8,128)(2,1)S(1)} %pad_maximum_fusion.refs_0_), channel_id=1, source_target_pairs={{0,256},{128,384},{256,0},{384,128},{1,257},{129,385},{257,1},{385... | collective-permute-start | bytes 884744 | tf_op jit(solution)/shard_map/ppermute | solution.py:464
  91.7 2.7 %collective-permute-start.6 = (bf16[2,192,384]{2,1,0:T(8,128)(2,1)S(1)}, bf16[2,192,384]{2,1,0:T(8,128)(2,1)S(1)}, u32[]{:S(2)}, u32[]{:S(2)}) collective-permute-start(bf16[2,192,384]{2,1,0:T(8,128)(2,1)S(1)} %pad_maximum_fusion.refs_0_), channel_id=1, source_target_pairs={{0,384},{128,256},{256,128},{384,0},{1,385},{129,257},{257,129},{3... | collective-permute-start | bytes 884744 | tf_op jit(solution)/shard_map/ppermute | solution.py:464
  94.4 8.5 %all-to-all-done.1 = bf16[64,2,640]{2,1,0:T(2,128)(2,1)S(1)} async-done(((bf16[64,2,640]{2,1,0:T(2,128)(2,1)}), bf16[64,2,640]{2,1,0:T(2,128)(2,1)S(1)}, u32[]{:S(2)}, u32[]{:S(2)}) %all-to-all-start.1) | async-done | bytes 163872 | tf_op jit(solution)/shard_map/all_to_all | solution.py:510
  102.9 0.2 convert_reduce_fusion.mine_ref
  103.0 3.1 %collective-permute-start.2 = (f32[2,640]{1,0:T(2,128)S(1)}, f32[2,640]{1,0:T(2,128)S(1)}, u32[]{:S(2)}, u32[]{:S(2)}) collective-permute-start(f32[2,640]{1,0:T(2,128)S(1)} %convert_reduce_fusion.mine_ref), channel_id=1, source_target_pairs={{0,1},{1,0},{2,3},{3,2},{4,5},{5,4},{6,7},{7,6},{8,9},{9,8},{10,11... | collective-permute-start | bytes 15368 | tf_op jit(solution)/shard_map/ppermute | solution.py:464
  106.2 2.7 %collective-permute-done.2.other_ref = f32[2,640]{1,0:T(2,128)S(1)} collective-permute-done((f32[2,640]{1,0:T(2,128)S(1)}, f32[2,640]{1,0:T(2,128)S(1)}, u32[]{:S(2)}, u32[]{:S(2)}) %collective-permute-start.2) | collective-permute-done | bytes 5152 | tf_op jit(solution)/shard_map/ppermute | solution.py:464
  108.9 0.8 expand.1
  109.7 7.2 %all-to-all-start.2 = ((f32[64,1,256]{2,1,0:T(1,128)}), f32[64,1,256]{2,1,0:T(1,128)S(1)}, u32[]{:S(2)}, u32[]{:S(2)}) async-start(f32[64,1,256]{2,1,0:T(1,128)} %get-tuple-element.43), calls=%async_computation.2 | async-start | bytes 131072 | tf_op jit(solution)/shard_map/all_to_all | solution.py:518
  116.9 0.0 collective-permute-done.4.refs_1_
  116.9 0.0 collective-permute-done.5.refs_2_
  116.9 0.0 collective-permute-done.6.refs_3_
  116.9 0.9 finish.1
  117.9 13.6 %all-to-all-done.2 = f32[64,1,256]{2,1,0:T(1,128)S(1)} async-done(((f32[64,1,256]{2,1,0:T(1,128)}), f32[64,1,256]{2,1,0:T(1,128)S(1)}, u32[]{:S(2)}, u32[]{:S(2)}) %all-to-all-start.2) | async-done | bytes 65568 | tf_op jit(solution)/shard_map/all_to_all | solution.py:518
  131.5 0.7 reduce_max.11
  (5 shorter events, 0.2 us)
Async XLA Ops:
  5.2 54.1 %all-to-all-start = ((bf16[64,40,128]{2,1,0:T(8,128)(2,1)}), bf16[64,40,128]{2,1,0:T(8,128)(2,1)S(1)}, u32[]{:S(2)}, u32[]{:S(2)}) async-start(bf16[64,40,128]{2,1,0:T(8,128)(2,1)} %get-tuple-element.28), calls=%async_computation | async-start | bytes 1310720 | tf_op jit(solution)/shard_map/all_to_all | solution.py:502
  59.3 5.3 %collective-permute-start = (bf16[64,24,128]{2,1,0:T(8,128)(2,1)S(1)}, bf16[64,24,128]{2,1,0:T(8,128)(2,1)S(1)}, u32[]{:S(2)}, u32[]{:S(2)}) collective-permute-start(bf16[64,24,128]{2,1,0:T(8,128)(2,1)S(1)} %slice.14.own_ref), channel_id=1, source_target_pairs={{0,2},{2,0},{4,6},{6,4},{8,10},{10,8},{12,14},{14,12},{16,18},{18,... | collective-permute-start | bytes 1179656 | tf_op jit(solution)/shard_map/ppermute | solution.py:464
  61.3 11.4 %copy-start = (bf16[384,768]{1,0:T(8,128)(2,1)S(1)}, bf16[384,768]{1,0:T(8,128)(2,1)}, u32[]{:S(2)}) copy-start(bf16[384,768]{1,0:T(8,128)(2,1)} %constant.42.clone.tabx_hbm.tabx_ref) | copy-start | bytes 1769476
  61.3 11.4 %collective-permute-start.1 = (bf16[64,16,128]{2,1,0:T(8,128)(2,1)S(1)}, bf16[64,16,128]{2,1,0:T(8,128)(2,1)S(1)}, u32[]{:S(2)}, u32[]{:S(2)}) collective-permute-start(bf16[64,16,128]{2,1,0:T(8,128)(2,1)S(1)} %slice.15), channel_id=1, source_target_pairs={{0,128},{128,0},{256,384},{384,256},{1,129},{129,1},{257,385},{385... | collective-permute-start | bytes 786440 | tf_op jit(solution)/shard_map/ppermute | solution.py:464
  68.3 16.2 %collective-permute-start.3 = (bf16[2,192,384]{2,1,0:T(8,128)(2,1)S(1)}, bf16[2,192,384]{2,1,0:T(8,128)(2,1)S(1)}, u32[]{:S(2)}, u32[]{:S(2)}) collective-permute-start(bf16[2,192,384]{2,1,0:T(8,128)(2,1)S(1)} %get-tuple-element.45), channel_id=1, source_target_pairs={{0,1},{1,0},{2,3},{3,2},{4,5},{5,4},{6,7},{7,6},{8,9},{9,8},{10,11... | collective-permute-start | bytes 884744 | tf_op jit(solution)/shard_map/ppermute | solution.py:464
  76.8 26.0 %all-to-all-start.1 = ((bf16[64,2,640]{2,1,0:T(2,128)(2,1)}), bf16[64,2,640]{2,1,0:T(2,128)(2,1)S(1)}, u32[]{:S(2)}, u32[]{:S(2)}) async-start(bf16[64,2,640]{2,1,0:T(2,128)(2,1)} %get-tuple-element.42), calls=%async_computation.1 | async-start | bytes 327680 | tf_op jit(solution)/shard_map/all_to_all | solution.py:510
  84.7 32.2 %collective-permute-start.4 = (bf16[2,192,384]{2,1,0:T(8,128)(2,1)S(1)}, bf16[2,192,384]{2,1,0:T(8,128)(2,1)S(1)}, u32[]{:S(2)}, u32[]{:S(2)}) collective-permute-start(bf16[2,192,384]{2,1,0:T(8,128)(2,1)S(1)} %pad_maximum_fusion.refs_0_), channel_id=1, source_target_pairs={{0,128},{128,0},{256,384},{384,256},{1,129},{129,1},{257,385},{385... | collective-permute-start | bytes 884744 | tf_op jit(solution)/shard_map/ppermute | solution.py:464
  86.8 30.1 %collective-permute-start.5 = (bf16[2,192,384]{2,1,0:T(8,128)(2,1)S(1)}, bf16[2,192,384]{2,1,0:T(8,128)(2,1)S(1)}, u32[]{:S(2)}, u32[]{:S(2)}) collective-permute-start(bf16[2,192,384]{2,1,0:T(8,128)(2,1)S(1)} %pad_maximum_fusion.refs_0_), channel_id=1, source_target_pairs={{0,256},{128,384},{256,0},{384,128},{1,257},{129,385},{257,1},{385... | collective-permute-start | bytes 884744 | tf_op jit(solution)/shard_map/ppermute | solution.py:464
  91.7 25.3 %collective-permute-start.6 = (bf16[2,192,384]{2,1,0:T(8,128)(2,1)S(1)}, bf16[2,192,384]{2,1,0:T(8,128)(2,1)S(1)}, u32[]{:S(2)}, u32[]{:S(2)}) collective-permute-start(bf16[2,192,384]{2,1,0:T(8,128)(2,1)S(1)} %pad_maximum_fusion.refs_0_), channel_id=1, source_target_pairs={{0,384},{128,256},{256,128},{384,0},{1,385},{129,257},{257,129},{3... | collective-permute-start | bytes 884744 | tf_op jit(solution)/shard_map/ppermute | solution.py:464
  103.0 5.9 %collective-permute-start.2 = (f32[2,640]{1,0:T(2,128)S(1)}, f32[2,640]{1,0:T(2,128)S(1)}, u32[]{:S(2)}, u32[]{:S(2)}) collective-permute-start(f32[2,640]{1,0:T(2,128)S(1)} %convert_reduce_fusion.mine_ref), channel_id=1, source_target_pairs={{0,1},{1,0},{2,3},{3,2},{4,5},{5,4},{6,7},{7,6},{8,9},{9,8},{10,11... | collective-permute-start | bytes 15368 | tf_op jit(solution)/shard_map/ppermute | solution.py:464
  109.7 21.8 %all-to-all-start.2 = ((f32[64,1,256]{2,1,0:T(1,128)}), f32[64,1,256]{2,1,0:T(1,128)S(1)}, u32[]{:S(2)}, u32[]{:S(2)}) async-start(f32[64,1,256]{2,1,0:T(1,128)} %get-tuple-element.43), calls=%async_computation.2 | async-start | bytes 131072 | tf_op jit(solution)/shard_map/all_to_all | solution.py:518

commit v8 on v7

--- a/solution.py
+++ b/solution.py
@@ -102,7 +102,7 @@
                 value_s[c, rows, :] = pick(c, 4, 0) * weight_s[rows, :]
             return carry
 
-        lax.fori_loop(0, 2 * BLOCKS, step, 0, unroll=6)
+        lax.fori_loop(0, 2 * BLOCKS, step, 0, unroll=9)
         for c in range(2):
             total = value_s[c, 0 : 2 * BLOCKS, :]
             for k in range(1, 8):
@@ -288,7 +288,7 @@
 def score(place, got, share, slices, tabx):
     def kernel(
         at_ref, got_ref, share_ref, slice_ref, tabx_ref,
-        out_ref, place_hbm, got_s, share_s, place_s, place_ref, sem, out_s,
+        out_hbm, place_hbm, got_s, share_s, place_s, place_ref, sems, out_s, out_ref,
     ):
         got_s[...] = got_ref[...].astype(F32).reshape(got_s.shape)
         side = at_ref[2] & 1
@@ -321,8 +321,8 @@
                 place_s[h, pl.ds(i, TILES, stride=SLOTS), :] = hot[:, h * LANES : (h + 1) * LANES]
             place.append(hot.astype(BF))
         place_ref[...] = place_s[...].astype(BF)
-        leave = pltpu.make_async_copy(place_ref, place_hbm, sem)
-        leave.start()
+        leave = [pltpu.make_async_copy(place_ref, place_hbm, sems.at[0])]
+        leave[0].start()
         hot_x = jnp.concatenate(hot_x, axis=0)
         hot_y = jnp.concatenate(hot_y, axis=0)
         place = jnp.concatenate(place, axis=0)
@@ -382,8 +382,14 @@
             extra = jnp.where(lanes == q, block[:, LANES : LANES + 1], extra)
         out_s[:, 1, (SPAN - 2) * LANES : (SPAN - 1) * LANES] = extra
         out_s[:, 1, (SPAN - 1) * LANES :] = jnp.zeros((TILES, LANES), F32)
-        out_ref[...] = out_s[...].astype(BF)
-        leave.wait()
+        piece = TILES // 4
+        for k in range(4):
+            at = pl.ds(k * piece, piece)
+            out_ref[k * piece : (k + 1) * piece] = out_s[k * piece : (k + 1) * piece].astype(BF)
+            leave.append(pltpu.make_async_copy(out_ref.at[at], out_hbm.at[at], sems.at[1 + k]))
+            leave[-1].start()
+        for copy in leave:
+            copy.wait()
 
     return pl.pallas_call(
         kernel,
@@ -392,8 +398,8 @@
             jax.ShapeDtypeStruct((2, SLOTS * TILES, LANES), BF),
         ),
         in_specs=[SM] + [VM] * 4,
-        out_specs=(VM, HB),
-        scratch_shapes=[pltpu.VMEM((TILES * XROWS, LANES), F32), pltpu.VMEM((2, TILES * SHARE, LANES), F32), pltpu.VMEM((2, SLOTS * TILES, LANES), F32), pltpu.VMEM((2, SLOTS * TILES, LANES), BF), pltpu.SemaphoreType.DMA, pltpu.VMEM((TILES, 2, SPAN * LANES), F32)],
+        out_specs=(HB, HB),
+        scratch_shapes=[pltpu.VMEM((TILES * XROWS, LANES), F32), pltpu.VMEM((2, TILES * SHARE, LANES), F32), pltpu.VMEM((2, SLOTS * TILES, LANES), F32), pltpu.VMEM((2, SLOTS * TILES, LANES), BF), pltpu.SemaphoreType.DMA((5,)), pltpu.VMEM((TILES, 2, SPAN * LANES), F32), pltpu.VMEM((TILES, 2, SPAN * LANES), BF)],
         compiler_params=pltpu.CompilerParams(vmem_limit_bytes=VMEM_LIMIT),
         cost_estimate=pl.CostEstimate(flops=6_000_000_000, transcendentals=0, bytes_accessed=8_000_000),
         name="score",

time: 133 us -> 133 us (level)
  no operation moved by 1% of the time
where the time goes in v8:
time: 133 us; the launch traced here: 132 us
  waiting for transfers between devices  59.3 us (45%)
  starting transfers between devices  55.3 us (42%)
  Pallas kernels  14.8 us (11%)
  between operations  1.52 us (1%)
    all_to_all x1, waiting for transfers between devices, shards(): got = lax.all_to_all(blocks, 'tile', 0, 0, tiled=True)  34.5 us
    ppermute x7, starting transfers between devices, exchange(): return lax.ppermute(x, axis, [(k, k ^ bit) for k in range(size)])  22.3 us
    all_to_all x1, starting transfers between devices, shards(): got = lax.all_to_all(blocks, 'tile', 0, 0, tiled=True)  18.1 us
    all_to_all x1, waiting for transfers between devices, shards(): tops = lax.all_to_all(tops, 'tile', 0, 0)  13.6 us
    all_to_all x1, waiting for transfers between devices, shards(): sums = lax.all_to_all(packed, 'tile', 0, 0, tiled=True)  8.52 us
    all_to_all x1, starting transfers between devices, shards(): sums = lax.all_to_all(packed, 'tile', 0, 0, tiled=True)  7.69 us
    all_to_all x1, starting transfers between devices, shards(): tops = lax.all_to_all(tops, 'tile', 0, 0)  7.16 us
    pallas_call x1, Pallas kernels, score(): pl.pallas_call(kernel, out_shape=(jax.ShapeDtypeStruct((TILES, 2, SPAN *...  4.12 us
  transfers between devices with their start and end apart: 10, of which 4 were waited for; matrix products, arithmetic and copies ran while one was open for 0% of the time, Pallas kernels for 8%

profile of v8, /device:TPU:1, one launch (start us, length us, event | category | flops | bytes accessed | tf_op | source)
XLA Modules:
  0.0 132.1 jit_solution(8467044406871448003)
XLA Ops:
  1.3 3.8 %prepare.1 = (bf16[64,40,128]{2,1,0:T(8,128)(2,1)}, f32[2,18,128]{2,1,0:T(8,128)S(1)}) custom-call(s32[1]{0:T(128)} %bitcast.rot_ref, s32[1,1]{1,0:T(1,128)S(6)} %copy.16.count_ref, s32[144,128]{1,0:T(8,128)} %bitcast.20, bf16[8,1,3,2,384]{4,3,2,1,0:T(2,128)(2,1)} %bitcast.21, bf16[2,4096]{1,0:T(2,128)(2,1)} %bitcast.22, bf16[2,192,384]{2,1,0:T(8,128)(2,1)} %bitcast.16, ...), custom_call_target="tpu_custom_call" | custom-call | tf_op jit(solution)/shard_map/prepare/pallas_call | solution.py:163
  5.1 18.1 %all-to-all-start = ((bf16[64,40,128]{2,1,0:T(8,128)(2,1)}), bf16[64,40,128]{2,1,0:T(8,128)(2,1)S(1)}, u32[]{:S(2)}, u32[]{:S(2)}) async-start(bf16[64,40,128]{2,1,0:T(8,128)(2,1)} %get-tuple-element.28), calls=%async_computation | async-start | bytes 1310720 | tf_op jit(solution)/shard_map/all_to_all | solution.py:508
  23.2 1.5 %arrange.1 = (f32[27,64,128]{2,1,0:T(8,128)S(1)}, bf16[768,768]{1,0:T(8,128)(2,1)S(1)}) custom-call(bf16[2,192,384]{2,1,0:T(8,128)(2,1)} %bitcast.17, bf16[192,384]{1,0:T(8,128)(2,1)} %bitcast.19, bf16[384,768]{1,0:T(8,128)(2,1)} %constant.42.clone.tabx_hbm.tabx_ref), custom_call_target="tpu_custom_call" | custom-call | tf_op jit(solution)/shard_map/arrange/pallas_call | solution.py:211
  24.7 0.1 pad_add_fusion.at_ref
  24.8 34.5 %all-to-all-done.got_ref = bf16[64,40,128]{2,1,0:T(8,128)(2,1)S(1)} async-done(((bf16[64,40,128]{2,1,0:T(8,128)(2,1)}), bf16[64,40,128]{2,1,0:T(8,128)(2,1)S(1)}, u32[]{:S(2)}, u32[]{:S(2)}) %all-to-all-start) | async-done | bytes 655392 | tf_op jit(solution)/shard_map/all_to_all | solution.py:508
  59.3 1.9 %collective-permute-start = (bf16[64,24,128]{2,1,0:T(8,128)(2,1)S(1)}, bf16[64,24,128]{2,1,0:T(8,128)(2,1)S(1)}, u32[]{:S(2)}, u32[]{:S(2)}) collective-permute-start(bf16[64,24,128]{2,1,0:T(8,128)(2,1)S(1)} %slice.14.own_ref), channel_id=1, source_target_pairs={{0,2},{2,0},{4,6},{6,4},{8,10},{10,8},{12,14},{14,12},{16,18},{18,... | collective-permute-start | bytes 1179656 | tf_op jit(solution)/shard_map/ppermute | solution.py:470
  61.2 0.0 copy-start
  61.2 3.3 %collective-permute-start.1 = (bf16[64,16,128]{2,1,0:T(8,128)(2,1)S(1)}, bf16[64,16,128]{2,1,0:T(8,128)(2,1)S(1)}, u32[]{:S(2)}, u32[]{:S(2)}) collective-permute-start(bf16[64,16,128]{2,1,0:T(8,128)(2,1)S(1)} %slice.15), channel_id=1, source_target_pairs={{0,128},{128,0},{256,384},{384,256},{1,129},{129,1},{257,385},{385... | collective-permute-start | bytes 786440 | tf_op jit(solution)/shard_map/ppermute | solution.py:470
  64.6 0.0 collective-permute-done.other_ref
  64.6 3.6 %correlate.1 = (bf16[2,192,384]{2,1,0:T(8,128)(2,1)S(1)}, bf16[2,192,384]{2,1,0:T(8,128)(2,1)S(1)}) custom-call(s32[4]{0:T(128)S(1)} %pad_add_fusion.at_ref, bf16[64,24,128]{2,1,0:T(8,128)(2,1)S(1)} %slice.14.own_ref, bf16[64,24,128]{2,1,0:T(8,128)(2,1)S(1)} %collective-permute-done.other_ref, f32[27,64,128]{2,1,0:T(8,128)S(1)} %get-tuple-element.36.block_ref, ...), custom_call_target="tpu_custom_call" | custom-call | tf_op jit(solution)/shard_map/correlate/pallas_call | solution.py:272
  68.2 4.4 %collective-permute-start.3 = (bf16[2,192,384]{2,1,0:T(8,128)(2,1)S(1)}, bf16[2,192,384]{2,1,0:T(8,128)(2,1)S(1)}, u32[]{:S(2)}, u32[]{:S(2)}) collective-permute-start(bf16[2,192,384]{2,1,0:T(8,128)(2,1)S(1)} %get-tuple-element.45), channel_id=1, source_target_pairs={{0,1},{1,0},{2,3},{3,2},{4,5},{5,4},{6,7},{7,6},{8,9},{9,8},{10,11... | collective-permute-start | bytes 884744 | tf_op jit(solution)/shard_map/ppermute | solution.py:470
  72.6 0.0 collective-permute-done.1.share_ref
  72.6 0.0 copy-done
  72.6 4.1 %score.1 = (bf16[64,2,640]{2,1,0:T(2,128)(2,1)}, bf16[2,256,128]{2,1,0:T(8,128)(2,1)S(1)}) custom-call(s32[4]{0:T(128)S(1)} %pad_add_fusion.at_ref, bf16[64,40,128]{2,1,0:T(8,128)(2,1)S(1)} %all-to-all-done.got_ref, bf16[64,16,128]{2,1,0:T(8,128)(2,1)S(1)} %collective-permute-done.1.share_ref, f32[2,18,128]{2,1,0:T(8,128)S(1)} %get-tuple-element.40.slice_ref, ...), custom_call_target="tpu_custom_call" | custom-call | flops 6000000000 | bytes 8000000 | tf_op jit(solution)/shard_map/score/pallas_call | solution.py:394
  76.7 7.7 %all-to-all-start.1 = ((bf16[64,2,640]{2,1,0:T(2,128)(2,1)}), bf16[64,2,640]{2,1,0:T(2,128)(2,1)S(1)}, u32[]{:S(2)}, u32[]{:S(2)}) async-start(bf16[64,2,640]{2,1,0:T(2,128)(2,1)} %get-tuple-element.42), calls=%async_computation.1 | async-start | bytes 327680 | tf_op jit(solution)/shard_map/all_to_all | solution.py:516
  84.4 0.0 collective-permute-done.3
  84.4 0.1 add_multiply_fusion
  84.7 2.1 %collective-permute-start.4 = (bf16[2,192,384]{2,1,0:T(8,128)(2,1)S(1)}, bf16[2,192,384]{2,1,0:T(8,128)(2,1)S(1)}, u32[]{:S(2)}, u32[]{:S(2)}) collective-permute-start(bf16[2,192,384]{2,1,0:T(8,128)(2,1)S(1)} %pad_maximum_fusion.refs_0_), channel_id=1, source_target_pairs={{0,128},{128,0},{256,384},{384,256},{1,129},{129,1},{257,385},{385... | collective-permute-start | bytes 884744 | tf_op jit(solution)/shard_map/ppermute | solution.py:470
  86.7 4.8 %collective-permute-start.5 = (bf16[2,192,384]{2,1,0:T(8,128)(2,1)S(1)}, bf16[2,192,384]{2,1,0:T(8,128)(2,1)S(1)}, u32[]{:S(2)}, u32[]{:S(2)}) collective-permute-start(bf16[2,192,384]{2,1,0:T(8,128)(2,1)S(1)} %pad_maximum_fusion.refs_0_), channel_id=1, source_target_pairs={{0,256},{128,384},{256,0},{384,128},{1,257},{129,385},{257,1},{385... | collective-permute-start | bytes 884744 | tf_op jit(solution)/shard_map/ppermute | solution.py:470
  91.6 2.7 %collective-permute-start.6 = (bf16[2,192,384]{2,1,0:T(8,128)(2,1)S(1)}, bf16[2,192,384]{2,1,0:T(8,128)(2,1)S(1)}, u32[]{:S(2)}, u32[]{:S(2)}) collective-permute-start(bf16[2,192,384]{2,1,0:T(8,128)(2,1)S(1)} %pad_maximum_fusion.refs_0_), channel_id=1, source_target_pairs={{0,384},{128,256},{256,128},{384,0},{1,385},{129,257},{257,129},{3... | collective-permute-start | bytes 884744 | tf_op jit(solution)/shard_map/ppermute | solution.py:470
  94.3 8.5 %all-to-all-done.1 = bf16[64,2,640]{2,1,0:T(2,128)(2,1)S(1)} async-done(((bf16[64,2,640]{2,1,0:T(2,128)(2,1)}), bf16[64,2,640]{2,1,0:T(2,128)(2,1)S(1)}, u32[]{:S(2)}, u32[]{:S(2)}) %all-to-all-start.1) | async-done | bytes 163872 | tf_op jit(solution)/shard_map/all_to_all | solution.py:516
  102.8 0.2 convert_reduce_fusion.mine_ref
  103.0 3.1 %collective-permute-start.2 = (f32[2,640]{1,0:T(2,128)S(1)}, f32[2,640]{1,0:T(2,128)S(1)}, u32[]{:S(2)}, u32[]{:S(2)}) collective-permute-start(f32[2,640]{1,0:T(2,128)S(1)} %convert_reduce_fusion.mine_ref), channel_id=1, source_target_pairs={{0,1},{1,0},{2,3},{3,2},{4,5},{5,4},{6,7},{7,6},{8,9},{9,8},{10,11... | collective-permute-start | bytes 15368 | tf_op jit(solution)/shard_map/ppermute | solution.py:470
  106.1 2.7 %collective-permute-done.2.other_ref = f32[2,640]{1,0:T(2,128)S(1)} collective-permute-done((f32[2,640]{1,0:T(2,128)S(1)}, f32[2,640]{1,0:T(2,128)S(1)}, u32[]{:S(2)}, u32[]{:S(2)}) %collective-permute-start.2) | collective-permute-done | bytes 5152 | tf_op jit(solution)/shard_map/ppermute | solution.py:470
  108.8 0.8 expand.1
  109.7 7.2 %all-to-all-start.2 = ((f32[64,1,256]{2,1,0:T(1,128)}), f32[64,1,256]{2,1,0:T(1,128)S(1)}, u32[]{:S(2)}, u32[]{:S(2)}) async-start(f32[64,1,256]{2,1,0:T(1,128)} %get-tuple-element.43), calls=%async_computation.2 | async-start | bytes 131072 | tf_op jit(solution)/shard_map/all_to_all | solution.py:524
  116.8 0.0 collective-permute-done.4.refs_1_
  116.8 0.0 collective-permute-done.5.refs_2_
  116.8 0.0 collective-permute-done.6.refs_3_
  116.9 0.9 finish.1
  117.8 13.6 %all-to-all-done.2 = f32[64,1,256]{2,1,0:T(1,128)S(1)} async-done(((f32[64,1,256]{2,1,0:T(1,128)}), f32[64,1,256]{2,1,0:T(1,128)S(1)}, u32[]{:S(2)}, u32[]{:S(2)}) %all-to-all-start.2) | async-done | bytes 65568 | tf_op jit(solution)/shard_map/all_to_all | solution.py:524
  131.4 0.7 reduce_max.11
  (5 shorter events, 0.2 us)
Async XLA Ops:
  5.1 54.1 %all-to-all-start = ((bf16[64,40,128]{2,1,0:T(8,128)(2,1)}), bf16[64,40,128]{2,1,0:T(8,128)(2,1)S(1)}, u32[]{:S(2)}, u32[]{:S(2)}) async-start(bf16[64,40,128]{2,1,0:T(8,128)(2,1)} %get-tuple-element.28), calls=%async_computation | async-start | bytes 1310720 | tf_op jit(solution)/shard_map/all_to_all | solution.py:508
  59.3 5.3 %collective-permute-start = (bf16[64,24,128]{2,1,0:T(8,128)(2,1)S(1)}, bf16[64,24,128]{2,1,0:T(8,128)(2,1)S(1)}, u32[]{:S(2)}, u32[]{:S(2)}) collective-permute-start(bf16[64,24,128]{2,1,0:T(8,128)(2,1)S(1)} %slice.14.own_ref), channel_id=1, source_target_pairs={{0,2},{2,0},{4,6},{6,4},{8,10},{10,8},{12,14},{14,12},{16,18},{18,... | collective-permute-start | bytes 1179656 | tf_op jit(solution)/shard_map/ppermute | solution.py:470
  61.2 11.4 %copy-start = (bf16[384,768]{1,0:T(8,128)(2,1)S(1)}, bf16[384,768]{1,0:T(8,128)(2,1)}, u32[]{:S(2)}) copy-start(bf16[384,768]{1,0:T(8,128)(2,1)} %constant.42.clone.tabx_hbm.tabx_ref) | copy-start | bytes 1769476
  61.2 11.4 %collective-permute-start.1 = (bf16[64,16,128]{2,1,0:T(8,128)(2,1)S(1)}, bf16[64,16,128]{2,1,0:T(8,128)(2,1)S(1)}, u32[]{:S(2)}, u32[]{:S(2)}) collective-permute-start(bf16[64,16,128]{2,1,0:T(8,128)(2,1)S(1)} %slice.15), channel_id=1, source_target_pairs={{0,128},{128,0},{256,384},{384,256},{1,129},{129,1},{257,385},{385... | collective-permute-start | bytes 786440 | tf_op jit(solution)/shard_map/ppermute | solution.py:470
  68.2 16.2 %collective-permute-start.3 = (bf16[2,192,384]{2,1,0:T(8,128)(2,1)S(1)}, bf16[2,192,384]{2,1,0:T(8,128)(2,1)S(1)}, u32[]{:S(2)}, u32[]{:S(2)}) collective-permute-start(bf16[2,192,384]{2,1,0:T(8,128)(2,1)S(1)} %get-tuple-element.45), channel_id=1, source_target_pairs={{0,1},{1,0},{2,3},{3,2},{4,5},{5,4},{6,7},{7,6},{8,9},{9,8},{10,11... | collective-permute-start | bytes 884744 | tf_op jit(solution)/shard_map/ppermute | solution.py:470
  76.7 26.0 %all-to-all-start.1 = ((bf16[64,2,640]{2,1,0:T(2,128)(2,1)}), bf16[64,2,640]{2,1,0:T(2,128)(2,1)S(1)}, u32[]{:S(2)}, u32[]{:S(2)}) async-start(bf16[64,2,640]{2,1,0:T(2,128)(2,1)} %get-tuple-element.42), calls=%async_computation.1 | async-start | bytes 327680 | tf_op jit(solution)/shard_map/all_to_all | solution.py:516
  84.7 32.2 %collective-permute-start.4 = (bf16[2,192,384]{2,1,0:T(8,128)(2,1)S(1)}, bf16[2,192,384]{2,1,0:T(8,128)(2,1)S(1)}, u32[]{:S(2)}, u32[]{:S(2)}) collective-permute-start(bf16[2,192,384]{2,1,0:T(8,128)(2,1)S(1)} %pad_maximum_fusion.refs_0_), channel_id=1, source_target_pairs={{0,128},{128,0},{256,384},{384,256},{1,129},{129,1},{257,385},{385... | collective-permute-start | bytes 884744 | tf_op jit(solution)/shard_map/ppermute | solution.py:470
  86.7 30.1 %collective-permute-start.5 = (bf16[2,192,384]{2,1,0:T(8,128)(2,1)S(1)}, bf16[2,192,384]{2,1,0:T(8,128)(2,1)S(1)}, u32[]{:S(2)}, u32[]{:S(2)}) collective-permute-start(bf16[2,192,384]{2,1,0:T(8,128)(2,1)S(1)} %pad_maximum_fusion.refs_0_), channel_id=1, source_target_pairs={{0,256},{128,384},{256,0},{384,128},{1,257},{129,385},{257,1},{385... | collective-permute-start | bytes 884744 | tf_op jit(solution)/shard_map/ppermute | solution.py:470
  91.6 25.3 %collective-permute-start.6 = (bf16[2,192,384]{2,1,0:T(8,128)(2,1)S(1)}, bf16[2,192,384]{2,1,0:T(8,128)(2,1)S(1)}, u32[]{:S(2)}, u32[]{:S(2)}) collective-permute-start(bf16[2,192,384]{2,1,0:T(8,128)(2,1)S(1)} %pad_maximum_fusion.refs_0_), channel_id=1, source_target_pairs={{0,384},{128,256},{256,128},{384,0},{1,385},{129,257},{257,129},{3... | collective-permute-start | bytes 884744 | tf_op jit(solution)/shard_map/ppermute | solution.py:470
  103.0 5.9 %collective-permute-start.2 = (f32[2,640]{1,0:T(2,128)S(1)}, f32[2,640]{1,0:T(2,128)S(1)}, u32[]{:S(2)}, u32[]{:S(2)}) collective-permute-start(f32[2,640]{1,0:T(2,128)S(1)} %convert_reduce_fusion.mine_ref), channel_id=1, source_target_pairs={{0,1},{1,0},{2,3},{3,2},{4,5},{5,4},{6,7},{7,6},{8,9},{9,8},{10,11... | collective-permute-start | bytes 15368 | tf_op jit(solution)/shard_map/ppermute | solution.py:470
  109.7 21.8 %all-to-all-start.2 = ((f32[64,1,256]{2,1,0:T(1,128)}), f32[64,1,256]{2,1,0:T(1,128)S(1)}, u32[]{:S(2)}, u32[]{:S(2)}) async-start(f32[64,1,256]{2,1,0:T(1,128)} %get-tuple-element.43), calls=%async_computation.2 | async-start | bytes 131072 | tf_op jit(solution)/shard_map/all_to_all | solution.py:524
